TPU v7x, 256 devices: a whole 4x4x8 slice. The times are simulated.
256 devices in a mesh: blk: 128 (over x_hi, y, z, core), head: 2 (over x_lo).
Axes of the slice: x: 4 (x_hi: 2, x_lo: 2; x = x_hi * 2 + x_lo), y: 4, z: 8, core: 2. Of those that a mesh axis runs over, the one named last changes fastest.
Arguments:
- query: bfloat16 [32768, 1024], P('blk', 'head'), may hold values from -192 to 192
- key: bfloat16 [32768, 1024], P('blk', 'head'), may hold values from -6 to 6
- value: bfloat16 [32768, 1024], P('blk', 'head'), may hold values from -6 to 6
- out_grad: bfloat16 [32768, 1024], P('blk', 'head'), may hold values from -48 to 48
- q_weight: bfloat16 [1024, 1024], P(None, 'head'), may hold values from -0.1875 to 0.1875
- k_weight: bfloat16 [1024, 1024], P(None, 'head'), may hold values from -0.1875 to 0.1875
- v_weight: bfloat16 [1024, 1024], P(None, 'head'), may hold values from -0.1875 to 0.1875
- adjacency: int32 [256, 14], P('blk'), may hold values from 0 to 1, as said below
- owner: int32 [32768, 1], P('blk'), may hold values from 0 to 127; in each aligned block of 256 rows (0 to 255, 256 to 511, ...) at most 4 rows name the same one
Outputs:
- grad_input: bfloat16 [65536, 1024], P('blk', 'head')
Inputs may be any that keep to these rules, and one draw needn't show every extreme that they name: adjacency[b, c] is 1 where the hits of block b attend the hits of key block c mod 2 of the sector c // 2 - 3 places further along the cycle. Among the hits of one sector at most 4 have the same owner, and that many do in some sectors.
All inputs are finite; a program needn't handle non-finite values.
Results may differ from a plain program's by a relative error of at most 0.017.
Values may be sent and summed in bfloat16 or wider, within the bound.
No kernel may reach another device: no remote copies, remote signals or barrier semaphores. Data moves between devices by JAX's collectives and lax.ppermute only.
A program may use at most 64 MiB of HBM per device.

v0:
```python
import math

import jax
import jax.numpy as jnp
from jax import lax
from jax.sharding import PartitionSpec as P

HD = 64
BLOCK = 128
REACH = 3


def passed_along(value, axis, steps):
    count = lax.axis_size(axis)
    pairs = [(source, (source + steps) % count) for source in range(count)]
    return lax.ppermute(value, axis, pairs)


def on_device(query, key, value, out_grad, q_weight, k_weight, v_weight, adjacency, owner):
    hit_rows = query.shape[0]
    head_cols = query.shape[1]
    head_count = head_cols // HD
    blk_count = hit_rows // BLOCK
    span_count = 2 * REACH + 1
    factor = 1.0 / math.sqrt(HD)
    row_pos = lax.broadcasted_iota(jnp.int32, (blk_count, span_count * blk_count), 0)
    col_pos = lax.broadcasted_iota(jnp.int32, (blk_count, span_count * blk_count), 1)
    allowed = (adjacency > 0) | (col_pos == REACH * blk_count + row_pos)
    allowed = jnp.repeat(jnp.repeat(allowed, BLOCK, axis=0), BLOCK, axis=1)
    offset_list = [0] + [offset for offset in range(-REACH, REACH + 1) if offset != 0]

    def mask_for(offset):
        position = offset + REACH
        return allowed[:, position * hit_rows : (position + 1) * hit_rows][None]

    packed = jnp.stack([key, value])
    window = {0: packed}
    for offset in offset_list[1:]:
        window[offset] = passed_along(packed, "blk", -offset)
    q_heads = query.reshape(hit_rows, head_count, HD)
    g_heads = out_grad.reshape(hit_rows, head_count, HD)

    def split_heads(offset):
        return (
            window[offset][0].reshape(hit_rows, head_count, HD),
            window[offset][1].reshape(hit_rows, head_count, HD),
        )

    score_store = {}
    run_max = None
    run_sum = None
    for offset in offset_list:
        keys_h, vals_h = split_heads(offset)
        scores = (
            jnp.einsum("ihd,jhd->hij", q_heads, keys_h, preferred_element_type=jnp.float32) * factor
        )
        masked = jnp.where(mask_for(offset), scores, -jnp.inf)
        score_store[offset] = masked
        block_max = jnp.max(masked, axis=2, keepdims=True)
        if offset == 0:
            run_max = block_max
            run_sum = jnp.sum(jnp.exp(masked - run_max), axis=2, keepdims=True)
        else:
            new_max = jnp.maximum(run_max, block_max)
            run_sum = run_sum * jnp.exp(run_max - new_max) + jnp.sum(
                jnp.exp(masked - new_max), axis=2, keepdims=True
            )
            run_max = new_max
    log_total = run_max + jnp.log(run_sum)
    prob_store = {}
    attended = jnp.zeros((hit_rows, head_count, HD), jnp.float32)
    for offset in offset_list:
        keys_h, vals_h = split_heads(offset)
        prob_full = jnp.where(mask_for(offset), jnp.exp(score_store[offset] - log_total), 0.0)
        prob_store[offset] = prob_full
        prob_low = prob_full.astype(jnp.bfloat16)
        attended = attended + jnp.einsum(
            "hij,jhd->ihd", prob_low, vals_h, preferred_element_type=jnp.float32
        )
    row_delta = jnp.sum(g_heads.astype(jnp.float32) * attended, axis=2)
    delta_cols = jnp.transpose(row_delta)[:, :, None]
    q_acc = jnp.zeros((hit_rows, head_count, HD), jnp.float32)
    key_grads = {}
    for offset in offset_list:
        keys_h, vals_h = split_heads(offset)
        prob_full = prob_store[offset]
        prob_low = prob_full.astype(jnp.bfloat16)
        prob_grad = jnp.einsum("ihd,jhd->hij", g_heads, vals_h, preferred_element_type=jnp.float32)
        score_grad = (prob_full * (prob_grad - delta_cols)).astype(jnp.bfloat16)
        q_acc = q_acc + jnp.einsum(
            "hij,jhd->ihd", score_grad, keys_h, preferred_element_type=jnp.float32
        )
        k_term = (
            jnp.einsum("hij,ihd->jhd", score_grad, q_heads, preferred_element_type=jnp.float32)
            * factor
        ).astype(jnp.bfloat16)
        v_term = jnp.einsum(
            "hij,ihd->jhd", prob_low, g_heads, preferred_element_type=jnp.float32
        ).astype(jnp.bfloat16)
        key_grads[offset] = jnp.stack(
            [k_term.reshape(hit_rows, head_cols), v_term.reshape(hit_rows, head_cols)]
        )
    q_grad = (q_acc * factor).reshape(hit_rows, head_cols).astype(jnp.bfloat16)
    summed = key_grads[0].astype(jnp.float32)
    for offset in offset_list[1:]:
        summed = summed + passed_along(key_grads[offset], "blk", offset).astype(jnp.float32)
    k_grad = summed[0].astype(jnp.bfloat16)
    v_grad = summed[1].astype(jnp.bfloat16)
    contract = (((1,), (1,)), ((), ()))
    partial_value = lax.dot_general(q_grad, q_weight, contract, preferred_element_type=jnp.float32)
    partial_value = partial_value + lax.dot_general(
        k_grad, k_weight, contract, preferred_element_type=jnp.float32
    )
    partial_value = partial_value + lax.dot_general(
        v_grad, v_weight, contract, preferred_element_type=jnp.float32
    )
    reduced = lax.psum_scatter(
        partial_value.astype(jnp.bfloat16), "head", scatter_dimension=1, tiled=True
    )
    sectors = lax.axis_size("blk")
    capacity = 2 * hit_rows // sectors
    destination = owner[:, 0]
    earlier = lax.broadcasted_iota(jnp.int32, (hit_rows, hit_rows), 0) > lax.broadcasted_iota(
        jnp.int32, (hit_rows, hit_rows), 1
    )
    same_dest = destination[:, None] == destination[None, :]
    slot_rank = jnp.sum((same_dest & earlier).astype(jnp.int32), axis=1)
    outgoing = jnp.zeros((sectors * capacity, reduced.shape[1]), jnp.bfloat16)
    outgoing = outgoing.at[destination * capacity + slot_rank].set(reduced)
    return lax.all_to_all(outgoing, "blk", split_axis=0, concat_axis=0, tiled=True)


def solution(mesh):
    return jax.shard_map(
        on_device,
        mesh=mesh,
        in_specs=(
            P("blk", "head"),
            P("blk", "head"),
            P("blk", "head"),
            P("blk", "head"),
            P(None, "head"),
            P(None, "head"),
            P(None, "head"),
            P("blk", None),
            P("blk", None),
        ),
        out_specs=P("blk", "head"),
        check_vma=False,
    )
```

profile of v0, /device:TPU:1, one launch (start us, length us, event | category | flops | bytes accessed | tf_op | source)
XLA Modules:
  0.0 215.5 jit_solution(13051438682556080351)
XLA Ops:
  6.5 2.0 pad_maximum_fusion
  8.5 11.9 %collective-permute-start.5 = (bf16[2,256,512]{2,1,0:T(8,128)(2,1)}, bf16[2,256,512]{2,1,0:T(8,128)(2,1)}, u32[]{:S(2)}, u32[]{:S(2)}) collective-permute-start(bf16[2,256,512]{2,1,0:T(8,128)(2,1)} %pad_maximum_fusion), channel_id=1, source_target_pairs={{0,250},{2,252},{4,254},{6,0},{8,2},{10,4},{12,6},{14,8},{16,10},{... | collective-permute-start | bytes 1572872 | tf_op jit(solution)/shard_map/ppermute | solution.py:16
  28.3 1.8 copy.130
  31.9 5.8 %collective-permute-done.5 = bf16[2,256,512]{2,1,0:T(8,128)(2,1)} collective-permute-done((bf16[2,256,512]{2,1,0:T(8,128)(2,1)}, bf16[2,256,512]{2,1,0:T(8,128)(2,1)}, u32[]{:S(2)}, u32[]{:S(2)}) %collective-permute-start.5) | collective-permute-done | bytes 524320 | tf_op jit(solution)/shard_map/ppermute | solution.py:16
  37.7 1.9 fusion.69
  39.6 9.4 %collective-permute-done.4 = bf16[2,256,512]{2,1,0:T(8,128)(2,1)} collective-permute-done((bf16[2,256,512]{2,1,0:T(8,128)(2,1)}, bf16[2,256,512]{2,1,0:T(8,128)(2,1)}, u32[]{:S(2)}, u32[]{:S(2)}) %collective-permute-start.4) | collective-permute-done | bytes 524320 | tf_op jit(solution)/shard_map/ppermute | solution.py:16
  48.9 1.9 fusion.70
  50.8 1.9 fusion.71
  54.5 1.8 copy.127
  56.3 1.8 copy.126
  58.1 1.9 fusion.72
  59.9 1.8 copy.125
  61.7 1.9 fusion.73
  63.6 1.8 copy.124
  65.4 1.8 fusion.74
  69.0 1.8 copy.132
  70.8 1.8 copy.134
  72.6 1.8 copy.136
  74.4 1.8 copy.138
  76.2 1.8 copy.140
  78.0 1.8 copy.142
  100.1 8.7 %collective-permute-start.6 = (bf16[2,256,512]{1,2,0:T(8,128)(2,1)S(1)}, bf16[2,256,512]{1,2,0:T(8,128)(2,1)S(1)}, u32[]{:S(2)}, u32[]{:S(2)}) collective-permute-start(bf16[2,256,512]{1,2,0:T(8,128)(2,1)S(1)} %pad_maximum_fusion.1), channel_id=1, source_target_pairs={{0,250},{2,252},{4,254},{6,0},{8,2},{10,4},{12,6},{14,8},{16,10},{... | collective-permute-start | bytes 1572872 | tf_op jit(solution)/shard_map/ppermute | solution.py:16
  109.3 3.3 %collective-permute-start.7 = (bf16[2,256,512]{1,2,0:T(8,128)(2,1)S(1)}, bf16[2,256,512]{1,2,0:T(8,128)(2,1)S(1)}, u32[]{:S(2)}, u32[]{:S(2)}) collective-permute-start(bf16[2,256,512]{1,2,0:T(8,128)(2,1)S(1)} %pad_maximum_fusion.2), channel_id=1, source_target_pairs={{0,252},{2,254},{4,0},{6,2},{8,4},{10,6},{12,8},{14,10},{16,12},{1... | collective-permute-start | bytes 1572872 | tf_op jit(solution)/shard_map/ppermute | solution.py:16
  113.7 1.8 collective-permute-start.9
  121.2 3.3 %collective-permute-done.6 = bf16[2,256,512]{1,2,0:T(8,128)(2,1)S(1)} collective-permute-done((bf16[2,256,512]{1,2,0:T(8,128)(2,1)S(1)}, bf16[2,256,512]{1,2,0:T(8,128)(2,1)S(1)}, u32[]{:S(2)}, u32[]{:S(2)}) %collective-permute-start.6) | collective-permute-done | bytes 524320 | tf_op jit(solution)/shard_map/ppermute | solution.py:16
  125.5 11.9 %collective-permute-done.7 = bf16[2,256,512]{1,2,0:T(8,128)(2,1)S(1)} collective-permute-done((bf16[2,256,512]{1,2,0:T(8,128)(2,1)S(1)}, bf16[2,256,512]{1,2,0:T(8,128)(2,1)S(1)}, u32[]{:S(2)}, u32[]{:S(2)}) %collective-permute-start.7) | collective-permute-done | bytes 524320 | tf_op jit(solution)/shard_map/ppermute | solution.py:16
  137.4 2.5 %collective-permute-done.8 = bf16[2,256,512]{1,2,0:T(8,128)(2,1)S(1)} collective-permute-done((bf16[2,256,512]{1,2,0:T(8,128)(2,1)S(1)}, bf16[2,256,512]{1,2,0:T(8,128)(2,1)S(1)}, u32[]{:S(2)}, u32[]{:S(2)}) %collective-permute-start.8) | collective-permute-done | bytes 524320 | tf_op jit(solution)/shard_map/ppermute | solution.py:16
  140.0 9.0 %collective-permute-done.10 = bf16[2,256,512]{1,2,0:T(8,128)(2,1)S(1)} collective-permute-done((bf16[2,256,512]{1,2,0:T(8,128)(2,1)S(1)}, bf16[2,256,512]{1,2,0:T(8,128)(2,1)S(1)}, u32[]{:S(2)}, u32[]{:S(2)}) %collective-permute-start.10) | collective-permute-done | bytes 524320 | tf_op jit(solution)/shard_map/ppermute | solution.py:16
  148.9 2.6 %collective-permute-done.11 = bf16[2,256,512]{1,2,0:T(8,128)(2,1)S(1)} collective-permute-done((bf16[2,256,512]{1,2,0:T(8,128)(2,1)S(1)}, bf16[2,256,512]{1,2,0:T(8,128)(2,1)S(1)}, u32[]{:S(2)}, u32[]{:S(2)}) %collective-permute-start.11) | collective-permute-done | bytes 524320 | tf_op jit(solution)/shard_map/ppermute | solution.py:16
  155.5 16.6 %reduce-scatter.2.cloned.1.call-done = bf16[256,512]{1,0:T(8,128)(2,1)} async-done(((bf16[256,1024]{1,0:T(8,128)(2,1)}), bf16[256,512]{1,0:T(8,128)(2,1)}) %reduce-scatter.2.cloned.1.call-update) | async-done | bytes 262160 | tf_op jit(solution)/shard_map/reduce_scatter | solution.py:117
  172.2 2.1 scatter_custom_fusion
  174.4 33.3 %all_to_all.12 = bf16[128,4,512]{2,1,0:T(4,128)(2,1)S(1)} all-to-all(bf16[128,4,512]{2,1,0:T(4,128)(2,1)S(1)} %all_to_all.8), channel_id=1, replica_groups=mesh['blk'=128,'head'=2] {'blk'}, dimensions={0} | all-to-all | bytes 1048576 | tf_op jit(solution)/shard_map/all_to_all | solution.py:130
  (142 shorter events, 46.4 us)
Async XLA Ops:
  6.5 114.2 %copy-start = (bf16[1024,512]{1,0:T(8,128)(2,1)S(1)}, bf16[1024,512]{1,0:T(8,128)(2,1)}, u32[]{:S(2)}) copy-start(bf16[1024,512]{1,0:T(8,128)(2,1)} %param.13) | copy-start | bytes 3145732
  6.5 19.0 %copy-start.22 = (bf16[256,512]{1,0:T(8,128)(2,1)S(1)}, bf16[256,512]{1,0:T(8,128)(2,1)}, u32[]{:S(2)}) copy-start(bf16[256,512]{1,0:T(8,128)(2,1)} %param.10) | copy-start | bytes 786436
  6.5 19.9 %copy-start.24 = (bf16[256,512]{1,0:T(8,128)(2,1)S(1)}, bf16[256,512]{1,0:T(8,128)(2,1)}, u32[]{:S(2)}) copy-start(bf16[256,512]{1,0:T(8,128)(2,1)} %param.9) | copy-start | bytes 786436
  6.5 165.6 %reduce-scatter.2.cloned.1.call-start = ((), (), s32[]{:S(2)}) async-start(), calls=%async_computation.2 | async-start | bytes 786432 | tf_op jit(solution)/shard_map/reduce_scatter | solution.py:117
  8.5 29.2 %collective-permute-start.5 = (bf16[2,256,512]{2,1,0:T(8,128)(2,1)}, bf16[2,256,512]{2,1,0:T(8,128)(2,1)}, u32[]{:S(2)}, u32[]{:S(2)}) collective-permute-start(bf16[2,256,512]{2,1,0:T(8,128)(2,1)} %pad_maximum_fusion), channel_id=1, source_target_pairs={{0,250},{2,252},{4,254},{6,0},{8,2},{10,4},{12,6},{14,8},{16,10},{... | collective-permute-start | bytes 1572872 | tf_op jit(solution)/shard_map/ppermute | solution.py:16
  20.4 28.5 %collective-permute-start.4 = (bf16[2,256,512]{2,1,0:T(8,128)(2,1)}, bf16[2,256,512]{2,1,0:T(8,128)(2,1)}, u32[]{:S(2)}, u32[]{:S(2)}) collective-permute-start(bf16[2,256,512]{2,1,0:T(8,128)(2,1)} %pad_maximum_fusion), channel_id=1, source_target_pairs={{0,252},{2,254},{4,0},{6,2},{8,4},{10,6},{12,8},{14,10},{16,12},{1... | collective-permute-start | bytes 1572872 | tf_op jit(solution)/shard_map/ppermute | solution.py:16
  21.1 29.7 %collective-permute-start.3 = (bf16[2,256,512]{2,1,0:T(8,128)(2,1)}, bf16[2,256,512]{2,1,0:T(8,128)(2,1)}, u32[]{:S(2)}, u32[]{:S(2)}) collective-permute-start(bf16[2,256,512]{2,1,0:T(8,128)(2,1)} %pad_maximum_fusion), channel_id=1, source_target_pairs={{0,254},{2,0},{4,2},{6,4},{8,6},{10,8},{12,10},{14,12},{16,14},{18... | collective-permute-start | bytes 1572872 | tf_op jit(solution)/shard_map/ppermute | solution.py:16
  21.7 36.4 %collective-permute-start.2 = (bf16[2,256,512]{2,1,0:T(8,128)(2,1)}, bf16[2,256,512]{2,1,0:T(8,128)(2,1)}, u32[]{:S(2)}, u32[]{:S(2)}) collective-permute-start(bf16[2,256,512]{2,1,0:T(8,128)(2,1)} %pad_maximum_fusion), channel_id=1, source_target_pairs={{0,2},{2,4},{4,6},{6,8},{8,10},{10,12},{12,14},{14,16},{16,18},{18... | collective-permute-start | bytes 1572872 | tf_op jit(solution)/shard_map/ppermute | solution.py:16
  22.9 38.8 %collective-permute-start.1 = (bf16[2,256,512]{2,1,0:T(8,128)(2,1)}, bf16[2,256,512]{2,1,0:T(8,128)(2,1)}, u32[]{:S(2)}, u32[]{:S(2)}) collective-permute-start(bf16[2,256,512]{2,1,0:T(8,128)(2,1)} %pad_maximum_fusion), channel_id=1, source_target_pairs={{0,4},{2,6},{4,8},{6,10},{8,12},{10,14},{12,16},{14,18},{16,20},{1... | collective-permute-start | bytes 1572872 | tf_op jit(solution)/shard_map/ppermute | solution.py:16
  37.7 27.7 %collective-permute-start = (bf16[2,256,512]{2,1,0:T(8,128)(2,1)}, bf16[2,256,512]{2,1,0:T(8,128)(2,1)}, u32[]{:S(2)}, u32[]{:S(2)}) collective-permute-start(bf16[2,256,512]{2,1,0:T(8,128)(2,1)} %pad_maximum_fusion), channel_id=1, source_target_pairs={{0,6},{2,8},{4,10},{6,12},{8,14},{10,16},{12,18},{14,20},{16,22},{... | collective-permute-start | bytes 1572872 | tf_op jit(solution)/shard_map/ppermute | solution.py:16
  79.7 1.5 copy-start.10
  79.7 1.6 copy-start.16
  79.8 2.1 copy-start.11
  79.8 2.1 copy-start.17
  81.3 1.1 copy-start.12
  81.3 1.1 copy-start.18
  81.9 1.1 copy-start.13
  81.9 1.1 copy-start.19
  82.5 1.1 copy-start.14
  82.5 1.1 copy-start.20
  86.8 1.0 copy-start.7
  87.4 1.0 copy-start.8
  100.1 24.5 %collective-permute-start.6 = (bf16[2,256,512]{1,2,0:T(8,128)(2,1)S(1)}, bf16[2,256,512]{1,2,0:T(8,128)(2,1)S(1)}, u32[]{:S(2)}, u32[]{:S(2)}) collective-permute-start(bf16[2,256,512]{1,2,0:T(8,128)(2,1)S(1)} %pad_maximum_fusion.1), channel_id=1, source_target_pairs={{0,250},{2,252},{4,254},{6,0},{8,2},{10,4},{12,6},{14,8},{16,10},{... | collective-permute-start | bytes 1572872 | tf_op jit(solution)/shard_map/ppermute | solution.py:16
  109.3 28.1 %collective-permute-start.7 = (bf16[2,256,512]{1,2,0:T(8,128)(2,1)S(1)}, bf16[2,256,512]{1,2,0:T(8,128)(2,1)S(1)}, u32[]{:S(2)}, u32[]{:S(2)}) collective-permute-start(bf16[2,256,512]{1,2,0:T(8,128)(2,1)S(1)} %pad_maximum_fusion.2), channel_id=1, source_target_pairs={{0,252},{2,254},{4,0},{6,2},{8,4},{10,6},{12,8},{14,10},{16,12},{1... | collective-permute-start | bytes 1572872 | tf_op jit(solution)/shard_map/ppermute | solution.py:16
  113.1 26.9 %collective-permute-start.8 = (bf16[2,256,512]{1,2,0:T(8,128)(2,1)S(1)}, bf16[2,256,512]{1,2,0:T(8,128)(2,1)S(1)}, u32[]{:S(2)}, u32[]{:S(2)}) collective-permute-start(bf16[2,256,512]{1,2,0:T(8,128)(2,1)S(1)} %pad_maximum_fusion.3), channel_id=1, source_target_pairs={{0,254},{2,0},{4,2},{6,4},{8,6},{10,8},{12,10},{14,12},{16,14},{18... | collective-permute-start | bytes 1572872 | tf_op jit(solution)/shard_map/ppermute | solution.py:16
  113.7 4.3 %copy-start.9 = (bf16[256,512]{0,1:T(8,128)(2,1)S(1)}, bf16[256,512]{0,1:T(8,128)(2,1)}, u32[]{:S(2)}) copy-start(bf16[256,512]{0,1:T(8,128)(2,1)} %copy.121) | copy-start | bytes 786436
  113.7 26.3 %collective-permute-start.9 = (bf16[2,256,512]{1,2,0:T(8,128)(2,1)S(1)}, bf16[2,256,512]{1,2,0:T(8,128)(2,1)S(1)}, u32[]{:S(2)}, u32[]{:S(2)}) collective-permute-start(bf16[2,256,512]{1,2,0:T(8,128)(2,1)S(1)} %pad_maximum_fusion.4), channel_id=1, source_target_pairs={{0,2},{2,4},{4,6},{6,8},{8,10},{10,12},{12,14},{14,16},{16,18},{18... | collective-permute-start | bytes 1572872 | tf_op jit(solution)/shard_map/ppermute | solution.py:16
  116.0 33.0 %collective-permute-start.10 = (bf16[2,256,512]{1,2,0:T(8,128)(2,1)S(1)}, bf16[2,256,512]{1,2,0:T(8,128)(2,1)S(1)}, u32[]{:S(2)}, u32[]{:S(2)}) collective-permute-start(bf16[2,256,512]{1,2,0:T(8,128)(2,1)S(1)} %pad_maximum_fusion.5), channel_id=1, source_target_pairs={{0,4},{2,6},{4,8},{6,10},{8,12},{10,14},{12,16},{14,18},{16,20},{1... | collective-permute-start | bytes 1572872 | tf_op jit(solution)/shard_map/ppermute | solution.py:16
  124.6 27.0 %collective-permute-start.11 = (bf16[2,256,512]{1,2,0:T(8,128)(2,1)S(1)}, bf16[2,256,512]{1,2,0:T(8,128)(2,1)S(1)}, u32[]{:S(2)}, u32[]{:S(2)}) collective-permute-start(bf16[2,256,512]{1,2,0:T(8,128)(2,1)S(1)} %pad_maximum_fusion.6), channel_id=1, source_target_pairs={{0,6},{2,8},{4,10},{6,12},{8,14},{10,16},{12,18},{14,20},{16,22},{... | collective-permute-start | bytes 1572872 | tf_op jit(solution)/shard_map/ppermute | solution.py:16
  151.6 1.2 copy-start.21
  152.8 1.2 copy-start.23
  154.0 1.3 copy-start.25
  (7 other events, 6.8 us)
Sparse Core Ops, SparseCore 0:
  155.4 16.6 reduce-scatter.1
where the time goes:
time: 216 us; the launch traced here: 215 us
  waiting for transfers between devices  61.2 us (28%)
  local copies, waits for them, and re-layouts  45.4 us (21%)
  blocking collectives  33.3 us (15%)
  starting transfers between devices  30.5 us (14%)
  matrix products  25.2 us (12%)
  between operations  14 us (6%)
  other arithmetic  5.87 us (3%)
    ppermute x12, waiting for transfers between devices, passed_along(): return lax.ppermute(value, axis, pairs)  44.6 us
    all_to_all x1, blocking collectives, on_device(): lax.all_to_all(outgoing, 'blk', split_axis=0, concat_axis=0, tiled=True)  33.3 us
    ppermute x12, starting transfers between devices, passed_along(): return lax.ppermute(value, axis, pairs)  30.5 us
    slice x12, local copies, waits for them, and re-layouts, split_heads(): window[offset][1].reshape(hit_rows, head_count, HD)  21.9 us
    reduce_scatter x1, waiting for transfers between devices, on_device(): lax.psum_scatter(partial_value.astype(jnp.bfloat16), 'head', scatter_dime...  16.6 us
    slice x6, local copies, waits for them, and re-layouts, split_heads(): window[offset][0].reshape(hit_rows, head_count, HD)  10.8 us
    unnamed x59, local copies, waits for them, and re-layouts  8.62 us
    dot_general x7, matrix products, on_device(): jnp.einsum('ihd,jhd->hij', q_heads, keys_h, preferred_element_type=jnp.fl...  5.61 us
  transfers between devices with their start and end apart: 13, of which 8 were waited for; matrix products, arithmetic and copies ran while one was open for 15% of the time, Pallas kernels for 0%

commit v1 on v0

v1 whole, which is shorter than its diff:
```python
import functools
import math

import jax
import jax.numpy as jnp
from jax import lax
from jax.experimental import pallas as pl
from jax.experimental.pallas import tpu as pltpu
from jax.sharding import PartitionSpec as P

HD = 64
BLOCK = 128
REACH = 3
SPAN = 2 * REACH + 1
LOG2E = math.log2(math.e)
MASKED = -1e30
BF = jnp.bfloat16
F32 = jnp.float32
NT = (((1,), (1,)), ((), ()))
NN = (((1,), (0,)), ((), ()))
TN = (((0,), (0,)), ((), ()))
PARAMS = dict(vmem_limit_bytes=48 << 20)


def dot(a, b, dims):
    return lax.dot_general(a, b, dims, preferred_element_type=F32)


def moved(value, steps):
    count = lax.axis_size("blk")
    return lax.ppermute(value, "blk", [(s, (s + steps) % count) for s in range(count)])


def core_swapped(value):
    count = lax.axis_size("blk")
    return lax.ppermute(value, "blk", [(s, s ^ 1) for s in range(count)])


def bias_rows(adj_ref):
    shape = (16, 2 * BLOCK)
    row = lax.broadcasted_iota(jnp.int32, shape, 0)
    query_block = lax.broadcasted_iota(jnp.int32, shape, 1) // BLOCK
    allowed = row == 2 * REACH + query_block
    for c in range(2 * SPAN):
        for b in range(2):
            hit = (row == c) & (query_block == b) & (adj_ref[b, c] > 0)
            allowed = allowed | hit
    return jnp.where(allowed, 0.0, MASKED)


def pack_kernel(par_ref, adj_ref, q_ref, k_ref, v_ref, g_ref, send_ref):
    rows, cols = q_ref.shape
    send_ref[0:rows, 0:cols] = k_ref[...]
    send_ref[0:rows, cols : 2 * cols] = v_ref[...]
    send_ref[0:rows, 2 * cols : 3 * cols] = q_ref[...]
    send_ref[0:rows, 3 * cols : 4 * cols] = g_ref[...]
    send_ref[rows : rows + 16, 0:cols] = bias_rows(adj_ref).astype(BF)
    send_ref[rows : rows + 16, cols:] = jnp.zeros((16, 3 * cols), BF)


def order_kernel(par_ref, adj_ref, q_ref, k_ref, v_ref, g_ref, got_ref, kv_ref, first_ref, second_ref, qg_ref, bias_ref):
    rows, cols = q_ref.shape
    par = par_ref[0]
    other = 1 - par
    kv_ref[0, par] = k_ref[...]
    kv_ref[1, par] = v_ref[...]
    qg_ref[0, par] = q_ref[...] * (1.0 / math.sqrt(HD))
    qg_ref[1, par] = g_ref[...]
    kv_ref[0, other] = got_ref[0:rows, 0:cols]
    kv_ref[1, other] = got_ref[0:rows, cols : 2 * cols]
    qg_ref[0, other] = got_ref[0:rows, 2 * cols : 3 * cols] * (1.0 / math.sqrt(HD))
    qg_ref[1, other] = got_ref[0:rows, 3 * cols : 4 * cols]
    bias_ref[par] = bias_rows(adj_ref)
    bias_ref[other] = got_ref[rows : rows + 16, 0:cols].astype(F32)
    first_ref[...] = kv_ref[:, 0]
    second_ref[...] = kv_ref[:, 1]


def attention_kernel(
    par_ref, left2_ref, left_ref, mid_ref, right_ref, right2_ref, qg_ref, bias_ref,
    dleft2_ref, dleft_ref, dmid_ref, dright_ref, dright2_ref, dq_own_ref, dq_send_ref,
    s_ref, d_ref, p_ref, ds_ref, qs_ref, gs_ref,
):
    rows = qg_ref.shape[2]
    lanes = qg_ref.shape[3]

    def window(which, w):
        if w == 0:
            return left2_ref[which]
        if w < 3:
            return left_ref[which, w - 1]
        if w < 5:
            return mid_ref[which, w - 3]
        if w < 7:
            return right_ref[which, w - 5]
        return right2_ref[which]

    lane_head = lax.broadcasted_iota(jnp.int32, (rows, lanes), 1) // HD
    for t in range(2):
        for h in range(2):
            block = t * 2 + h
            cols = slice(block * rows, (block + 1) * rows)
            qh = jnp.where(lane_head == h, qg_ref[0, t], 0.0).astype(BF)
            gh = jnp.where(lane_head == h, qg_ref[1, t], 0.0).astype(BF)
            qs_ref[cols, :] = qh
            gs_ref[cols, :] = gh
            top = None
            for j in range(SPAN):
                scores = dot(window(0, t + j), qh, NT)
                s_ref[j * rows : (j + 1) * rows, :] = scores
                for b in range(2):
                    c = 2 * j + b
                    block_top = jnp.max(scores[b * BLOCK : (b + 1) * BLOCK], axis=0, keepdims=True)
                    block_top = block_top + bias_ref[t, c : c + 1, :]
                    top = block_top if top is None else jnp.maximum(top, block_top)
            total = jnp.zeros((1, rows), F32)
            delta = jnp.zeros((1, rows), F32)
            for j in range(SPAN):
                grads = dot(window(1, t + j), gh, NT)
                d_ref[j * rows : (j + 1) * rows, :] = grads
                for b in range(2):
                    c = 2 * j + b
                    at = slice(j * rows + b * BLOCK, j * rows + (b + 1) * BLOCK)
                    shift = (bias_ref[t, c : c + 1, :] - top) * LOG2E
                    weight = jnp.exp2(s_ref[at, :] * LOG2E + shift)
                    s_ref[at, :] = weight
                    total = total + jnp.sum(weight, axis=0, keepdims=True)
                    delta = delta + jnp.sum(
                        weight * grads[b * BLOCK : (b + 1) * BLOCK], axis=0, keepdims=True
                    )
            scale = 1.0 / total
            delta = delta * scale
            for j in range(SPAN):
                at = slice(j * rows, (j + 1) * rows)
                to = slice((t + j) * rows, (t + j + 1) * rows)
                prob = s_ref[at, :] * scale
                p_ref[to, cols] = prob.astype(BF)
                ds_ref[to, cols] = (prob * (d_ref[at, :] - delta)).astype(BF)
    for w in range(SPAN + 1):
        low = 0 if w < SPAN else 2 * rows
        high = 4 * rows if w > 0 else 2 * rows
        at = slice(w * rows, (w + 1) * rows)
        for which, (left_operand, right_operand) in enumerate(((ds_ref, qs_ref), (p_ref, gs_ref))):
            term = dot(left_operand[at, low:high], right_operand[low:high, :], NN)
            if w == 0:
                dleft2_ref[which] = term.astype(BF)
            elif w < 3:
                dleft_ref[which, w - 1] = term.astype(BF)
            elif w < 5:
                dmid_ref[which, w - 3] = term
            elif w < 7:
                dright_ref[which, w - 5] = term.astype(BF)
            else:
                dright2_ref[which] = term.astype(BF)
    sector_grads = []
    for t in range(2):
        parts = []
        for h in range(2):
            block = t * 2 + h
            acc = None
            for j in range(SPAN):
                w = t + j
                part = dot(ds_ref[w * rows : (w + 1) * rows, block * rows : (block + 1) * rows], window(0, w), TN)
                acc = part if acc is None else acc + part
            parts.append(acc)
        sector_grads.append(jnp.where(lane_head == 0, parts[0], parts[1]) * (1.0 / math.sqrt(HD)))
    first = par_ref[0] == 0
    dq_own_ref[...] = jnp.where(first, sector_grads[0], sector_grads[1]).astype(BF)
    dq_send_ref[...] = jnp.where(first, sector_grads[1], sector_grads[0]).astype(BF)


def total_kernel(par_ref, mid_ref, right_ref, left_ref, right2_ref, left2_ref, keep_ref, send_ref):
    par = par_ref[0]
    other = 1 - par
    first = par == 0
    for which in range(2):
        far0 = left2_ref[which].astype(F32)
        far1 = right2_ref[which].astype(F32)
        for sector, out_ref in ((par, keep_ref), (other, send_ref)):
            far = jnp.where(first, far0, far1) if out_ref is keep_ref else jnp.where(first, far1, far0)
            value = mid_ref[which, sector] + right_ref[which, sector].astype(F32)
            value = value + left_ref[which, sector].astype(F32) + far
            out_ref[which] = value.astype(BF)


def project_kernel(par_ref, dq_ref, dq2_ref, dkv_ref, dkv2_ref, wq_ref, wk_ref, wv_ref, out_ref):
    first = par_ref[0] == 0
    half = dq_ref.shape[1]
    total = None
    for own, got, weight in (
        (dq_ref[...], dq2_ref[...], wq_ref),
        (dkv_ref[0], dkv2_ref[0], wk_ref),
        (dkv_ref[1], dkv2_ref[1], wv_ref),
    ):
        low = jnp.where(first, own, got)
        high = jnp.where(first, got, own)
        term = dot(low, weight[:, 0:half], NT) + dot(high, weight[:, half:], NT)
        total = term if total is None else total + term
    out_ref[...] = total.astype(out_ref.dtype)


def route_kernel(owner_col_ref, owner_row_ref, place_ref):
    rows = owner_col_ref.shape[0]
    slots = place_ref.shape[0]
    owner_row = owner_row_ref[...]
    earlier = lax.broadcasted_iota(jnp.int32, (rows, rows), 0) < lax.broadcasted_iota(jnp.int32, (rows, rows), 1)
    same = (owner_col_ref[...] == owner_row) & earlier
    rank = jnp.sum(same.astype(jnp.int32), axis=0, keepdims=True)
    target = owner_row * 4 + rank
    slot = lax.broadcasted_iota(jnp.int32, (slots, rows), 0)
    place_ref[...] = jnp.where(slot == target, 1.0, 0.0).astype(BF)


def scatter_kernel(own_ref, got_ref, place_ref, out_ref):
    value = (own_ref[...] + got_ref[...].astype(F32)).astype(BF)
    out_ref[...] = dot(place_ref[...], value, NN).astype(BF)


def cost(flops, moved_bytes, exps=0):
    return pl.CostEstimate(flops=flops, bytes_accessed=moved_bytes, transcendentals=exps)


def on_device(query, key, value, out_grad, q_weight, k_weight, v_weight, adjacency, owner):
    rows, cols = query.shape
    half = cols // 2
    pair = 2 * HD
    sds = jax.ShapeDtypeStruct
    par = jnp.reshape(lax.axis_index("blk") % 2, (1,)).astype(jnp.int32)
    head = jnp.reshape(lax.axis_index("head"), (1,)).astype(jnp.int32)
    smem = pl.BlockSpec(memory_space=pltpu.SMEM)
    vmem = pl.BlockSpec(memory_space=pltpu.VMEM)

    def call(kernel, outs, grid, in_specs, out_specs, scratch=(), scalars=1, estimate=None):
        return pl.pallas_call(
            kernel,
            out_shape=outs,
            grid_spec=pltpu.PrefetchScalarGridSpec(
                num_scalar_prefetch=scalars, grid=grid, in_specs=in_specs, out_specs=out_specs,
                scratch_shapes=list(scratch),
            ),
            compiler_params=pltpu.CompilerParams(**PARAMS),
            cost_estimate=estimate,
        )

    own_half = pl.BlockSpec((rows, half), lambda i, p: (0, p[0]))
    other_half = pl.BlockSpec((rows, half), lambda i, p: (0, 1 - p[0]))

    def whole(*shape):
        return pl.BlockSpec(shape, lambda i, p: (0,) * len(shape))

    send = call(
        pack_kernel, sds((rows + 16, 4 * half), BF), (1,), [smem] + [other_half] * 4, whole(rows + 16, 4 * half)
    )(par, adjacency, query, key, value, out_grad)
    got = core_swapped(send)
    kv, kv_first, kv_second, qg, bias = call(
        order_kernel,
        (
            sds((2, 2, rows, half), BF),
            sds((2, rows, half), BF),
            sds((2, rows, half), BF),
            sds((2, 2, rows, half), BF),
            sds((2, 16, rows), F32),
        ),
        (1,),
        [smem] + [own_half] * 4 + [whole(rows + 16, 4 * half)],
        (whole(2, 2, rows, half), whole(2, rows, half), whole(2, rows, half), whole(2, 2, rows, half), whole(2, 16, rows)),
    )(par, adjacency, query, key, value, out_grad, got)
    from_left = moved(kv, 2)
    from_right = moved(kv, -2)
    from_left2 = moved(kv_second, 4)
    from_right2 = moved(kv_first, -4)

    slots = 4 * lax.axis_size("blk")
    place = pl.pallas_call(
        route_kernel, out_shape=sds((slots, rows), BF), in_specs=[vmem, vmem], out_specs=vmem
    )(owner, owner.reshape(1, rows))

    near = pl.BlockSpec((2, 2, rows, pair), lambda i, p: (0, 0, 0, i))
    far = pl.BlockSpec((2, rows, pair), lambda i, p: (0, 0, i))
    dq_spec = pl.BlockSpec((rows, pair), lambda i, p: (0, i))
    big = (SPAN + 1) * rows
    dleft2, dleft, dmid, dright, dright2, dq_own, dq_send = call(
        attention_kernel,
        (
            sds((2, rows, half), BF),
            sds((2, 2, rows, half), BF),
            sds((2, 2, rows, half), F32),
            sds((2, 2, rows, half), BF),
            sds((2, rows, half), BF),
            sds((rows, half), BF),
            sds((rows, half), BF),
        ),
        (half // pair,),
        [far, near, near, near, far, near, whole(2, 16, rows)],
        (far, near, near, near, far, dq_spec, dq_spec),
        scratch=(
            pltpu.VMEM((SPAN * rows, rows), F32),
            pltpu.VMEM((SPAN * rows, rows), F32),
            pltpu.VMEM((big, 4 * rows), BF),
            pltpu.VMEM((big, 4 * rows), BF),
            pltpu.VMEM((4 * rows, pair), BF),
            pltpu.VMEM((4 * rows, pair), BF),
        ),
    )(par, from_left2, from_left, kv, from_right, from_right2, qg, bias)
    got_right = moved(dleft, -2)
    got_left = moved(dright, 2)
    got_right2 = moved(dleft2, -4)
    got_left2 = moved(dright2, 4)
    dq_got = core_swapped(dq_send)
    keep, give = call(
        total_kernel,
        (sds((2, rows, half), BF), sds((2, rows, half), BF)),
        (1,),
        [whole(2, 2, rows, half)] * 3 + [whole(2, rows, half)] * 2,
        (whole(2, rows, half), whole(2, rows, half)),
    )(par, dmid, got_right, got_left, got_right2, got_left2)
    gave = core_swapped(give)

    scalars = jnp.concatenate([par, head])
    weight_other = pl.BlockSpec((cols, cols), lambda i, p: (1 - p[1], 0))
    weight_own = pl.BlockSpec((cols, cols), lambda i, p: (p[1], 0))
    terms = [whole(rows, half)] * 2 + [whole(2, rows, half)] * 2
    operands = (scalars, dq_own, dq_got, keep, gave, q_weight, k_weight, v_weight)
    partial_other = call(
        project_kernel, sds((rows, cols), BF), (1,), terms + [weight_other] * 3, whole(rows, cols)
    )(*operands)
    partial_got = lax.ppermute(partial_other, "head", [(0, 1), (1, 0)])
    partial_own = call(
        project_kernel, sds((rows, cols), F32), (1,), terms + [weight_own] * 3, whole(rows, cols)
    )(*operands)
    outgoing = pl.pallas_call(
        scatter_kernel, out_shape=sds((slots, cols), BF), in_specs=[vmem] * 3, out_specs=vmem
    )(partial_own, partial_got, place)
    return lax.all_to_all(outgoing, "blk", split_axis=0, concat_axis=0, tiled=True)


def solution(mesh):
    return jax.shard_map(
        on_device,
        mesh=mesh,
        in_specs=(
            P("blk", "head"),
            P("blk", "head"),
            P("blk", "head"),
            P("blk", "head"),
            P(None, "head"),
            P(None, "head"),
            P(None, "head"),
            P("blk", None),
            P("blk", None),
        ),
        out_specs=P("blk", "head"),
        check_vma=False,
    )
```

time: 216 us -> 136 us (0.63)
  local copies, waits for them, and re-layouts: 45.4 us -> 8.16 us
  Pallas kernels: 0 us -> 27.3 us
  waiting for transfers between devices: 61.2 us -> 35.3 us
  matrix products: 25.2 us -> 0 us
  between operations: 14 us -> 0.1 us
  starting transfers between devices: 30.5 us -> 38.9 us
  blocking collectives: 33.3 us -> 25.8 us
  other arithmetic: 5.87 us -> 0.07 us
    slice x19 -> x0, local copies, waits for them, and re-layouts: 33.5 us -> none  [the longest x12 21.9 us: split_heads(): window[offset][1].reshape(hit_rows, head_count, HD)]
    pallas_call x0 -> x8, Pallas kernels: none -> 27.3 us  [the longest x1 15.9 us: on_device(): call(attention_kernel, (sds((2, rows, half), BF), sds((2, 2, rows, half),...]
    dot_general x45 -> x0, matrix products: 25.2 us -> none  [the longest x7 5.61 us: on_device(): jnp.einsum('ihd,jhd->hij', q_heads, keys_h, preferred_element_type=jnp.fl...]
    reduce_scatter x1 -> x0, waiting for transfers between devices: 16.6 us -> none  [on_device(): lax.psum_scatter(partial_value.astype(jnp.bfloat16), 'head', scatter_dime...]
    ppermute x12, waiting for transfers between devices: 44.6 us -> 35.3 us  [the longest x8 30.2 us: moved(): lax.ppermute(value, 'blk', [(s, (s + steps) % count) for s in range(count)])]
    ppermute x12, starting transfers between devices: 30.5 us -> 38.9 us  [the longest x8 27.3 us: moved(): lax.ppermute(value, 'blk', [(s, (s + steps) % count) for s in range(count)])]
    all_to_all x1, blocking collectives: 33.3 us -> 25.8 us  [on_device(): lax.all_to_all(outgoing, 'blk', split_axis=0, concat_axis=0, tiled=True)]
    another operation x8 -> x0, other arithmetic: 2.81 us -> none  [the longest x1 1.99 us: on_device(): packed = jnp.stack([key, value])]
  transfers between devices with their start and end apart: 13 -> 12, of which waited for: 8 -> 7; matrix products, arithmetic and copies ran while one was open for 15% -> 1% of each run, Pallas kernels for 0% -> 3%
where the time goes in v1:
time: 136 us
  starting transfers between devices  38.9 us (29%)
  waiting for transfers between devices  35.3 us (26%)
  Pallas kernels  27.3 us (20%)
  blocking collectives  25.8 us (19%)
  local copies, waits for them, and re-layouts  8.16 us (6%)
    ppermute x8, waiting for transfers between devices, moved(): lax.ppermute(value, 'blk', [(s, (s + steps) % count) for s in range(count)])  30.2 us
    ppermute x8, starting transfers between devices, moved(): lax.ppermute(value, 'blk', [(s, (s + steps) % count) for s in range(count)])  27.3 us
    all_to_all x1, blocking collectives, on_device(): lax.all_to_all(outgoing, 'blk', split_axis=0, concat_axis=0, tiled=True)  25.8 us
    pallas_call x1, Pallas kernels, on_device(): call(attention_kernel, (sds((2, rows, half), BF), sds((2, 2, rows, half),...  15.9 us
    ppermute x3, starting transfers between devices, core_swapped(): return lax.ppermute(value, 'blk', [(s, s ^ 1) for s in range(count)])  11.3 us
    unnamed x21, local copies, waits for them, and re-layouts  6.08 us
    ppermute x3, waiting for transfers between devices, core_swapped(): return lax.ppermute(value, 'blk', [(s, s ^ 1) for s in range(count)])  3.2 us
    pallas_call x1, Pallas kernels, on_device(): call(project_kernel, sds((rows, cols), BF), (1,), terms + [weight_other]...  2.88 us
  transfers between devices with their start and end apart: 12, of which 7 were waited for; matrix products, arithmetic and copies ran while one was open for 1% of the time, Pallas kernels for 3%

profile of v1, /device:TPU:1, one launch (start us, length us, event | category | flops | bytes accessed | tf_op | source)
XLA Modules:
  0.0 135.7 jit_solution(11278708009050371917)
XLA Ops:
  0.0 0.7 copy-done.8
  0.7 0.9 copy-done.4
  1.6 0.9 copy-done.5
  2.6 0.9 copy-done.6
  3.5 0.9 copy-done.7
  4.5 0.7 shard_map.91
  5.2 3.3 %collective-permute-start = (bf16[272,1024]{1,0:T(8,128)(2,1)S(1)}, bf16[272,1024]{1,0:T(8,128)(2,1)S(1)}, u32[]{:S(2)}, u32[]{:S(2)}) collective-permute-start(bf16[272,1024]{1,0:T(8,128)(2,1)S(1)} %shard_map.91), channel_id=1, source_target_pairs={{0,2},{2,0},{4,6},{6,4},{8,10},{10,8},{12,14},{14,12},{16,18},{18,... | collective-permute-start | bytes 1671176 | tf_op jit(solution)/shard_map/ppermute | solution.py:36
  8.5 1.6 %collective-permute-done.got_ref = bf16[272,1024]{1,0:T(8,128)(2,1)S(1)} collective-permute-done((bf16[272,1024]{1,0:T(8,128)(2,1)S(1)}, bf16[272,1024]{1,0:T(8,128)(2,1)S(1)}, u32[]{:S(2)}, u32[]{:S(2)}) %collective-permute-start) | collective-permute-done | bytes 557088 | tf_op jit(solution)/shard_map/ppermute | solution.py:36
  10.1 0.7 shard_map.92
  10.9 8.8 %collective-permute-start.3 = (bf16[2,2,256,256]{3,2,1,0:T(8,128)(2,1)S(1)}, bf16[2,2,256,256]{3,2,1,0:T(8,128)(2,1)S(1)}, u32[]{:S(2)}, u32[]{:S(2)}) collective-permute-start(bf16[2,2,256,256]{3,2,1,0:T(8,128)(2,1)S(1)} %get-tuple-element.20.mid_ref), channel_id=1, source_target_pairs={{0,252},{2,254},{4,0},{6,2},{8,4},{10,6},{12,8},{14,10},{16,12},{1... | collective-permute-start | bytes 1572872 | tf_op jit(solution)/shard_map/ppermute | solution.py:31
  19.7 8.1 %collective-permute-start.4 = (bf16[2,256,256]{2,1,0:T(8,128)(2,1)S(1)}, bf16[2,256,256]{2,1,0:T(8,128)(2,1)S(1)}, u32[]{:S(2)}, u32[]{:S(2)}) collective-permute-start(bf16[2,256,256]{2,1,0:T(8,128)(2,1)S(1)} %get-tuple-element.21), channel_id=1, source_target_pairs={{0,248},{2,250},{4,252},{6,254},{8,0},{10,2},{12,4},{14,6},{16,8},... | collective-permute-start | bytes 786440 | tf_op jit(solution)/shard_map/ppermute | solution.py:31
  27.8 11.0 %collective-permute-done.1.left2_ref = bf16[2,256,256]{2,1,0:T(8,128)(2,1)S(1)} collective-permute-done((bf16[2,256,256]{2,1,0:T(8,128)(2,1)S(1)}, bf16[2,256,256]{2,1,0:T(8,128)(2,1)S(1)}, u32[]{:S(2)}, u32[]{:S(2)}) %collective-permute-start.1) | collective-permute-done | bytes 262176 | tf_op jit(solution)/shard_map/ppermute | solution.py:31
  38.7 3.1 %collective-permute-done.4.right2_ref = bf16[2,256,256]{2,1,0:T(8,128)(2,1)S(1)} collective-permute-done((bf16[2,256,256]{2,1,0:T(8,128)(2,1)S(1)}, bf16[2,256,256]{2,1,0:T(8,128)(2,1)S(1)}, u32[]{:S(2)}, u32[]{:S(2)}) %collective-permute-start.4) | collective-permute-done | bytes 262176 | tf_op jit(solution)/shard_map/ppermute | solution.py:31
  41.9 15.9 %shard_map.93 = (bf16[2,256,256]{2,1,0:T(8,128)(2,1)S(1)}, bf16[2,2,256,256]{3,2,1,0:T(8,128)(2,1)S(1)}, f32[2,2,256,256]{3,2,1,0:T(8,128)S(1)}, bf16[2,2,256,25...) custom-call(s32[1]{0:T(128)} %bitcast.par_ref, ...), custom_call_target="tpu_custom_call" | custom-call | tf_op jit(solution)/shard_map/pallas_call | solution.py:282
  57.7 2.6 %collective-permute-start.6 = (bf16[2,2,256,256]{3,2,1,0:T(8,128)(2,1)S(1)}, bf16[2,2,256,256]{3,2,1,0:T(8,128)(2,1)S(1)}, u32[]{:S(2)}, u32[]{:S(2)}) collective-permute-start(bf16[2,2,256,256]{3,2,1,0:T(8,128)(2,1)S(1)} %get-tuple-element.27), channel_id=1, source_target_pairs={{0,252},{2,254},{4,0},{6,2},{8,4},{10,6},{12,8},{14,10},{16,12},{1... | collective-permute-start | bytes 1572872 | tf_op jit(solution)/shard_map/ppermute | solution.py:31
  60.3 7.7 %collective-permute-start.8 = (bf16[2,256,256]{2,1,0:T(8,128)(2,1)S(1)}, bf16[2,256,256]{2,1,0:T(8,128)(2,1)S(1)}, u32[]{:S(2)}, u32[]{:S(2)}) collective-permute-start(bf16[2,256,256]{2,1,0:T(8,128)(2,1)S(1)} %get-tuple-element.29), channel_id=1, source_target_pairs={{0,248},{2,250},{4,252},{6,254},{8,0},{10,2},{12,4},{14,6},{16,8},... | collective-permute-start | bytes 786440 | tf_op jit(solution)/shard_map/ppermute | solution.py:31
  68.0 15.5 %collective-permute-done.8.right2_ref = bf16[2,256,256]{2,1,0:T(8,128)(2,1)S(1)} collective-permute-done((bf16[2,256,256]{2,1,0:T(8,128)(2,1)S(1)}, bf16[2,256,256]{2,1,0:T(8,128)(2,1)S(1)}, u32[]{:S(2)}, u32[]{:S(2)}) %collective-permute-start.8) | collective-permute-done | bytes 262176 | tf_op jit(solution)/shard_map/ppermute | solution.py:31
  83.5 0.6 collective-permute-done.9.left2_ref
  84.2 0.9 shard_map.94
  85.0 8.0 %collective-permute-start.10 = (bf16[2,256,256]{2,1,0:T(8,128)(2,1)}, bf16[2,256,256]{2,1,0:T(8,128)(2,1)}, u32[]{:S(2)}, u32[]{:S(2)}) collective-permute-start(bf16[2,256,256]{2,1,0:T(8,128)(2,1)} %get-tuple-element.32), channel_id=1, source_target_pairs={{0,2},{2,0},{4,6},{6,4},{8,10},{10,8},{12,14},{14,12},{16,18},{18,... | collective-permute-start | bytes 786440 | tf_op jit(solution)/shard_map/ppermute | solution.py:36
  93.1 1.6 %collective-permute-done.5.dq2_ref = bf16[256,256]{1,0:T(8,128)(2,1)} collective-permute-done((bf16[256,256]{1,0:T(8,128)(2,1)}, bf16[256,256]{1,0:T(8,128)(2,1)}, u32[]{:S(2)}, u32[]{:S(2)}) %collective-permute-start.5) | collective-permute-done | bytes 131104 | tf_op jit(solution)/shard_map/ppermute | solution.py:36
  94.8 2.9 %shard_map.96 = bf16[256,512]{1,0:T(8,128)(2,1)} custom-call(s32[2]{0:T(128)S(1)} %pad_add_fusion.par_ref, bf16[256,256]{1,0:T(8,128)(2,1)S(1)} %get-tuple-element.24.dq_ref, bf16[256,256]{1,0:T(8,128)(2,1)} %collective-permute-done.5.dq2_ref, bf16[2,256,256]{2,1,0:T(8,128)(2,1)S(1)} %get-tuple-element.31.dkv_ref, ...), custom_call_target="tpu_custom_call" | custom-call | tf_op jit(solution)/shard_map/pallas_call | solution.py:324
  97.6 0.3 collective-permute-start.11
  98.0 0.8 copy.10.owner_col_ref
  98.8 1.8 %shard_map.97.place_ref = bf16[512,256]{1,0:T(8,128)(2,1)} custom-call(s32[256,1]{1,0:T(8,128)} %copy.10.owner_col_ref, s32[1,256]{1,0:T(1,128)} %bitcast.3), custom_call_target="tpu_custom_call" | custom-call | tf_op jit(solution)/shard_map/pallas_call | solution.py:274
  100.6 2.2 %shard_map.95.own_ref = f32[256,512]{1,0:T(8,128)S(1)} custom-call(s32[2]{0:T(128)S(1)} %pad_add_fusion.par_ref, bf16[256,256]{1,0:T(8,128)(2,1)S(1)} %get-tuple-element.24.dq_ref, bf16[256,256]{1,0:T(8,128)(2,1)} %collective-permute-done.5.dq2_ref, bf16[2,256,256]{2,1,0:T(8,128)(2,1)S(1)} %get-tuple-element.31.dkv_ref, ...), custom_call_target="tpu_custom_call" | custom-call | tf_op jit(solution)/shard_map/pallas_call | solution.py:328
  102.8 0.8 copy-done.3
  103.6 1.9 %collective-permute-done.11.got_ref = bf16[256,512]{1,0:T(8,128)(2,1)} collective-permute-done((bf16[256,512]{1,0:T(8,128)(2,1)}, bf16[256,512]{1,0:T(8,128)(2,1)}, u32[]{:S(2)}, u32[]{:S(2)}) %collective-permute-start.11) | collective-permute-done | bytes 262176 | tf_op jit(solution)/shard_map/ppermute | solution.py:327
  105.5 2.3 %shard_map.98 = bf16[512,512]{1,0:T(8,128)(2,1)} custom-call(f32[256,512]{1,0:T(8,128)} %copy-done.3, bf16[256,512]{1,0:T(8,128)(2,1)} %collective-permute-done.11.got_ref, bf16[512,256]{1,0:T(8,128)(2,1)} %shard_map.97.place_ref), custom_call_target="tpu_custom_call" | custom-call | tf_op jit(solution)/shard_map/pallas_call | solution.py:331
  107.8 1.2 all_to_all.8
  109.0 25.8 %all_to_all.12 = bf16[128,4,512]{2,1,0:T(4,128)(2,1)S(1)} all-to-all(bf16[128,4,512]{2,1,0:T(4,128)(2,1)S(1)} %all_to_all.8), channel_id=1, replica_groups=mesh['blk'=128,'head'=2] {'blk'}, dimensions={0} | all-to-all | bytes 1048576 | tf_op jit(solution)/shard_map/all_to_all | solution.py:334
  134.8 0.9 all_to_all.10
  (25 shorter events, 0.2 us)
Async XLA Ops:
  0.0 0.7 copy-start.8
  0.7 0.9 copy-start.4
  1.6 0.9 copy-start.5
  2.6 0.9 copy-start.6
  3.5 0.9 copy-start.7
  5.2 4.9 %collective-permute-start = (bf16[272,1024]{1,0:T(8,128)(2,1)S(1)}, bf16[272,1024]{1,0:T(8,128)(2,1)S(1)}, u32[]{:S(2)}, u32[]{:S(2)}) collective-permute-start(bf16[272,1024]{1,0:T(8,128)(2,1)S(1)} %shard_map.91), channel_id=1, source_target_pairs={{0,2},{2,0},{4,6},{6,4},{8,10},{10,8},{12,14},{14,12},{16,18},{18,... | collective-permute-start | bytes 1671176 | tf_op jit(solution)/shard_map/ppermute | solution.py:36
  10.8 31.1 %collective-permute-start.2 = (bf16[2,2,256,256]{3,2,1,0:T(8,128)(2,1)S(1)}, bf16[2,2,256,256]{3,2,1,0:T(8,128)(2,1)S(1)}, u32[]{:S(2)}, u32[]{:S(2)}) collective-permute-start(bf16[2,2,256,256]{3,2,1,0:T(8,128)(2,1)S(1)} %get-tuple-element.20.mid_ref), channel_id=1, source_target_pairs={{0,4},{2,6},{4,8},{6,10},{8,12},{10,14},{12,16},{14,18},{16,20},{1... | collective-permute-start | bytes 1572872 | tf_op jit(solution)/shard_map/ppermute | solution.py:31
  10.9 31.0 %collective-permute-start.3 = (bf16[2,2,256,256]{3,2,1,0:T(8,128)(2,1)S(1)}, bf16[2,2,256,256]{3,2,1,0:T(8,128)(2,1)S(1)}, u32[]{:S(2)}, u32[]{:S(2)}) collective-permute-start(bf16[2,2,256,256]{3,2,1,0:T(8,128)(2,1)S(1)} %get-tuple-element.20.mid_ref), channel_id=1, source_target_pairs={{0,252},{2,254},{4,0},{6,2},{8,4},{10,6},{12,8},{14,10},{16,12},{1... | collective-permute-start | bytes 1572872 | tf_op jit(solution)/shard_map/ppermute | solution.py:31
  19.7 19.1 %collective-permute-start.1 = (bf16[2,256,256]{2,1,0:T(8,128)(2,1)S(1)}, bf16[2,256,256]{2,1,0:T(8,128)(2,1)S(1)}, u32[]{:S(2)}, u32[]{:S(2)}) collective-permute-start(bf16[2,256,256]{2,1,0:T(8,128)(2,1)S(1)} %get-tuple-element.19), channel_id=1, source_target_pairs={{0,8},{2,10},{4,12},{6,14},{8,16},{10,18},{12,20},{14,22},{16,24},... | collective-permute-start | bytes 786440 | tf_op jit(solution)/shard_map/ppermute | solution.py:31
  19.7 22.2 %collective-permute-start.4 = (bf16[2,256,256]{2,1,0:T(8,128)(2,1)S(1)}, bf16[2,256,256]{2,1,0:T(8,128)(2,1)S(1)}, u32[]{:S(2)}, u32[]{:S(2)}) collective-permute-start(bf16[2,256,256]{2,1,0:T(8,128)(2,1)S(1)} %get-tuple-element.21), channel_id=1, source_target_pairs={{0,248},{2,250},{4,252},{6,254},{8,0},{10,2},{12,4},{14,6},{16,8},... | collective-permute-start | bytes 786440 | tf_op jit(solution)/shard_map/ppermute | solution.py:31
  41.9 52.9 %copy-start.2 = (bf16[1024,512]{1,0:T(8,128)(2,1)S(1)}, bf16[1024,512]{1,0:T(8,128)(2,1)}, u32[]{:S(2)}) copy-start(bf16[1024,512]{1,0:T(8,128)(2,1)} %wv_ref.3) | copy-start | bytes 3145732
  57.7 26.4 %collective-permute-start.6 = (bf16[2,2,256,256]{3,2,1,0:T(8,128)(2,1)S(1)}, bf16[2,2,256,256]{3,2,1,0:T(8,128)(2,1)S(1)}, u32[]{:S(2)}, u32[]{:S(2)}) collective-permute-start(bf16[2,2,256,256]{3,2,1,0:T(8,128)(2,1)S(1)} %get-tuple-element.27), channel_id=1, source_target_pairs={{0,252},{2,254},{4,0},{6,2},{8,4},{10,6},{12,8},{14,10},{16,12},{1... | collective-permute-start | bytes 1572872 | tf_op jit(solution)/shard_map/ppermute | solution.py:31
  60.3 23.8 %collective-permute-start.7 = (bf16[2,2,256,256]{3,2,1,0:T(8,128)(2,1)S(1)}, bf16[2,2,256,256]{3,2,1,0:T(8,128)(2,1)S(1)}, u32[]{:S(2)}, u32[]{:S(2)}) collective-permute-start(bf16[2,2,256,256]{3,2,1,0:T(8,128)(2,1)S(1)} %get-tuple-element.28), channel_id=1, source_target_pairs={{0,4},{2,6},{4,8},{6,10},{8,12},{10,14},{12,16},{14,18},{16,20},{1... | collective-permute-start | bytes 1572872 | tf_op jit(solution)/shard_map/ppermute | solution.py:31
  60.3 23.2 %collective-permute-start.8 = (bf16[2,256,256]{2,1,0:T(8,128)(2,1)S(1)}, bf16[2,256,256]{2,1,0:T(8,128)(2,1)S(1)}, u32[]{:S(2)}, u32[]{:S(2)}) collective-permute-start(bf16[2,256,256]{2,1,0:T(8,128)(2,1)S(1)} %get-tuple-element.29), channel_id=1, source_target_pairs={{0,248},{2,250},{4,252},{6,254},{8,0},{10,2},{12,4},{14,6},{16,8},... | collective-permute-start | bytes 786440 | tf_op jit(solution)/shard_map/ppermute | solution.py:31
  68.0 16.1 %collective-permute-start.9 = (bf16[2,256,256]{2,1,0:T(8,128)(2,1)S(1)}, bf16[2,256,256]{2,1,0:T(8,128)(2,1)S(1)}, u32[]{:S(2)}, u32[]{:S(2)}) collective-permute-start(bf16[2,256,256]{2,1,0:T(8,128)(2,1)S(1)} %get-tuple-element.30), channel_id=1, source_target_pairs={{0,8},{2,10},{4,12},{6,14},{8,16},{10,18},{12,20},{14,22},{16,24},... | collective-permute-start | bytes 786440 | tf_op jit(solution)/shard_map/ppermute | solution.py:31
  84.1 10.6 %copy-start = (bf16[1024,512]{1,0:T(8,128)(2,1)S(1)}, bf16[1024,512]{1,0:T(8,128)(2,1)}, u32[]{:S(2)}) copy-start(bf16[1024,512]{1,0:T(8,128)(2,1)} %wq_ref.3) | copy-start | bytes 3145732
  84.2 10.6 %copy-start.1 = (bf16[1024,512]{1,0:T(8,128)(2,1)S(1)}, bf16[1024,512]{1,0:T(8,128)(2,1)}, u32[]{:S(2)}) copy-start(bf16[1024,512]{1,0:T(8,128)(2,1)} %wk_ref.3) | copy-start | bytes 3145732
  85.0 9.7 %collective-permute-start.10 = (bf16[2,256,256]{2,1,0:T(8,128)(2,1)}, bf16[2,256,256]{2,1,0:T(8,128)(2,1)}, u32[]{:S(2)}, u32[]{:S(2)}) collective-permute-start(bf16[2,256,256]{2,1,0:T(8,128)(2,1)} %get-tuple-element.32), channel_id=1, source_target_pairs={{0,2},{2,0},{4,6},{6,4},{8,10},{10,8},{12,14},{14,12},{16,18},{18,... | collective-permute-start | bytes 786440 | tf_op jit(solution)/shard_map/ppermute | solution.py:36
  93.0 1.7 %collective-permute-start.5 = (bf16[256,256]{1,0:T(8,128)(2,1)}, bf16[256,256]{1,0:T(8,128)(2,1)}, u32[]{:S(2)}, u32[]{:S(2)}) collective-permute-start(bf16[256,256]{1,0:T(8,128)(2,1)} %get-tuple-element.25), channel_id=1, source_target_pairs={{0,2},{2,0},{4,6},{6,4},{8,10},{10,8},{12,14},{14,12},{16,18},{18,... | collective-permute-start | bytes 393224 | tf_op jit(solution)/shard_map/ppermute | solution.py:36
  94.8 3.2 %copy-start.9 = (s32[256,1]{0,1:T(1,128)S(1)}, s32[256,1]{0,1:T(1,128)}, u32[]{:S(2)}) copy-start(s32[256,1]{0,1:T(1,128)} %param.17) | copy-start | bytes 3076
  97.6 7.8 %collective-permute-start.11 = (bf16[256,512]{1,0:T(8,128)(2,1)}, bf16[256,512]{1,0:T(8,128)(2,1)}, u32[]{:S(2)}, u32[]{:S(2)}) collective-permute-start(bf16[256,512]{1,0:T(8,128)(2,1)} %shard_map.96), channel_id=1, source_target_pairs={{0,1},{1,0},{2,3},{3,2},{4,5},{5,4},{6,7},{7,6},{8,9},{9,8},{10,11... | collective-permute-start | bytes 786440 | tf_op jit(solution)/shard_map/ppermute | solution.py:327
  102.8 0.8 copy-start.3

commit v2 on v0

v2 whole, which is shorter than its diff:
```python
import functools
import math

import jax
import jax.numpy as jnp
import numpy as np
from jax import lax
from jax.experimental import pallas as pl
from jax.experimental.pallas import tpu as pltpu
from jax.sharding import PartitionSpec as P

HD = 64
BLOCK = 128
REACH = 3
SPAN = 2 * REACH + 1
LOG2E = math.log2(math.e)
MASKED = -1e30
FLOOR = -1e29
CAP = 4
BF = jnp.bfloat16
F32 = jnp.float32
NT = (((1,), (1,)), ((), ()))
NN = (((1,), (0,)), ((), ()))
TN = (((0,), (0,)), ((), ()))


def dot(a, b, dims):
    return lax.dot_general(a, b, dims, preferred_element_type=F32)


def core_swapped(value):
    count = lax.axis_size("blk")
    return lax.ppermute(value, "blk", [(s, s ^ 1) for s in range(count)])


def chip_swapped(value, odd):
    count = lax.axis_size("blk")
    ahead = [2 if (s // 2) % 2 == odd else -2 for s in range(count)]
    return lax.ppermute(value, "blk", [(s, (s + ahead[s]) % count) for s in range(count)])


def bias_rows(adj_ref):
    shape = (16, 2 * BLOCK)
    row = lax.broadcasted_iota(jnp.int32, shape, 0)
    query_block = lax.broadcasted_iota(jnp.int32, shape, 1) // BLOCK
    allowed = row == 2 * REACH + query_block
    for c in range(2 * SPAN):
        for b in range(2):
            hit = (row == c) & (query_block == b) & (adj_ref[b, c] > 0)
            allowed = allowed | hit
    return jnp.where(allowed, 0.0, MASKED)


def pack_kernel(ids_ref, adj_ref, k_ref, v_ref, q_ref, g_ref, send_ref, own_ref, sems):
    rows, cols = k_ref.shape
    half = cols // 2
    copies = []
    for to_ref, which in ((send_ref, 1 - ids_ref[0]), (own_ref, ids_ref[0])):
        at = pl.ds(pl.multiple_of(which * half, half), half)
        for n, from_ref in enumerate((k_ref, v_ref, q_ref, g_ref)):
            copies.append(
                pltpu.make_async_copy(
                    from_ref.at[:, at], to_ref.at[0:rows, n * half : (n + 1) * half], sems.at[len(copies)]
                )
            )
    for copy in copies:
        copy.start()
    bias = bias_rows(adj_ref).astype(BF)
    for to_ref in (send_ref, own_ref):
        to_ref[rows : rows + 16, 0:half] = bias
        to_ref[rows : rows + 16, half:] = jnp.zeros((16, 3 * half), BF)
    for copy in copies:
        copy.wait()


def order_kernel(ids_ref, own_ref, got_ref, a_ref, b_ref, qg_ref, bias_ref):
    rows = a_ref.shape[1]
    cols = a_ref.shape[2]
    par = ids_ref[0]
    scale = 1.0 / math.sqrt(HD)
    for sector, from_ref in ((par, own_ref), (1 - par, got_ref)):
        qg_ref[0, sector] = from_ref[0:rows, 2 * cols : 3 * cols] * scale
        qg_ref[1, sector] = from_ref[0:rows, 3 * cols : 4 * cols]
        bias_ref[sector] = from_ref[rows : rows + 16, 0:cols].astype(F32)
    b_own = par == ids_ref[1]
    for which in range(2):
        own = own_ref[0:rows, which * cols : (which + 1) * cols]
        got = got_ref[0:rows, which * cols : (which + 1) * cols]
        a_ref[which] = jnp.where(b_own, got, own)
        b_ref[which] = jnp.where(b_own, own, got)


def one_head(pair_ref, h):
    value = pair_ref[...]
    lane_head = lax.broadcasted_iota(jnp.int32, value.shape, 1) // HD
    return jnp.where(lane_head == h, value, 0.0).astype(BF)


def bias_pair_of(bias_ref, t, j):
    return [bias_ref[t, pl.ds(2 * j + b, 1), :] for b in range(2)]


def fold_stats(stats, key_value, query_head, grad_head, bias_pair):
    scores = dot(key_value[0], query_head, NT)
    grads = dot(key_value[1], grad_head, NT)
    top, total, delta = stats
    for b in range(2):
        at = slice(b * BLOCK, (b + 1) * BLOCK)
        new_top = jnp.maximum(top, jnp.max(scores[at], axis=0, keepdims=True) + bias_pair[b])
        weight = jnp.exp2(scores[at] * LOG2E + (bias_pair[b] - new_top) * LOG2E)
        shrink = jnp.exp2((top - new_top) * LOG2E)
        total = jnp.sum(weight, axis=0, keepdims=True) + total * shrink
        delta = jnp.sum(weight * grads[at], axis=0, keepdims=True) + delta * shrink
        top = new_top
    return (top, total, delta), scores, grads


def near_stats_kernel(ids_ref, *refs):
    windows = refs[0:6]
    qg_ref, bias_ref, stats_ref = refs[6:9]
    odd = ids_ref[1]
    names = (4 - odd, 3 + odd, 5 - 3 * odd, 2 + 3 * odd, 6 - 5 * odd, 1 + 5 * odd)
    rows = qg_ref.shape[2]
    for t in range(2):
        for h in range(2):
            qh = one_head(qg_ref.at[0, t], h)
            gh = one_head(qg_ref.at[1, t], h)
            zero = jnp.zeros((1, rows), F32)
            stats = (zero + FLOOR, zero, zero)
            for w, window in zip(names, windows):
                stats, _, _ = fold_stats(stats, window, qh, gh, bias_pair_of(bias_ref, t, w - t))
            for row in range(3):
                stats_ref[t, h, row : row + 1, :] = stats[row]


def head_rows_of(first, second):
    row_head = lax.broadcasted_iota(jnp.int32, first.shape, 0) // HD
    return jnp.where(row_head == 0, first, second)


def query_grad(keys_t, grads, rows):
    both = dot(keys_t, grads, NN)
    return head_rows_of(both[:, 0:rows], both[:, rows:])


def flipped(value):
    return jnp.transpose(value.astype(F32)).astype(BF)


def far_kernel(
    ids_ref, e_ref, o_ref, qg_ref, bias_ref, stats_ref, final_ref, de_ref, do_ref, dq_ref,
    ps_ref, ds_ref, qs_ref, gs_ref,
):
    rows = qg_ref.shape[2]
    odd = ids_ref[1]
    for n, (t, window, out_ref) in enumerate(((1 - odd, e_ref, de_ref), (odd, o_ref, do_ref))):
        for h in range(2):
            cols = slice(h * rows, (h + 1) * rows)
            qh = one_head(qg_ref.at[0, t], h)
            gh = one_head(qg_ref.at[1, t], h)
            qs_ref[n, cols, :] = qh
            gs_ref[n, cols, :] = gh
            bias_pair = bias_pair_of(bias_ref, t, (SPAN - 1) * t)
            stats = tuple(stats_ref[t, h, row : row + 1, :] for row in range(3))
            (top, total, delta), scores, grads = fold_stats(stats, window, qh, gh, bias_pair)
            log_total = top * LOG2E + jnp.log2(total)
            delta = delta / total
            final_ref[t, h, 0:1, :] = log_total
            final_ref[t, h, 1:2, :] = delta
            for b in range(2):
                at = slice(b * BLOCK, (b + 1) * BLOCK)
                prob = jnp.exp2(scores[at] * LOG2E + (bias_pair[b] * LOG2E - log_total))
                ps_ref[n, at, cols] = prob.astype(BF)
                ds_ref[n, at, cols] = (prob * (grads[at] - delta)).astype(BF)
        out_ref[0] = dot(ds_ref[n], qs_ref[n], NN).astype(BF)
        out_ref[1] = dot(ps_ref[n], gs_ref[n], NN).astype(BF)
        dq_ref[0, t] = query_grad(flipped(window[0]), ds_ref[n], rows)


def shared_kernel(names, qg_ref, bias_ref, final_ref, windows, outs, ps_ref, ds_ref, qs_ref, gs_ref, kt_ref):
    rows = qg_ref.shape[2]
    for t in range(2):
        for h in range(2):
            block = 2 * t + h
            cols = slice(block * rows, (block + 1) * rows)
            qs_ref[cols, :] = one_head(qg_ref.at[0, t], h)
            gs_ref[cols, :] = one_head(qg_ref.at[1, t], h)
    for n, (w, window) in enumerate(zip(names, windows)):
        keys = slice(n * rows, (n + 1) * rows)
        kt_ref[:, keys] = flipped(window[0])
        for t in range(2):
            for h in range(2):
                block = 2 * t + h
                cols = slice(block * rows, (block + 1) * rows)
                scores = dot(window[0], qs_ref[cols, :], NT)
                grads = dot(window[1], gs_ref[cols, :], NT)
                log_total = final_ref[t, h, 0:1, :]
                delta = final_ref[t, h, 1:2, :]
                bias_pair = bias_pair_of(bias_ref, t, w - t)
                for b in range(2):
                    at = slice(b * BLOCK, (b + 1) * BLOCK)
                    to = slice(n * rows + b * BLOCK, n * rows + (b + 1) * BLOCK)
                    prob = jnp.exp2(scores[at] * LOG2E + (bias_pair[b] * LOG2E - log_total))
                    ps_ref[to, cols] = prob.astype(BF)
                    ds_ref[to, cols] = (prob * (grads[at] - delta)).astype(BF)
        out_ref = outs[n]
        out_ref[0] = dot(ds_ref[keys, :], qs_ref[...], NN).astype(out_ref.dtype)
        out_ref[1] = dot(ps_ref[keys, :], gs_ref[...], NN).astype(out_ref.dtype)
    return [
        query_grad(kt_ref[...], ds_ref[:, 2 * t * rows : 2 * (t + 1) * rows], rows) for t in range(2)
    ]


def near_kernel(ids_ref, ea_ref, oa_ref, eb_ref, ob_ref, qg_ref, bias_ref, final_ref, part_ref, *refs):
    outs, dq_ref, scratch = refs[0:4], refs[4], refs[5:]
    odd = ids_ref[1]
    names = (5 - 3 * odd, 2 + 3 * odd, 6 - 5 * odd, 1 + 5 * odd)
    grads = shared_kernel(names, qg_ref, bias_ref, final_ref, (ea_ref, oa_ref, eb_ref, ob_ref), outs, *scratch)
    for t in range(2):
        dq_ref[0, t] = part_ref[0, t] + grads[t]


def local_kernel(ids_ref, a_ref, b_ref, qg_ref, bias_ref, final_ref, part_ref, *refs):
    outs, (dq_own_ref, dq_send_ref), scratch = refs[0:2], refs[2:4], refs[4:]
    odd = ids_ref[1]
    grads = shared_kernel((4 - odd, 3 + odd), qg_ref, bias_ref, final_ref, (a_ref, b_ref), outs, *scratch)
    total = [part_ref[0, t] + grads[t] for t in range(2)]
    first = ids_ref[0] == 0
    scale = 1.0 / math.sqrt(HD)
    dq_own_ref[...] = jnp.transpose(jnp.where(first, total[0], total[1]) * scale).astype(BF)
    dq_send_ref[...] = jnp.transpose(jnp.where(first, total[1], total[0]) * scale).astype(BF)


def joined(first, second):
    return (first.astype(F32) + second.astype(F32)).astype(BF)


def total_kernel(ids_ref, a_ref, b_ref, ea_ref, oa_ref, eb_ref, ob_ref, keep_ref, send_ref):
    b_own = ids_ref[0] == ids_ref[1]
    for which in range(2):
        value_a = a_ref[which] + ob_ref[which].astype(F32) + ea_ref[which].astype(F32)
        value_b = b_ref[which] + eb_ref[which].astype(F32) + oa_ref[which].astype(F32)
        keep_ref[which] = jnp.where(b_own, value_b, value_a).astype(BF)
        send_ref[which] = jnp.where(b_own, value_a, value_b).astype(BF)


def query_kernel(ids_ref, own_ref, got_ref, weight_ref, other_out_ref, own_out_ref):
    first = ids_ref[0] == 0
    half = own_ref.shape[1]
    low = jnp.where(first, own_ref[...], got_ref[...])
    high = jnp.where(first, got_ref[...], own_ref[...])
    cols = own_out_ref.shape[1]
    here = ids_ref[2]
    for out_ref, which in ((other_out_ref, 1 - here), (own_out_ref, here)):
        at = pl.ds(pl.multiple_of(which * cols, cols), cols)
        out_ref[...] = dot(low, weight_ref[at, 0:half], NT) + dot(high, weight_ref[at, half:], NT)


def add_kernel(ids_ref, base_ref, grads_ref, wk_ref, wv_ref, out_ref):
    value = base_ref[...] + dot(grads_ref[0], wk_ref[...], NT) + dot(grads_ref[1], wv_ref[...], NT)
    out_ref[...] = value.astype(out_ref.dtype)


def both_kernel(ids_ref, base_ref, keep_ref, gave_ref, wk_ref, wv_ref, out_ref):
    first = ids_ref[0] == 0
    half = keep_ref.shape[2]
    value = base_ref[...]
    for which, weight in ((0, wk_ref), (1, wv_ref)):
        low = jnp.where(first, keep_ref[which], gave_ref[which])
        high = jnp.where(first, gave_ref[which], keep_ref[which])
        value = value + dot(low, weight[:, 0:half], NT) + dot(high, weight[:, half:], NT)
    out_ref[...] = value


def route_kernel(owner_col_ref, owner_row_ref, label_ref, place_ref):
    rows = owner_col_ref.shape[0]
    owner_row = owner_row_ref[...]
    earlier = lax.broadcasted_iota(jnp.int32, (rows, rows), 0) < lax.broadcasted_iota(jnp.int32, (rows, rows), 1)
    same = (owner_col_ref[...] == owner_row) & earlier
    rank = jnp.sum(same.astype(jnp.int32), axis=0, keepdims=True)
    target = owner_row * CAP + rank
    place_ref[...] = jnp.where(label_ref[...] == target, 1.0, 0.0).astype(BF)


def scatter_kernel(own_ref, got_ref, place_ref, out_ref):
    value = (own_ref[...] + got_ref[...].astype(F32)).astype(BF)
    out_ref[...] = dot(place_ref[...], value, NN).astype(BF)


def spread_order(count):
    groups = [int(g) for g in np.random.default_rng(1).permutation(count // 4)]
    return [4 * g + i for g in groups for i in range(4)]


def restore_kernel(from_ref, out_ref, *, home):
    rows = out_ref.shape[0] // len(home)
    for i, g in enumerate(home):
        out_ref[i * rows : (i + 1) * rows, :] = from_ref[g * rows : (g + 1) * rows, :]


def cost(flops, moved_bytes, exps=0):
    return pl.CostEstimate(flops=flops, bytes_accessed=moved_bytes, transcendentals=exps)


def on_device(query, key, value, out_grad, q_weight, k_weight, v_weight, adjacency, owner):
    rows, cols = query.shape
    half = cols // 2
    pair = 2 * HD
    sds = jax.ShapeDtypeStruct
    block = lax.axis_index("blk")
    ids = jnp.stack([block % 2, (block // 2) % 2, lax.axis_index("head")]).astype(jnp.int32)
    smem = pl.BlockSpec(memory_space=pltpu.SMEM)
    hbm = pl.BlockSpec(memory_space=pltpu.HBM)

    def call(kernel, outs, grid, in_specs, out_specs, scratch=(), scalars=1, estimate=None, limit=16):
        return pl.pallas_call(
            kernel,
            out_shape=outs,
            grid_spec=pltpu.PrefetchScalarGridSpec(
                num_scalar_prefetch=scalars, grid=grid, in_specs=in_specs, out_specs=out_specs,
                scratch_shapes=list(scratch),
            ),
            compiler_params=pltpu.CompilerParams(vmem_limit_bytes=limit << 20),
            cost_estimate=estimate,
        )

    def whole(*shape):
        return pl.BlockSpec(shape, lambda i, *p: (0,) * len(shape))

    packed = sds((rows + 16, 4 * half), BF)
    send, own = call(
        pack_kernel, (packed, packed), (1,), [smem] + [hbm] * 4, (whole(rows + 16, 4 * half),) * 2,
        scratch=(pltpu.SemaphoreType.DMA((8,)),), limit=60,
    )(ids, adjacency, key, value, query, out_grad)
    got = core_swapped(send)
    kv_shape = sds((2, rows, half), BF)
    kv_whole = whole(2, rows, half)
    a, b, qg, bias = call(
        order_kernel,
        (kv_shape, kv_shape, sds((2, 2, rows, half), BF), sds((2, 16, rows), F32)),
        (1,),
        [whole(rows + 16, 4 * half)] * 2,
        (kv_whole, kv_whole, whole(2, 2, rows, half), whole(2, 16, rows)),
    )(ids, own, got)
    ea = chip_swapped(a, 0)
    oa = chip_swapped(b, 1)
    eb = chip_swapped(b, 0)
    ob = chip_swapped(a, 1)
    ef = chip_swapped(oa, 0)
    of = chip_swapped(ea, 1)

    count = lax.axis_size("blk")
    slots = CAP * count
    order = spread_order(count)
    labels = jnp.asarray(np.array([[CAP * s + r] for s in order for r in range(CAP)], np.int32))
    place = call(
        route_kernel, sds((slots, rows), BF), (1,),
        [whole(rows, 1), whole(1, rows), whole(slots, 1)], whole(slots, rows), scalars=0,
        estimate=cost(rows * rows * 8, 1 << 20),
    )(owner, owner.reshape(1, rows), labels)

    pairs = half // pair
    win = pl.BlockSpec((2, rows, pair), lambda i, p: (0, 0, i))
    near = pl.BlockSpec((2, 2, rows, pair), lambda i, p: (0, 0, 0, i))
    dq_spec = pl.BlockSpec((rows, pair), lambda i, p: (0, i))
    stat_spec = pl.BlockSpec((2, 2, 8, rows), lambda i, p: (0, i, 0, 0))
    bias_spec = whole(2, 16, rows)
    stat_shape = sds((2, 2 * pairs, 8, rows), F32)
    step = 2 * rows * rows * HD * 4
    part_shape = sds((pairs, 2, pair, rows), F32)
    part_spec = pl.BlockSpec((1, 2, pair, rows), lambda i, p: (i, 0, 0, 0))

    def scratch(blocks):
        return (
            pltpu.VMEM((blocks * rows, 4 * rows), BF),
            pltpu.VMEM((blocks * rows, 4 * rows), BF),
            pltpu.VMEM((4 * rows, pair), BF),
            pltpu.VMEM((4 * rows, pair), BF),
            pltpu.VMEM((pair, blocks * rows), BF),
        )

    stats = call(
        near_stats_kernel, stat_shape, (pairs,), [win] * 6 + [near, bias_spec], stat_spec,
        estimate=cost(24 * step, 6 << 20),
    )(ids, a, b, ea, oa, eb, ob, qg, bias)
    stats, place = lax.optimization_barrier((stats, place))
    far_probs = pltpu.VMEM((2, rows, 2 * rows), BF)
    far_rows = pltpu.VMEM((2, 2 * rows, pair), BF)
    final, d_ef, d_of, dq_far = call(
        far_kernel, (stat_shape, kv_shape, kv_shape, part_shape), (pairs,),
        [win] * 2 + [near, bias_spec, stat_spec], (stat_spec, win, win, part_spec),
        scratch=(far_probs, far_probs, far_rows, far_rows), estimate=cost(8 * step, 2 << 20),
    )(ids, ef, of, qg, bias, stats)
    back_ef = chip_swapped(d_ef, 0)
    back_of = chip_swapped(d_of, 1)
    d_ea, d_oa, d_eb, d_ob, dq_near = call(
        near_kernel, (kv_shape,) * 4 + (part_shape,), (pairs,), [win] * 4 + [near, bias_spec, stat_spec, part_spec],
        (win,) * 4 + (part_spec,), scratch=scratch(4), estimate=cost(32 * step, 4 << 20),
    )(ids, ea, oa, eb, ob, qg, bias, final, dq_far)
    back_eb = chip_swapped(d_eb, 0)
    back_ob = chip_swapped(d_ob, 1)
    back_ea = chip_swapped(joined(d_ea, back_of), 0)
    back_oa = chip_swapped(joined(d_oa, back_ef), 1)
    own_shape = sds((2, rows, half), F32)
    d_a, d_b, dq_own, dq_send = call(
        local_kernel, (own_shape, own_shape, sds((rows, half), BF), sds((rows, half), BF)), (pairs,),
        [win] * 2 + [near, bias_spec, stat_spec, part_spec], (win, win, dq_spec, dq_spec),
        scratch=scratch(2), estimate=cost(16 * step, 4 << 20),
    )(ids, a, b, qg, bias, final, dq_near)
    dq_got = core_swapped(dq_send)
    q_other, q_own = call(
        query_kernel, (sds((rows, cols), F32), sds((rows, cols), F32)), (1,),
        [whole(rows, half)] * 2 + [whole(2 * cols, cols)], (whole(rows, cols), whole(rows, cols)),
        estimate=cost(2 * rows * cols * 2 * cols, 3 << 20),
    )(ids, dq_own, dq_got, q_weight)
    d_a, q_other, q_own = lax.optimization_barrier((d_a, q_other, q_own))
    keep, give = call(
        total_kernel, (kv_shape, kv_shape), (1,), [kv_whole] * 6, (kv_whole, kv_whole),
    )(ids, d_a, d_b, back_ea, back_oa, back_eb, back_ob)
    gave = core_swapped(give)
    weight_keep = pl.BlockSpec((cols, half), lambda i, p: (1 - p[2], p[0]))
    weight_gave = pl.BlockSpec((cols, half), lambda i, p: (1 - p[2], 1 - p[0]))
    weight_own = pl.BlockSpec((cols, cols), lambda i, p: (p[2], 0))
    add_cost = cost(2 * rows * cols * 2 * half, 2 << 20)
    partial_keep = call(
        add_kernel, sds((rows, cols), F32), (1,), [whole(rows, cols), kv_whole] + [weight_keep] * 2,
        whole(rows, cols), estimate=add_cost,
    )(ids, q_other, keep, k_weight, v_weight)
    partial_other = call(
        add_kernel, sds((rows, cols), BF), (1,), [whole(rows, cols), kv_whole] + [weight_gave] * 2,
        whole(rows, cols), estimate=add_cost,
    )(ids, partial_keep, gave, k_weight, v_weight)
    partial_got = lax.ppermute(partial_other, "head", [(0, 1), (1, 0)])
    partial_own = call(
        both_kernel, sds((rows, cols), F32), (1,),
        [whole(rows, cols)] + [kv_whole] * 2 + [weight_own] * 2, whole(rows, cols),
        estimate=cost(2 * rows * cols * 2 * cols, 2 << 20),
    )(ids, q_own, keep, gave, k_weight, v_weight)
    outgoing = call(
        scatter_kernel, sds((slots, cols), BF), (1,),
        [whole(rows, cols), whole(rows, cols), whole(slots, rows)], whole(slots, cols), scalars=0,
        estimate=cost(2 * slots * rows * cols, 2 << 20),
    )(partial_own, partial_got, place)
    arrived = lax.all_to_all(
        outgoing, "blk", split_axis=0, concat_axis=0, tiled=True, axis_index_groups=[order]
    )
    home = [int(g) for g in np.argsort(np.array(order[::4]) // 4)]
    return call(
        functools.partial(restore_kernel, home=home), sds((slots, cols), BF), (1,), [whole(slots, cols)],
        whole(slots, cols), scalars=0,
    )(arrived)


def solution(mesh):
    return jax.shard_map(
        on_device,
        mesh=mesh,
        in_specs=(
            P("blk", "head"),
            P("blk", "head"),
            P("blk", "head"),
            P("blk", "head"),
            P(None, "head"),
            P(None, "head"),
            P(None, "head"),
            P("blk", None),
            P("blk", None),
        ),
        out_specs=P("blk", "head"),
        check_vma=False,
    )
```

time: 216 us -> 115 us (0.53)
  waiting for transfers between devices: 61.2 us -> 14.3 us
  local copies, waits for them, and re-layouts: 45.4 us -> 1.47 us
  Pallas kernels: 0 us -> 29.6 us
  matrix products: 25.2 us -> 0 us
  between operations: 14 us -> 0.25 us
  starting transfers between devices: 30.5 us -> 42.2 us
  blocking collectives: 33.3 us -> 26.3 us
  other arithmetic: 5.87 us -> 0.74 us
    slice x19 -> x0, local copies, waits for them, and re-layouts: 33.5 us -> none  [the longest x12 21.9 us: split_heads(): window[offset][1].reshape(hit_rows, head_count, HD)]
    ppermute x12 -> x16, waiting for transfers between devices: 44.6 us -> 14.3 us  [the longest x1 6.11 us: on_device(): partial_got = lax.ppermute(partial_other, 'head', [(0, 1), (1, 0)])]
    pallas_call x0 -> x14, Pallas kernels: none -> 29.6 us  [the longest x1 6.38 us: on_device(): call(near_kernel, (kv_shape,) * 4 + (part_shape,), (pairs,), [win] * 4 +...]
    dot_general x45 -> x0, matrix products: 25.2 us -> none  [the longest x7 5.61 us: on_device(): jnp.einsum('ihd,jhd->hij', q_heads, keys_h, preferred_element_type=jnp.fl...]
    reduce_scatter x1 -> x0, waiting for transfers between devices: 16.6 us -> none  [on_device(): lax.psum_scatter(partial_value.astype(jnp.bfloat16), 'head', scatter_dime...]
    ppermute x12 -> x16, starting transfers between devices: 30.5 us -> 42.2 us  [the longest x12 31.7 us: chip_swapped(): lax.ppermute(value, 'blk', [(s, (s + ahead[s]) % count) for s in range(co...]
    unnamed x59 -> x15, local copies, waits for them, and re-layouts: 8.62 us -> 1.22 us
    all_to_all x1, blocking collectives: 33.3 us -> 26.3 us  [on_device(): lax.all_to_all(outgoing, 'blk', split_axis=0, concat_axis=0, tiled=True,...]
  transfers between devices with their start and end apart: 13 -> 16, of which waited for: 8 -> 5; matrix products, arithmetic and copies ran while one was open for 15% -> 0% of each run, Pallas kernels for 0% -> 16%
where the time goes in v2:
time: 115 us
  starting transfers between devices  42.2 us (37%)
  Pallas kernels  29.6 us (26%)
  blocking collectives  26.3 us (23%)
  waiting for transfers between devices  14.3 us (12%)
  local copies, waits for them, and re-layouts  1.47 us (1%)
    ppermute x12, starting transfers between devices, chip_swapped(): lax.ppermute(value, 'blk', [(s, (s + ahead[s]) % count) for s in range(co...  31.7 us
    all_to_all x1, blocking collectives, on_device(): lax.all_to_all(outgoing, 'blk', split_axis=0, concat_axis=0, tiled=True,...  26.3 us
    ppermute x3, starting transfers between devices, core_swapped(): return lax.ppermute(value, 'blk', [(s, s ^ 1) for s in range(count)])  10.1 us
    pallas_call x1, Pallas kernels, on_device(): call(near_kernel, (kv_shape,) * 4 + (part_shape,), (pairs,), [win] * 4 +...  6.38 us
    ppermute x1, waiting for transfers between devices, on_device(): partial_got = lax.ppermute(partial_other, 'head', [(0, 1), (1, 0)])  6.11 us
    pallas_call x1, Pallas kernels, on_device(): call(near_stats_kernel, stat_shape, (pairs,), [win] * 6 + [near, bias_spe...  5.58 us
    ppermute x12, waiting for transfers between devices, chip_swapped(): lax.ppermute(value, 'blk', [(s, (s + ahead[s]) % count) for s in range(co...  5.12 us
    pallas_call x1, Pallas kernels, on_device(): call(local_kernel, (own_shape, own_shape, sds((rows, half), BF), sds((row...  3.89 us
  transfers between devices with their start and end apart: 16, of which 5 were waited for; matrix products, arithmetic and copies ran while one was open for 0% of the time, Pallas kernels for 16%

profile of v2, /device:TPU:1, one launch (start us, length us, event | category | flops | bytes accessed | tf_op | source)
XLA Modules:
  0.0 114.8 jit_solution(13378073039996759216)
XLA Ops:
  0.0 0.6 pad_add_fusion.ids_ref
  0.6 3.7 %shard_map.100 = (bf16[272,1024]{1,0:T(8,128)(2,1)}, bf16[272,1024]{1,0:T(8,128)(2,1)}) custom-call(s32[3]{0:T(128)} %pad_add_fusion.ids_ref, s32[2,14]{1,0:T(2,128)} %adj_ref.1, bf16[256,512]{1,0:T(8,128)(2,1)} %k_ref.1, bf16[256,512]{1,0:T(8,128)(2,1)} %v_ref.1, bf16[256,512]{1,0:T(8,128)(2,1)} %q_ref.1, bf16[256,512]{1,0:T(8,128)(2,1)} %g_ref.1), custom_call_target="tpu_custom_call" | custom-call | tf_op jit(solution)/shard_map/pallas_call | solution.py:331
  4.4 3.3 %collective-permute-start = (bf16[272,1024]{1,0:T(8,128)(2,1)}, bf16[272,1024]{1,0:T(8,128)(2,1)S(1)}, u32[]{:S(2)}, u32[]{:S(2)}) collective-permute-start(bf16[272,1024]{1,0:T(8,128)(2,1)} %get-tuple-element.34), channel_id=1, source_target_pairs={{0,2},{2,0},{4,6},{6,4},{8,10},{10,8},{12,14},{14,12},{16,18},{18,... | collective-permute-start | bytes 1671176 | tf_op jit(solution)/shard_map/ppermute | solution.py:33
  7.7 1.8 %collective-permute-done.got_ref = bf16[272,1024]{1,0:T(8,128)(2,1)S(1)} collective-permute-done((bf16[272,1024]{1,0:T(8,128)(2,1)}, bf16[272,1024]{1,0:T(8,128)(2,1)S(1)}, u32[]{:S(2)}, u32[]{:S(2)}) %collective-permute-start) | collective-permute-done | bytes 557088 | tf_op jit(solution)/shard_map/ppermute | solution.py:33
  9.5 1.1 copy-done.3
  10.6 0.6 shard_map.101
  11.3 9.5 %collective-permute-start.1 = (bf16[2,256,256]{2,1,0:T(8,128)(2,1)S(1)}, bf16[2,256,256]{2,1,0:T(8,128)(2,1)S(1)}, u32[]{:S(2)}, u32[]{:S(2)}) collective-permute-start(bf16[2,256,256]{2,1,0:T(8,128)(2,1)S(1)} %get-tuple-element.36.refs_1_.b_ref), channel_id=1, source_target_pairs={{0,252},{2,254},{4,8},{6,10},{8,4},{10,6},{12,16},{14,18},{16,12},... | collective-permute-start | bytes 786440 | tf_op jit(solution)/shard_map/ppermute | solution.py:39
  20.8 7.2 %collective-permute-start.4 = (bf16[2,256,256]{2,1,0:T(8,128)(2,1)S(1)}, bf16[2,256,256]{2,1,0:T(8,128)(2,1)S(1)}, u32[]{:S(2)}, u32[]{:S(2)}) collective-permute-start(bf16[2,256,256]{2,1,0:T(8,128)(2,1)S(1)} %collective-permute-done.3.refs_2_.ea_ref), channel_id=1, source_target_pairs={{0,252},{2,254},{4,8},{6,10},{8,4},{10,6},{12,16},{14,18},{16,12},... | collective-permute-start | bytes 786440 | tf_op jit(solution)/shard_map/ppermute | solution.py:39
  28.1 0.2 shard_map.103.place_ref
  28.3 5.1 %collective-permute-done.6.refs_5_.ob_ref = bf16[2,256,256]{2,1,0:T(8,128)(2,1)S(1)} collective-permute-done((bf16[2,256,256]{2,1,0:T(8,128)(2,1)S(1)}, bf16[2,256,256]{2,1,0:T(8,128)(2,1)S(1)}, u32[]{:S(2)}, u32[]{:S(2)}) %collective-permute-start.6) | collective-permute-done | bytes 262176 | tf_op jit(solution)/shard_map/ppermute | solution.py:39
  33.4 5.6 %shard_map.102.stats_ref = f32[2,4,8,256]{3,2,1,0:T(8,128)S(1)} custom-call(s32[3]{0:T(128)S(1)} %copy-done.5, bf16[2,256,256]{2,1,0:T(8,128)(2,1)S(1)} %get-tuple-element.35.refs_0_.a_ref, bf16[2,256,256]{2,1,0:T(8,128)(2,1)S(1)} %get-tuple-element.36.refs_1_.b_ref, bf16[2,256,256]{2,1,0:T(8,128)(2,1)S(1)} %collective-permute-done.3.refs_2_.ea_ref, ...), custom_call_target="tpu_custom_call" | custom-call | flops 805306368 | bytes 6291456 | tf_op jit(solution)/shard_map/pallas_call | solution.py:382
  39.0 3.6 %shard_map.104 = (f32[2,4,8,256]{3,2,1,0:T(8,128)S(1)}, bf16[2,256,256]{2,1,0:T(8,128)(2,1)S(1)}, bf16[2,256,256]{2,1,0:T(8,128)(2,1)S(1)}, f32[2,2,128,256]{3,2,1,0:T(8,128)S(1)}) custom-call(s32[3]{0:T(128)S(1)} %copy-done.5, bf16[2,256,256]{2,1,0:T(8,128)(2,1)S(1)} %collective-permute-done.2.e_ref, bf16[2,256,256]{2,1,0:T(8,128)(2,1)S(1)} %collective-permute-done.4.o_ref, ...), custom_call_target="tpu_custom_call" | custom-call | flops 268435456 | bytes 2097152 | tf_op jit(solution)/shard_map/pallas_call | solution.py:389
  42.6 6.0 %collective-permute-start.8 = (bf16[2,256,256]{2,1,0:T(8,128)(2,1)S(1)}, bf16[2,256,256]{2,1,0:T(8,128)(2,1)S(1)}, u32[]{:S(2)}, u32[]{:S(2)}) collective-permute-start(bf16[2,256,256]{2,1,0:T(8,128)(2,1)S(1)} %get-tuple-element.52), channel_id=1, source_target_pairs={{0,252},{2,254},{4,8},{6,10},{8,4},{10,6},{12,16},{14,18},{16,12},... | collective-permute-start | bytes 786440 | tf_op jit(solution)/shard_map/ppermute | solution.py:39
  48.6 6.4 %shard_map.105 = (bf16[2,256,256]{2,1,0:T(8,128)(2,1)S(1)}, bf16[2,256,256]{2,1,0:T(8,128)(2,1)S(1)}, bf16[2,256,256]{2,1,0:T(8,128)(2,1)S(1)}, bf16[2,256,256]{2,1,0:T(8,128)(2,1)S(1)}, f32[2,2,128,256]{3,2,1,0:T(8,128)S(1)}) custom-call(s32[3]{0:T(128)S(1)} %copy-done.5, bf16[2,256,256]{2,1,0:T(8,128)(2,1)S(1)} %collective-permute-done.3.refs_2_.ea_ref, ...), custom_call_target="tpu_custom_call" | custom-call | flops 1073741824 | bytes 4194304 | tf_op jit(solution)/shard_map/pallas_call | solution.py:396
  55.0 1.6 %collective-permute-start.12 = (bf16[2,256,256]{2,1,0:T(8,128)(2,1)S(1)}, bf16[2,256,256]{2,1,0:T(8,128)(2,1)S(1)}, u32[]{:S(2)}, u32[]{:S(2)}) collective-permute-start(bf16[2,256,256]{2,1,0:T(8,128)(2,1)S(1)} %get-tuple-element.55), channel_id=1, source_target_pairs={{0,4},{2,6},{4,0},{6,2},{8,12},{10,14},{12,8},{14,10},{16,20},{18,... | collective-permute-start | bytes 786440 | tf_op jit(solution)/shard_map/ppermute | solution.py:39
  56.5 1.2 %collective-permute-start.13 = (bf16[2,256,256]{2,1,0:T(8,128)(2,1)S(1)}, bf16[2,256,256]{2,1,0:T(8,128)(2,1)S(1)}, u32[]{:S(2)}, u32[]{:S(2)}) collective-permute-start(bf16[2,256,256]{2,1,0:T(8,128)(2,1)S(1)} %get-tuple-element.56), channel_id=1, source_target_pairs={{0,252},{2,254},{4,8},{6,10},{8,4},{10,6},{12,16},{14,18},{16,12},... | collective-permute-start | bytes 786440 | tf_op jit(solution)/shard_map/ppermute | solution.py:39
  58.1 6.0 %collective-permute-start.11 = (bf16[2,256,256]{2,1,0:T(8,128)(2,1)S(1)}, bf16[2,256,256]{2,1,0:T(8,128)(2,1)S(1)}, u32[]{:S(2)}, u32[]{:S(2)}) collective-permute-start(bf16[2,256,256]{2,1,0:T(8,128)(2,1)S(1)} %add_convert_fusion), channel_id=1, source_target_pairs={{0,252},{2,254},{4,8},{6,10},{8,4},{10,6},{12,16},{14,18},{16,12},... | collective-permute-start | bytes 786440 | tf_op jit(solution)/shard_map/ppermute | solution.py:39
  64.1 3.9 %shard_map.106 = (f32[2,256,256]{2,1,0:T(8,128)S(1)}, f32[2,256,256]{2,1,0:T(8,128)S(1)}, bf16[256,256]{1,0:T(8,128)(2,1)S(1)}, bf16[256,256]{1,0:T(8,128)(2,1)S(1)}) custom-call(s32[3]{0:T(128)S(1)} %copy-done.5, bf16[2,256,256]{2,1,0:T(8,128)(2,1)S(1)} %get-tuple-element.35.refs_0_.a_ref, bf16[2,256,256]{2,1,0:T(8,128)(2,1)S(1)} %get-tuple-element.36.refs_1_.b_ref, ...), custom_call_target="tpu_custom_call" | custom-call | flops 536870912 | bytes 4194304 | tf_op jit(solution)/shard_map/pallas_call | solution.py:405
  68.0 4.1 %collective-permute-start.7 = (bf16[256,256]{1,0:T(8,128)(2,1)S(1)}, bf16[256,256]{1,0:T(8,128)(2,1)S(1)}, u32[]{:S(2)}, u32[]{:S(2)}) collective-permute-start(bf16[256,256]{1,0:T(8,128)(2,1)S(1)} %get-tuple-element.45), channel_id=1, source_target_pairs={{0,2},{2,0},{4,6},{6,4},{8,10},{10,8},{12,14},{14,12},{16,18},{18,... | collective-permute-start | bytes 393224 | tf_op jit(solution)/shard_map/ppermute | solution.py:33
  72.1 1.0 collective-permute-done.7.got_ref
  73.1 1.0 shard_map.107
  74.2 0.7 shard_map.108
  74.9 2.6 %collective-permute-start.14 = (bf16[2,256,256]{2,1,0:T(8,128)(2,1)S(1)}, bf16[2,256,256]{2,1,0:T(8,128)(2,1)S(1)}, u32[]{:S(2)}, u32[]{:S(2)}) collective-permute-start(bf16[2,256,256]{2,1,0:T(8,128)(2,1)S(1)} %get-tuple-element.58), channel_id=1, source_target_pairs={{0,2},{2,0},{4,6},{6,4},{8,10},{10,8},{12,14},{14,12},{16,18},{18,... | collective-permute-start | bytes 786440 | tf_op jit(solution)/shard_map/ppermute | solution.py:33
  77.6 0.9 shard_map.110.base_ref
  78.4 0.3 collective-permute-done.14.gave_ref.grads_ref
  78.7 0.9 shard_map.111
  79.6 0.4 collective-permute-start.15
  80.0 1.0 shard_map.109.own_ref
  81.0 6.1 %collective-permute-done.15.got_ref = bf16[256,512]{1,0:T(8,128)(2,1)S(1)} collective-permute-done((bf16[256,512]{1,0:T(8,128)(2,1)S(1)}, bf16[256,512]{1,0:T(8,128)(2,1)S(1)}, u32[]{:S(2)}, u32[]{:S(2)}) %collective-permute-start.15) | collective-permute-done | bytes 262176 | tf_op jit(solution)/shard_map/ppermute | solution.py:433
  87.1 0.3 shard_map.112
  87.6 26.3 %all_to_all.11 = bf16[128,4,512]{2,1,0:T(4,128)(2,1)S(1)} all-to-all(bf16[128,4,512]{2,1,0:T(4,128)(2,1)S(1)} %all_to_all.7), channel_id=1, replica_groups={{208,210,212,214,224,226,228,230,56,58,60,62,8,10,12,14,24,26,28,30,232..., dimensions={0} | all-to-all | bytes 1048576 | tf_op jit(solution)/shard_map/all_to_all | solution.py:444
  114.0 0.8 shard_map.113
  (35 shorter events, 0.8 us)
Async XLA Ops:
  4.4 5.1 %copy-start.5 = (s32[3]{0:T(128)S(1)}, s32[3]{0:T(128)}, u32[]{:S(2)}) copy-start(s32[3]{0:T(128)} %pad_add_fusion.ids_ref) | copy-start | bytes 40
  4.4 5.1 %collective-permute-start = (bf16[272,1024]{1,0:T(8,128)(2,1)}, bf16[272,1024]{1,0:T(8,128)(2,1)S(1)}, u32[]{:S(2)}, u32[]{:S(2)}) collective-permute-start(bf16[272,1024]{1,0:T(8,128)(2,1)} %get-tuple-element.34), channel_id=1, source_target_pairs={{0,2},{2,0},{4,6},{6,4},{8,10},{10,8},{12,14},{14,12},{16,18},{18,... | collective-permute-start | bytes 1671176 | tf_op jit(solution)/shard_map/ppermute | solution.py:33
  9.5 1.1 copy-start.3
  10.5 17.6 %copy-start.4 = (s32[512,1]{1,0:T(8,128)S(1)}, s32[512,1]{1,0:T(8,128)}, u32[]{:S(2)}) copy-start(s32[512,1]{1,0:T(8,128)} %constant.38.clone.label_ref) | copy-start | bytes 6148
  11.2 16.8 %copy-start.6 = (s32[256,1]{0,1:T(1,128)S(1)}, s32[256,1]{0,1:T(1,128)}, u32[]{:S(2)}) copy-start(s32[256,1]{0,1:T(1,128)} %param.18) | copy-start | bytes 3076
  11.2 9.6 %collective-permute-start.3 = (bf16[2,256,256]{2,1,0:T(8,128)(2,1)S(1)}, bf16[2,256,256]{2,1,0:T(8,128)(2,1)S(1)}, u32[]{:S(2)}, u32[]{:S(2)}) collective-permute-start(bf16[2,256,256]{2,1,0:T(8,128)(2,1)S(1)} %get-tuple-element.35.refs_0_.a_ref), channel_id=1, source_target_pairs={{0,4},{2,6},{4,0},{6,2},{8,12},{10,14},{12,8},{14,10},{16,20},{18,... | collective-permute-start | bytes 786440 | tf_op jit(solution)/shard_map/ppermute | solution.py:39
  11.3 16.7 %collective-permute-start.1 = (bf16[2,256,256]{2,1,0:T(8,128)(2,1)S(1)}, bf16[2,256,256]{2,1,0:T(8,128)(2,1)S(1)}, u32[]{:S(2)}, u32[]{:S(2)}) collective-permute-start(bf16[2,256,256]{2,1,0:T(8,128)(2,1)S(1)} %get-tuple-element.36.refs_1_.b_ref), channel_id=1, source_target_pairs={{0,252},{2,254},{4,8},{6,10},{8,4},{10,6},{12,16},{14,18},{16,12},... | collective-permute-start | bytes 786440 | tf_op jit(solution)/shard_map/ppermute | solution.py:39
  20.8 12.6 %collective-permute-start.6 = (bf16[2,256,256]{2,1,0:T(8,128)(2,1)S(1)}, bf16[2,256,256]{2,1,0:T(8,128)(2,1)S(1)}, u32[]{:S(2)}, u32[]{:S(2)}) collective-permute-start(bf16[2,256,256]{2,1,0:T(8,128)(2,1)S(1)} %get-tuple-element.35.refs_0_.a_ref), channel_id=1, source_target_pairs={{0,252},{2,254},{4,8},{6,10},{8,4},{10,6},{12,16},{14,18},{16,12},... | collective-permute-start | bytes 786440 | tf_op jit(solution)/shard_map/ppermute | solution.py:39
  20.8 12.6 %collective-permute-start.5 = (bf16[2,256,256]{2,1,0:T(8,128)(2,1)S(1)}, bf16[2,256,256]{2,1,0:T(8,128)(2,1)S(1)}, u32[]{:S(2)}, u32[]{:S(2)}) collective-permute-start(bf16[2,256,256]{2,1,0:T(8,128)(2,1)S(1)} %get-tuple-element.36.refs_1_.b_ref), channel_id=1, source_target_pairs={{0,4},{2,6},{4,0},{6,2},{8,12},{10,14},{12,8},{14,10},{16,20},{18,... | collective-permute-start | bytes 786440 | tf_op jit(solution)/shard_map/ppermute | solution.py:39
  20.8 18.2 %collective-permute-start.4 = (bf16[2,256,256]{2,1,0:T(8,128)(2,1)S(1)}, bf16[2,256,256]{2,1,0:T(8,128)(2,1)S(1)}, u32[]{:S(2)}, u32[]{:S(2)}) collective-permute-start(bf16[2,256,256]{2,1,0:T(8,128)(2,1)S(1)} %collective-permute-done.3.refs_2_.ea_ref), channel_id=1, source_target_pairs={{0,252},{2,254},{4,8},{6,10},{8,4},{10,6},{12,16},{14,18},{16,12},... | collective-permute-start | bytes 786440 | tf_op jit(solution)/shard_map/ppermute | solution.py:39
  28.0 11.0 %collective-permute-start.2 = (bf16[2,256,256]{2,1,0:T(8,128)(2,1)S(1)}, bf16[2,256,256]{2,1,0:T(8,128)(2,1)S(1)}, u32[]{:S(2)}, u32[]{:S(2)}) collective-permute-start(bf16[2,256,256]{2,1,0:T(8,128)(2,1)S(1)} %collective-permute-done.1.refs_3_.oa_ref), channel_id=1, source_target_pairs={{0,4},{2,6},{4,0},{6,2},{8,12},{10,14},{12,8},{14,10},{16,20},{18,... | collective-permute-start | bytes 786440 | tf_op jit(solution)/shard_map/ppermute | solution.py:39
  42.6 15.2 %collective-permute-start.8 = (bf16[2,256,256]{2,1,0:T(8,128)(2,1)S(1)}, bf16[2,256,256]{2,1,0:T(8,128)(2,1)S(1)}, u32[]{:S(2)}, u32[]{:S(2)}) collective-permute-start(bf16[2,256,256]{2,1,0:T(8,128)(2,1)S(1)} %get-tuple-element.52), channel_id=1, source_target_pairs={{0,252},{2,254},{4,8},{6,10},{8,4},{10,6},{12,16},{14,18},{16,12},... | collective-permute-start | bytes 786440 | tf_op jit(solution)/shard_map/ppermute | solution.py:39
  48.6 9.4 %collective-permute-start.10 = (bf16[2,256,256]{2,1,0:T(8,128)(2,1)S(1)}, bf16[2,256,256]{2,1,0:T(8,128)(2,1)S(1)}, u32[]{:S(2)}, u32[]{:S(2)}) collective-permute-start(bf16[2,256,256]{2,1,0:T(8,128)(2,1)S(1)} %get-tuple-element.54), channel_id=1, source_target_pairs={{0,4},{2,6},{4,0},{6,2},{8,12},{10,14},{12,8},{14,10},{16,20},{18,... | collective-permute-start | bytes 786440 | tf_op jit(solution)/shard_map/ppermute | solution.py:39
  55.0 19.1 %collective-permute-start.12 = (bf16[2,256,256]{2,1,0:T(8,128)(2,1)S(1)}, bf16[2,256,256]{2,1,0:T(8,128)(2,1)S(1)}, u32[]{:S(2)}, u32[]{:S(2)}) collective-permute-start(bf16[2,256,256]{2,1,0:T(8,128)(2,1)S(1)} %get-tuple-element.55), channel_id=1, source_target_pairs={{0,4},{2,6},{4,0},{6,2},{8,12},{10,14},{12,8},{14,10},{16,20},{18,... | collective-permute-start | bytes 786440 | tf_op jit(solution)/shard_map/ppermute | solution.py:39
  56.5 17.6 %collective-permute-start.13 = (bf16[2,256,256]{2,1,0:T(8,128)(2,1)S(1)}, bf16[2,256,256]{2,1,0:T(8,128)(2,1)S(1)}, u32[]{:S(2)}, u32[]{:S(2)}) collective-permute-start(bf16[2,256,256]{2,1,0:T(8,128)(2,1)S(1)} %get-tuple-element.56), channel_id=1, source_target_pairs={{0,252},{2,254},{4,8},{6,10},{8,4},{10,6},{12,16},{14,18},{16,12},... | collective-permute-start | bytes 786440 | tf_op jit(solution)/shard_map/ppermute | solution.py:39
  57.9 16.3 %collective-permute-start.9 = (bf16[2,256,256]{2,1,0:T(8,128)(2,1)S(1)}, bf16[2,256,256]{2,1,0:T(8,128)(2,1)S(1)}, u32[]{:S(2)}, u32[]{:S(2)}) collective-permute-start(bf16[2,256,256]{2,1,0:T(8,128)(2,1)S(1)} %add_convert_fusion.1), channel_id=1, source_target_pairs={{0,4},{2,6},{4,0},{6,2},{8,12},{10,14},{12,8},{14,10},{16,20},{18,... | collective-permute-start | bytes 786440 | tf_op jit(solution)/shard_map/ppermute | solution.py:39
  58.1 15.1 %copy-start.2 = (bf16[1024,512]{1,0:T(8,128)(2,1)S(1)}, bf16[1024,512]{1,0:T(8,128)(2,1)}, u32[]{:S(2)}) copy-start(bf16[1024,512]{1,0:T(8,128)(2,1)} %weight_ref.1) | copy-start | bytes 3145732
  58.1 16.1 %collective-permute-start.11 = (bf16[2,256,256]{2,1,0:T(8,128)(2,1)S(1)}, bf16[2,256,256]{2,1,0:T(8,128)(2,1)S(1)}, u32[]{:S(2)}, u32[]{:S(2)}) collective-permute-start(bf16[2,256,256]{2,1,0:T(8,128)(2,1)S(1)} %add_convert_fusion), channel_id=1, source_target_pairs={{0,252},{2,254},{4,8},{6,10},{8,4},{10,6},{12,16},{14,18},{16,12},... | collective-permute-start | bytes 786440 | tf_op jit(solution)/shard_map/ppermute | solution.py:39
  68.0 5.1 %collective-permute-start.7 = (bf16[256,256]{1,0:T(8,128)(2,1)S(1)}, bf16[256,256]{1,0:T(8,128)(2,1)S(1)}, u32[]{:S(2)}, u32[]{:S(2)}) collective-permute-start(bf16[256,256]{1,0:T(8,128)(2,1)S(1)} %get-tuple-element.45), channel_id=1, source_target_pairs={{0,2},{2,0},{4,6},{6,4},{8,10},{10,8},{12,14},{14,12},{16,18},{18,... | collective-permute-start | bytes 393224 | tf_op jit(solution)/shard_map/ppermute | solution.py:33
  74.2 3.4 %copy-start = (bf16[1024,512]{1,0:T(8,128)(2,1)S(1)}, bf16[1024,512]{1,0:T(8,128)(2,1)}, u32[]{:S(2)}) copy-start(bf16[1024,512]{1,0:T(8,128)(2,1)} %wk_ref.5) | copy-start | bytes 3145732
  74.2 3.4 %copy-start.1 = (bf16[1024,512]{1,0:T(8,128)(2,1)S(1)}, bf16[1024,512]{1,0:T(8,128)(2,1)}, u32[]{:S(2)}) copy-start(bf16[1024,512]{1,0:T(8,128)(2,1)} %wv_ref.5) | copy-start | bytes 3145732
  74.9 3.8 %collective-permute-start.14 = (bf16[2,256,256]{2,1,0:T(8,128)(2,1)S(1)}, bf16[2,256,256]{2,1,0:T(8,128)(2,1)S(1)}, u32[]{:S(2)}, u32[]{:S(2)}) collective-permute-start(bf16[2,256,256]{2,1,0:T(8,128)(2,1)S(1)} %get-tuple-element.58), channel_id=1, source_target_pairs={{0,2},{2,0},{4,6},{6,4},{8,10},{10,8},{12,14},{14,12},{16,18},{18,... | collective-permute-start | bytes 786440 | tf_op jit(solution)/shard_map/ppermute | solution.py:33
  79.6 7.5 %collective-permute-start.15 = (bf16[256,512]{1,0:T(8,128)(2,1)S(1)}, bf16[256,512]{1,0:T(8,128)(2,1)S(1)}, u32[]{:S(2)}, u32[]{:S(2)}) collective-permute-start(bf16[256,512]{1,0:T(8,128)(2,1)S(1)} %shard_map.111), channel_id=1, source_target_pairs={{0,1},{1,0},{2,3},{3,2},{4,5},{5,4},{6,7},{7,6},{8,9},{9,8},{10,11... | collective-permute-start | bytes 786440 | tf_op jit(solution)/shard_map/ppermute | solution.py:433

commit v3 on v2

--- a/solution.py
+++ b/solution.py
@@ -51,11 +51,15 @@
     return jnp.where(allowed, 0.0, MASKED)
 
 
-def pack_kernel(ids_ref, adj_ref, k_ref, v_ref, q_ref, g_ref, send_ref, own_ref, sems):
+def with_place(kernel, core_ref, chip_ref, head_ref, *refs):
+    kernel((core_ref[0], chip_ref[0], head_ref[0]), *refs)
+
+
+def pack_kernel(ids, adj_in_ref, k_ref, v_ref, q_ref, g_ref, send_ref, own_ref, adj_ref, sems):
     rows, cols = k_ref.shape
     half = cols // 2
-    copies = []
-    for to_ref, which in ((send_ref, 1 - ids_ref[0]), (own_ref, ids_ref[0])):
+    copies = [pltpu.make_async_copy(adj_in_ref, adj_ref, sems.at[0])]
+    for to_ref, which in ((send_ref, 1 - ids[0]), (own_ref, ids[0])):
         at = pl.ds(pl.multiple_of(which * half, half), half)
         for n, from_ref in enumerate((k_ref, v_ref, q_ref, g_ref)):
             copies.append(
@@ -65,24 +69,25 @@
             )
     for copy in copies:
         copy.start()
+    copies[0].wait()
     bias = bias_rows(adj_ref).astype(BF)
     for to_ref in (send_ref, own_ref):
         to_ref[rows : rows + 16, 0:half] = bias
         to_ref[rows : rows + 16, half:] = jnp.zeros((16, 3 * half), BF)
-    for copy in copies:
+    for copy in copies[1:]:
         copy.wait()
 
 
-def order_kernel(ids_ref, own_ref, got_ref, a_ref, b_ref, qg_ref, bias_ref):
+def order_kernel(ids, own_ref, got_ref, a_ref, b_ref, qg_ref, bias_ref):
     rows = a_ref.shape[1]
     cols = a_ref.shape[2]
-    par = ids_ref[0]
+    par = ids[0]
     scale = 1.0 / math.sqrt(HD)
     for sector, from_ref in ((par, own_ref), (1 - par, got_ref)):
         qg_ref[0, sector] = from_ref[0:rows, 2 * cols : 3 * cols] * scale
         qg_ref[1, sector] = from_ref[0:rows, 3 * cols : 4 * cols]
         bias_ref[sector] = from_ref[rows : rows + 16, 0:cols].astype(F32)
-    b_own = par == ids_ref[1]
+    b_own = par == ids[1]
     for which in range(2):
         own = own_ref[0:rows, which * cols : (which + 1) * cols]
         got = got_ref[0:rows, which * cols : (which + 1) * cols]
@@ -115,24 +120,35 @@
     return (top, total, delta), scores, grads
 
 
-def near_stats_kernel(ids_ref, *refs):
-    windows = refs[0:6]
-    qg_ref, bias_ref, stats_ref = refs[6:9]
-    odd = ids_ref[1]
-    names = (4 - odd, 3 + odd, 5 - 3 * odd, 2 + 3 * odd, 6 - 5 * odd, 1 + 5 * odd)
+def fold_windows(names, windows, qg_ref, bias_ref, before_ref, stats_ref):
     rows = qg_ref.shape[2]
     for t in range(2):
         for h in range(2):
             qh = one_head(qg_ref.at[0, t], h)
             gh = one_head(qg_ref.at[1, t], h)
-            zero = jnp.zeros((1, rows), F32)
-            stats = (zero + FLOOR, zero, zero)
+            if before_ref is None:
+                zero = jnp.zeros((1, rows), F32)
+                stats = (zero + FLOOR, zero, zero)
+            else:
+                stats = tuple(before_ref[t, h, row : row + 1, :] for row in range(3))
             for w, window in zip(names, windows):
                 stats, _, _ = fold_stats(stats, window, qh, gh, bias_pair_of(bias_ref, t, w - t))
             for row in range(3):
                 stats_ref[t, h, row : row + 1, :] = stats[row]
 
 
+def first_stats_kernel(ids, a_ref, b_ref, ea_ref, eb_ref, qg_ref, bias_ref, stats_ref):
+    odd = ids[1]
+    names = (4 - odd, 3 + odd, 5 - 3 * odd, 6 - 5 * odd)
+    fold_windows(names, (a_ref, b_ref, ea_ref, eb_ref), qg_ref, bias_ref, None, stats_ref)
+
+
+def second_stats_kernel(ids, oa_ref, ob_ref, qg_ref, bias_ref, before_ref, stats_ref):
+    odd = ids[1]
+    names = (2 + 3 * odd, 1 + 5 * odd)
+    fold_windows(names, (oa_ref, ob_ref), qg_ref, bias_ref, before_ref, stats_ref)
+
+
 def head_rows_of(first, second):
     row_head = lax.broadcasted_iota(jnp.int32, first.shape, 0) // HD
     return jnp.where(row_head == 0, first, second)
@@ -148,11 +164,11 @@
 
 
 def far_kernel(
-    ids_ref, e_ref, o_ref, qg_ref, bias_ref, stats_ref, final_ref, de_ref, do_ref, dq_ref,
+    ids, e_ref, o_ref, qg_ref, bias_ref, stats_ref, final_ref, de_ref, do_ref, dq_ref,
     ps_ref, ds_ref, qs_ref, gs_ref,
 ):
     rows = qg_ref.shape[2]
-    odd = ids_ref[1]
+    odd = ids[1]
     for n, (t, window, out_ref) in enumerate(((1 - odd, e_ref, de_ref), (odd, o_ref, do_ref))):
         for h in range(2):
             cols = slice(h * rows, (h + 1) * rows)
@@ -211,21 +227,21 @@
     ]
 
 
-def near_kernel(ids_ref, ea_ref, oa_ref, eb_ref, ob_ref, qg_ref, bias_ref, final_ref, part_ref, *refs):
+def near_kernel(ids, ea_ref, oa_ref, eb_ref, ob_ref, qg_ref, bias_ref, final_ref, part_ref, *refs):
     outs, dq_ref, scratch = refs[0:4], refs[4], refs[5:]
-    odd = ids_ref[1]
+    odd = ids[1]
     names = (5 - 3 * odd, 2 + 3 * odd, 6 - 5 * odd, 1 + 5 * odd)
     grads = shared_kernel(names, qg_ref, bias_ref, final_ref, (ea_ref, oa_ref, eb_ref, ob_ref), outs, *scratch)
     for t in range(2):
         dq_ref[0, t] = part_ref[0, t] + grads[t]
 
 
-def local_kernel(ids_ref, a_ref, b_ref, qg_ref, bias_ref, final_ref, part_ref, *refs):
+def local_kernel(ids, a_ref, b_ref, qg_ref, bias_ref, final_ref, part_ref, *refs):
     outs, (dq_own_ref, dq_send_ref), scratch = refs[0:2], refs[2:4], refs[4:]
-    odd = ids_ref[1]
+    odd = ids[1]
     grads = shared_kernel((4 - odd, 3 + odd), qg_ref, bias_ref, final_ref, (a_ref, b_ref), outs, *scratch)
     total = [part_ref[0, t] + grads[t] for t in range(2)]
-    first = ids_ref[0] == 0
+    first = ids[0] == 0
     scale = 1.0 / math.sqrt(HD)
     dq_own_ref[...] = jnp.transpose(jnp.where(first, total[0], total[1]) * scale).astype(BF)
     dq_send_ref[...] = jnp.transpose(jnp.where(first, total[1], total[0]) * scale).astype(BF)
@@ -235,8 +251,8 @@
     return (first.astype(F32) + second.astype(F32)).astype(BF)
 
 
-def total_kernel(ids_ref, a_ref, b_ref, ea_ref, oa_ref, eb_ref, ob_ref, keep_ref, send_ref):
-    b_own = ids_ref[0] == ids_ref[1]
+def total_kernel(ids, a_ref, b_ref, ea_ref, oa_ref, eb_ref, ob_ref, keep_ref, send_ref):
+    b_own = ids[0] == ids[1]
     for which in range(2):
         value_a = a_ref[which] + ob_ref[which].astype(F32) + ea_ref[which].astype(F32)
         value_b = b_ref[which] + eb_ref[which].astype(F32) + oa_ref[which].astype(F32)
@@ -244,25 +260,25 @@
         send_ref[which] = jnp.where(b_own, value_a, value_b).astype(BF)
 
 
-def query_kernel(ids_ref, own_ref, got_ref, weight_ref, other_out_ref, own_out_ref):
-    first = ids_ref[0] == 0
+def query_kernel(ids, own_ref, got_ref, weight_ref, other_out_ref, own_out_ref):
+    first = ids[0] == 0
     half = own_ref.shape[1]
     low = jnp.where(first, own_ref[...], got_ref[...])
     high = jnp.where(first, got_ref[...], own_ref[...])
     cols = own_out_ref.shape[1]
-    here = ids_ref[2]
+    here = ids[2]
     for out_ref, which in ((other_out_ref, 1 - here), (own_out_ref, here)):
         at = pl.ds(pl.multiple_of(which * cols, cols), cols)
         out_ref[...] = dot(low, weight_ref[at, 0:half], NT) + dot(high, weight_ref[at, half:], NT)
 
 
-def add_kernel(ids_ref, base_ref, grads_ref, wk_ref, wv_ref, out_ref):
+def add_kernel(ids, base_ref, grads_ref, wk_ref, wv_ref, out_ref):
     value = base_ref[...] + dot(grads_ref[0], wk_ref[...], NT) + dot(grads_ref[1], wv_ref[...], NT)
     out_ref[...] = value.astype(out_ref.dtype)
 
 
-def both_kernel(ids_ref, base_ref, keep_ref, gave_ref, wk_ref, wv_ref, out_ref):
-    first = ids_ref[0] == 0
+def both_kernel(ids, base_ref, keep_ref, gave_ref, wk_ref, wv_ref, out_ref):
+    first = ids[0] == 0
     half = keep_ref.shape[2]
     value = base_ref[...]
     for which, weight in ((0, wk_ref), (1, wv_ref)):
@@ -308,16 +324,19 @@
     pair = 2 * HD
     sds = jax.ShapeDtypeStruct
     block = lax.axis_index("blk")
-    ids = jnp.stack([block % 2, (block // 2) % 2, lax.axis_index("head")]).astype(jnp.int32)
+    ids = tuple(
+        jnp.reshape(value, (1,)).astype(jnp.int32)
+        for value in (block & 1, (block >> 1) & 1, lax.axis_index("head"))
+    )
     smem = pl.BlockSpec(memory_space=pltpu.SMEM)
     hbm = pl.BlockSpec(memory_space=pltpu.HBM)
 
-    def call(kernel, outs, grid, in_specs, out_specs, scratch=(), scalars=1, estimate=None, limit=16):
+    def call(kernel, outs, grid, in_specs, out_specs, scratch=(), placed=True, estimate=None, limit=16):
         return pl.pallas_call(
-            kernel,
+            functools.partial(with_place, kernel) if placed else kernel,
             out_shape=outs,
             grid_spec=pltpu.PrefetchScalarGridSpec(
-                num_scalar_prefetch=scalars, grid=grid, in_specs=in_specs, out_specs=out_specs,
+                num_scalar_prefetch=3 if placed else 0, grid=grid, in_specs=in_specs, out_specs=out_specs,
                 scratch_shapes=list(scratch),
             ),
             compiler_params=pltpu.CompilerParams(vmem_limit_bytes=limit << 20),
@@ -329,9 +348,9 @@
 
     packed = sds((rows + 16, 4 * half), BF)
     send, own = call(
-        pack_kernel, (packed, packed), (1,), [smem] + [hbm] * 4, (whole(rows + 16, 4 * half),) * 2,
-        scratch=(pltpu.SemaphoreType.DMA((8,)),), limit=60,
-    )(ids, adjacency, key, value, query, out_grad)
+        pack_kernel, (packed, packed), (1,), [hbm] * 5, (whole(rows + 16, 4 * half),) * 2,
+        scratch=(pltpu.SMEM(adjacency.shape, jnp.int32), pltpu.SemaphoreType.DMA((9,))),
+    )(*ids, *[pltpu.with_memory_space_constraint(x, pltpu.HBM) for x in (adjacency, key, value, query, out_grad)])
     got = core_swapped(send)
     kv_shape = sds((2, rows, half), BF)
     kv_whole = whole(2, rows, half)
@@ -341,7 +360,7 @@
         (1,),
         [whole(rows + 16, 4 * half)] * 2,
         (kv_whole, kv_whole, whole(2, 2, rows, half), whole(2, 16, rows)),
-    )(ids, own, got)
+    )(*ids, own, got)
     ea = chip_swapped(a, 0)
     oa = chip_swapped(b, 1)
     eb = chip_swapped(b, 0)
@@ -355,20 +374,20 @@
     labels = jnp.asarray(np.array([[CAP * s + r] for s in order for r in range(CAP)], np.int32))
     place = call(
         route_kernel, sds((slots, rows), BF), (1,),
-        [whole(rows, 1), whole(1, rows), whole(slots, 1)], whole(slots, rows), scalars=0,
+        [whole(rows, 1), whole(1, rows), whole(slots, 1)], whole(slots, rows), placed=False,
         estimate=cost(rows * rows * 8, 1 << 20),
     )(owner, owner.reshape(1, rows), labels)
 
     pairs = half // pair
-    win = pl.BlockSpec((2, rows, pair), lambda i, p: (0, 0, i))
-    near = pl.BlockSpec((2, 2, rows, pair), lambda i, p: (0, 0, 0, i))
-    dq_spec = pl.BlockSpec((rows, pair), lambda i, p: (0, i))
-    stat_spec = pl.BlockSpec((2, 2, 8, rows), lambda i, p: (0, i, 0, 0))
+    win = pl.BlockSpec((2, rows, pair), lambda i, *p: (0, 0, i))
+    near = pl.BlockSpec((2, 2, rows, pair), lambda i, *p: (0, 0, 0, i))
+    dq_spec = pl.BlockSpec((rows, pair), lambda i, *p: (0, i))
+    stat_spec = pl.BlockSpec((2, 2, 8, rows), lambda i, *p: (0, i, 0, 0))
     bias_spec = whole(2, 16, rows)
     stat_shape = sds((2, 2 * pairs, 8, rows), F32)
     step = 2 * rows * rows * HD * 4
     part_shape = sds((pairs, 2, pair, rows), F32)
-    part_spec = pl.BlockSpec((1, 2, pair, rows), lambda i, p: (i, 0, 0, 0))
+    part_spec = pl.BlockSpec((1, 2, pair, rows), lambda i, *p: (i, 0, 0, 0))
 
     def scratch(blocks):
         return (
@@ -380,9 +399,13 @@
         )
 
     stats = call(
-        near_stats_kernel, stat_shape, (pairs,), [win] * 6 + [near, bias_spec], stat_spec,
-        estimate=cost(24 * step, 6 << 20),
-    )(ids, a, b, ea, oa, eb, ob, qg, bias)
+        first_stats_kernel, stat_shape, (pairs,), [win] * 4 + [near, bias_spec], stat_spec,
+        estimate=cost(16 * step, 4 << 20),
+    )(*ids, a, b, ea, eb, qg, bias)
+    stats = call(
+        second_stats_kernel, stat_shape, (pairs,), [win] * 2 + [near, bias_spec, stat_spec], stat_spec,
+        estimate=cost(8 * step, 2 << 20),
+    )(*ids, oa, ob, qg, bias, stats)
     stats, place = lax.optimization_barrier((stats, place))
     far_probs = pltpu.VMEM((2, rows, 2 * rows), BF)
     far_rows = pltpu.VMEM((2, 2 * rows, pair), BF)
@@ -390,13 +413,13 @@
         far_kernel, (stat_shape, kv_shape, kv_shape, part_shape), (pairs,),
         [win] * 2 + [near, bias_spec, stat_spec], (stat_spec, win, win, part_spec),
         scratch=(far_probs, far_probs, far_rows, far_rows), estimate=cost(8 * step, 2 << 20),
-    )(ids, ef, of, qg, bias, stats)
+    )(*ids, ef, of, qg, bias, stats)
     back_ef = chip_swapped(d_ef, 0)
     back_of = chip_swapped(d_of, 1)
     d_ea, d_oa, d_eb, d_ob, dq_near = call(
         near_kernel, (kv_shape,) * 4 + (part_shape,), (pairs,), [win] * 4 + [near, bias_spec, stat_spec, part_spec],
         (win,) * 4 + (part_spec,), scratch=scratch(4), estimate=cost(32 * step, 4 << 20),
-    )(ids, ea, oa, eb, ob, qg, bias, final, dq_far)
+    )(*ids, ea, oa, eb, ob, qg, bias, final, dq_far)
     back_eb = chip_swapped(d_eb, 0)
     back_ob = chip_swapped(d_ob, 1)
     back_ea = chip_swapped(joined(d_ea, back_of), 0)
@@ -406,39 +429,39 @@
         local_kernel, (own_shape, own_shape, sds((rows, half), BF), sds((rows, half), BF)), (pairs,),
         [win] * 2 + [near, bias_spec, stat_spec, part_spec], (win, win, dq_spec, dq_spec),
         scratch=scratch(2), estimate=cost(16 * step, 4 << 20),
-    )(ids, a, b, qg, bias, final, dq_near)
+    )(*ids, a, b, qg, bias, final, dq_near)
     dq_got = core_swapped(dq_send)
     q_other, q_own = call(
         query_kernel, (sds((rows, cols), F32), sds((rows, cols), F32)), (1,),
         [whole(rows, half)] * 2 + [whole(2 * cols, cols)], (whole(rows, cols), whole(rows, cols)),
         estimate=cost(2 * rows * cols * 2 * cols, 3 << 20),
-    )(ids, dq_own, dq_got, q_weight)
+    )(*ids, dq_own, dq_got, q_weight)
     d_a, q_other, q_own = lax.optimization_barrier((d_a, q_other, q_own))
     keep, give = call(
         total_kernel, (kv_shape, kv_shape), (1,), [kv_whole] * 6, (kv_whole, kv_whole),
-    )(ids, d_a, d_b, back_ea, back_oa, back_eb, back_ob)
+    )(*ids, d_a, d_b, back_ea, back_oa, back_eb, back_ob)
     gave = core_swapped(give)
-    weight_keep = pl.BlockSpec((cols, half), lambda i, p: (1 - p[2], p[0]))
-    weight_gave = pl.BlockSpec((cols, half), lambda i, p: (1 - p[2], 1 - p[0]))
-    weight_own = pl.BlockSpec((cols, cols), lambda i, p: (p[2], 0))
+    weight_keep = pl.BlockSpec((cols, half), lambda i, *p: (1 - p[2][0], p[0][0]))
+    weight_gave = pl.BlockSpec((cols, half), lambda i, *p: (1 - p[2][0], 1 - p[0][0]))
+    weight_own = pl.BlockSpec((cols, cols), lambda i, *p: (p[2][0], 0))
     add_cost = cost(2 * rows * cols * 2 * half, 2 << 20)
     partial_keep = call(
         add_kernel, sds((rows, cols), F32), (1,), [whole(rows, cols), kv_whole] + [weight_keep] * 2,
         whole(rows, cols), estimate=add_cost,
-    )(ids, q_other, keep, k_weight, v_weight)
+    )(*ids, q_other, keep, k_weight, v_weight)
     partial_other = call(
         add_kernel, sds((rows, cols), BF), (1,), [whole(rows, cols), kv_whole] + [weight_gave] * 2,
         whole(rows, cols), estimate=add_cost,
-    )(ids, partial_keep, gave, k_weight, v_weight)
+    )(*ids, partial_keep, gave, k_weight, v_weight)
     partial_got = lax.ppermute(partial_other, "head", [(0, 1), (1, 0)])
     partial_own = call(
         both_kernel, sds((rows, cols), F32), (1,),
         [whole(rows, cols)] + [kv_whole] * 2 + [weight_own] * 2, whole(rows, cols),
         estimate=cost(2 * rows * cols * 2 * cols, 2 << 20),
-    )(ids, q_own, keep, gave, k_weight, v_weight)
+    )(*ids, q_own, keep, gave, k_weight, v_weight)
     outgoing = call(
         scatter_kernel, sds((slots, cols), BF), (1,),
-        [whole(rows, cols), whole(rows, cols), whole(slots, rows)], whole(slots, cols), scalars=0,
+        [whole(rows, cols), whole(rows, cols), whole(slots, rows)], whole(slots, cols), placed=False,
         estimate=cost(2 * slots * rows * cols, 2 << 20),
     )(partial_own, partial_got, place)
     arrived = lax.all_to_all(
@@ -447,7 +470,7 @@
     home = [int(g) for g in np.argsort(np.array(order[::4]) // 4)]
     return call(
         functools.partial(restore_kernel, home=home), sds((slots, cols), BF), (1,), [whole(slots, cols)],
-        whole(slots, cols), scalars=0,
+        whole(slots, cols), placed=False,
     )(arrived)
 
 

time: 115 us -> 108 us (0.939)
  Pallas kernels: 29.6 us -> 22.4 us
  waiting for transfers between devices: 14.3 us -> 16.5 us
    pallas_call x2 -> x3, Pallas kernels: 9.32 us -> 6.99 us  [the longest x1 3.56 us: on_device(): call(first_stats_kernel, stat_shape, (pairs,), [win] * 4 + [near, bias_sp...]
    ppermute x12, waiting for transfers between devices: 5.12 us -> 6.43 us  [chip_swapped(): lax.ppermute(value, 'blk', [(s, (s + ahead[s]) % count) for s in range(co...]
  transfers between devices with their start and end apart: 16 -> 16, of which waited for: 5 -> 7; matrix products, arithmetic and copies ran while one was open for 0% -> 0% of each run, Pallas kernels for 16% -> 15%
where the time goes in v3:
time: 108 us
  starting transfers between devices  41.9 us (39%)
  blocking collectives  26.3 us (24%)
  Pallas kernels  22.4 us (21%)
  waiting for transfers between devices  16.5 us (15%)
    ppermute x12, starting transfers between devices, chip_swapped(): lax.ppermute(value, 'blk', [(s, (s + ahead[s]) % count) for s in range(co...  31.7 us
    all_to_all x1, blocking collectives, on_device(): lax.all_to_all(outgoing, 'blk', split_axis=0, concat_axis=0, tiled=True,...  26.3 us
    ppermute x3, starting transfers between devices, core_swapped(): return lax.ppermute(value, 'blk', [(s, s ^ 1) for s in range(count)])  9.82 us
    ppermute x1, waiting for transfers between devices, on_device(): partial_got = lax.ppermute(partial_other, 'head', [(0, 1), (1, 0)])  6.65 us
    ppermute x12, waiting for transfers between devices, chip_swapped(): lax.ppermute(value, 'blk', [(s, (s + ahead[s]) % count) for s in range(co...  6.43 us
    pallas_call x1, Pallas kernels, on_device(): call(near_kernel, (kv_shape,) * 4 + (part_shape,), (pairs,), [win] * 4 +...  5.83 us
    pallas_call x1, Pallas kernels, on_device(): call(first_stats_kernel, stat_shape, (pairs,), [win] * 4 + [near, bias_sp...  3.56 us
    ppermute x3, waiting for transfers between devices, core_swapped(): return lax.ppermute(value, 'blk', [(s, s ^ 1) for s in range(count)])  3.39 us
  transfers between devices with their start and end apart: 16, of which 7 were waited for; matrix products, arithmetic and copies ran while one was open for 0% of the time, Pallas kernels for 15%

profile of v3, /device:TPU:1, one launch (start us, length us, event | category | flops | bytes accessed | tf_op | source)
XLA Modules:
  0.0 107.8 jit_solution(5555567240167439625)
XLA Ops:
  0.0 1.4 %shard_map.100 = (bf16[272,1024]{1,0:T(8,128)(2,1)S(1)}, bf16[272,1024]{1,0:T(8,128)(2,1)S(1)}) custom-call(s32[1]{0:T(128)} %bitcast.core_ref, s32[1]{0:T(128)} %bitcast.1.chip_ref, s32[1]{0:T(128)} %bitcast.2.head_ref, s32[2,14]{1,0:T(2,128)} %refs_0_.1, bf16[256,512]{1,0:T(8,128)(2,1)} %refs_1_.1, bf16[256,512]{1,0:T(8,128)(2,1)} %refs_2_.4, ...), custom_call_target="tpu_custom_call" | custom-call | tf_op jit(solution)/shard_map/pallas_call | solution.py:350
  1.4 3.3 %collective-permute-start = (bf16[272,1024]{1,0:T(8,128)(2,1)S(1)}, bf16[272,1024]{1,0:T(8,128)(2,1)S(1)}, u32[]{:S(2)}, u32[]{:S(2)}) collective-permute-start(bf16[272,1024]{1,0:T(8,128)(2,1)S(1)} %get-tuple-element.34), channel_id=1, source_target_pairs={{0,2},{2,0},{4,6},{6,4},{8,10},{10,8},{12,14},{14,12},{16,18},{18,... | collective-permute-start | bytes 1671176 | tf_op jit(solution)/shard_map/ppermute | solution.py:33
  4.7 1.6 %collective-permute-done.refs_1_ = bf16[272,1024]{1,0:T(8,128)(2,1)S(1)} collective-permute-done((bf16[272,1024]{1,0:T(8,128)(2,1)S(1)}, bf16[272,1024]{1,0:T(8,128)(2,1)S(1)}, u32[]{:S(2)}, u32[]{:S(2)}) %collective-permute-start) | collective-permute-done | bytes 557088 | tf_op jit(solution)/shard_map/ppermute | solution.py:33
  6.5 9.5 %collective-permute-start.1 = (bf16[2,256,256]{2,1,0:T(8,128)(2,1)S(1)}, bf16[2,256,256]{2,1,0:T(8,128)(2,1)S(1)}, u32[]{:S(2)}, u32[]{:S(2)}) collective-permute-start(bf16[2,256,256]{2,1,0:T(8,128)(2,1)S(1)} %get-tuple-element.36.refs_1_), channel_id=1, source_target_pairs={{0,252},{2,254},{4,8},{6,10},{8,4},{10,6},{12,16},{14,18},{16,12},... | collective-permute-start | bytes 786440 | tf_op jit(solution)/shard_map/ppermute | solution.py:39
  16.0 1.5 %collective-permute-start.5 = (bf16[2,256,256]{2,1,0:T(8,128)(2,1)S(1)}, bf16[2,256,256]{2,1,0:T(8,128)(2,1)S(1)}, u32[]{:S(2)}, u32[]{:S(2)}) collective-permute-start(bf16[2,256,256]{2,1,0:T(8,128)(2,1)S(1)} %get-tuple-element.35.refs_0_), channel_id=1, source_target_pairs={{0,252},{2,254},{4,8},{6,10},{8,4},{10,6},{12,16},{14,18},{16,12},... | collective-permute-start | bytes 786440 | tf_op jit(solution)/shard_map/ppermute | solution.py:39
  17.4 5.7 %collective-permute-start.4 = (bf16[2,256,256]{2,1,0:T(8,128)(2,1)S(1)}, bf16[2,256,256]{2,1,0:T(8,128)(2,1)S(1)}, u32[]{:S(2)}, u32[]{:S(2)}) collective-permute-start(bf16[2,256,256]{2,1,0:T(8,128)(2,1)S(1)} %collective-permute-done.3.refs_2_.refs_0_), channel_id=1, source_target_pairs={{0,252},{2,254},{4,8},{6,10},{8,4},{10,6},{12,16},{14,18},{16,12},... | collective-permute-start | bytes 786440 | tf_op jit(solution)/shard_map/ppermute | solution.py:39
  23.5 3.6 %shard_map.102.refs_4_ = f32[2,4,8,256]{3,2,1,0:T(8,128)S(1)} custom-call(s32[1]{0:T(128)} %bitcast.core_ref, s32[1]{0:T(128)} %bitcast.1.chip_ref, s32[1]{0:T(128)} %bitcast.2.head_ref, bf16[2,256,256]{2,1,0:T(8,128)(2,1)S(1)} %get-tuple-element.35.refs_0_, bf16[2,256,256]{2,1,0:T(8,128)(2,1)S(1)} %get-tuple-element.36.refs_1_, ...), custom_call_target="tpu_custom_call" | custom-call | flops 536870912 | bytes 4194304 | tf_op jit(solution)/shard_map/pallas_call | solution.py:401
  27.1 1.5 %collective-permute-done.5.refs_1_.refs_3_ = bf16[2,256,256]{2,1,0:T(8,128)(2,1)S(1)} collective-permute-done((bf16[2,256,256]{2,1,0:T(8,128)(2,1)S(1)}, bf16[2,256,256]{2,1,0:T(8,128)(2,1)S(1)}, u32[]{:S(2)}, u32[]{:S(2)}) %collective-permute-start.5) | collective-permute-done | bytes 262176 | tf_op jit(solution)/shard_map/ppermute | solution.py:39
  28.6 2.1 %shard_map.103.refs_4_ = f32[2,4,8,256]{3,2,1,0:T(8,128)S(1)} custom-call(s32[1]{0:T(128)} %bitcast.core_ref, s32[1]{0:T(128)} %bitcast.1.chip_ref, s32[1]{0:T(128)} %bitcast.2.head_ref, bf16[2,256,256]{2,1,0:T(8,128)(2,1)S(1)} %collective-permute-done.1.refs_0_.refs_1_, bf16[2,256,256]{2,1,0:T(8,128)(2,1)S(1)} %collective-permute-done.5.refs_1_.refs_3_, ...), custom_call_target="tpu_custom_call" | custom-call | flops 268435456 | bytes 2097152 | tf_op jit(solution)/shard_map/pallas_call | solution.py:405
  30.6 3.5 %collective-permute-done.4.refs_1_ = bf16[2,256,256]{2,1,0:T(8,128)(2,1)S(1)} collective-permute-done((bf16[2,256,256]{2,1,0:T(8,128)(2,1)S(1)}, bf16[2,256,256]{2,1,0:T(8,128)(2,1)S(1)}, u32[]{:S(2)}, u32[]{:S(2)}) %collective-permute-start.4) | collective-permute-done | bytes 262176 | tf_op jit(solution)/shard_map/ppermute | solution.py:39
  34.2 3.0 %shard_map.105 = (f32[2,4,8,256]{3,2,1,0:T(8,128)S(1)}, bf16[2,256,256]{2,1,0:T(8,128)(2,1)S(1)}, bf16[2,256,256]{2,1,0:T(8,128)(2,1)S(1)}, f32[2,2,128,256]{3,2,1,0:T(8,128)S(1)}) custom-call(s32[1]{0:T(128)} %bitcast.core_ref, s32[1]{0:T(128)} %bitcast.1.chip_ref, s32[1]{0:T(128)} %bitcast.2.head_ref, ...), custom_call_target="tpu_custom_call" | custom-call | flops 268435456 | bytes 2097152 | tf_op jit(solution)/shard_map/pallas_call | solution.py:412
  37.2 6.0 %collective-permute-start.8 = (bf16[2,256,256]{2,1,0:T(8,128)(2,1)S(1)}, bf16[2,256,256]{2,1,0:T(8,128)(2,1)S(1)}, u32[]{:S(2)}, u32[]{:S(2)}) collective-permute-start(bf16[2,256,256]{2,1,0:T(8,128)(2,1)S(1)} %get-tuple-element.52), channel_id=1, source_target_pairs={{0,252},{2,254},{4,8},{6,10},{8,4},{10,6},{12,16},{14,18},{16,12},... | collective-permute-start | bytes 786440 | tf_op jit(solution)/shard_map/ppermute | solution.py:39
  43.2 5.8 %shard_map.106 = (bf16[2,256,256]{2,1,0:T(8,128)(2,1)S(1)}, bf16[2,256,256]{2,1,0:T(8,128)(2,1)S(1)}, bf16[2,256,256]{2,1,0:T(8,128)(2,1)S(1)}, bf16[2,256,256]{2,1,0:T(8,128)(2,1)S(1)}, f32[2,2,128,256]{3,2,1,0:T(8,128)S(1)}) custom-call(s32[1]{0:T(128)} %bitcast.core_ref, s32[1]{0:T(128)} %bitcast.1.chip_ref, s32[1]{0:T(128)} %bitcast.2.head_ref, ...), custom_call_target="tpu_custom_call" | custom-call | flops 1073741824 | bytes 4194304 | tf_op jit(solution)/shard_map/pallas_call | solution.py:419
  49.1 1.5 %collective-permute-start.12 = (bf16[2,256,256]{2,1,0:T(8,128)(2,1)S(1)}, bf16[2,256,256]{2,1,0:T(8,128)(2,1)S(1)}, u32[]{:S(2)}, u32[]{:S(2)}) collective-permute-start(bf16[2,256,256]{2,1,0:T(8,128)(2,1)S(1)} %get-tuple-element.55), channel_id=1, source_target_pairs={{0,4},{2,6},{4,0},{6,2},{8,12},{10,14},{12,8},{14,10},{16,20},{18,... | collective-permute-start | bytes 786440 | tf_op jit(solution)/shard_map/ppermute | solution.py:39
  50.6 1.3 %collective-permute-start.13 = (bf16[2,256,256]{2,1,0:T(8,128)(2,1)S(1)}, bf16[2,256,256]{2,1,0:T(8,128)(2,1)S(1)}, u32[]{:S(2)}, u32[]{:S(2)}) collective-permute-start(bf16[2,256,256]{2,1,0:T(8,128)(2,1)S(1)} %get-tuple-element.56), channel_id=1, source_target_pairs={{0,252},{2,254},{4,8},{6,10},{8,4},{10,6},{12,16},{14,18},{16,12},... | collective-permute-start | bytes 786440 | tf_op jit(solution)/shard_map/ppermute | solution.py:39
  52.2 6.0 %collective-permute-start.11 = (bf16[2,256,256]{2,1,0:T(8,128)(2,1)S(1)}, bf16[2,256,256]{2,1,0:T(8,128)(2,1)S(1)}, u32[]{:S(2)}, u32[]{:S(2)}) collective-permute-start(bf16[2,256,256]{2,1,0:T(8,128)(2,1)S(1)} %add_convert_fusion), channel_id=1, source_target_pairs={{0,252},{2,254},{4,8},{6,10},{8,4},{10,6},{12,16},{14,18},{16,12},... | collective-permute-start | bytes 786440 | tf_op jit(solution)/shard_map/ppermute | solution.py:39
  58.2 3.3 %shard_map.107 = (f32[2,256,256]{2,1,0:T(8,128)S(1)}, f32[2,256,256]{2,1,0:T(8,128)S(1)}, bf16[256,256]{1,0:T(8,128)(2,1)S(1)}, bf16[256,256]{1,0:T(8,128)(2,1)S(1)}) custom-call(s32[1]{0:T(128)} %bitcast.core_ref, s32[1]{0:T(128)} %bitcast.1.chip_ref, s32[1]{0:T(128)} %bitcast.2.head_ref, bf16[2,256,256]{2,1,0:T(8,128)(2,1)S(1)} %get-tuple-element.35.refs_0_, ...), custom_call_target="tpu_custom_call" | custom-call | flops 536870912 | bytes 4194304 | tf_op jit(solution)/shard_map/pallas_call | solution.py:428
  61.5 3.0 %collective-permute-start.7 = (bf16[256,256]{1,0:T(8,128)(2,1)S(1)}, bf16[256,256]{1,0:T(8,128)(2,1)S(1)}, u32[]{:S(2)}, u32[]{:S(2)}) collective-permute-start(bf16[256,256]{1,0:T(8,128)(2,1)S(1)} %get-tuple-element.45), channel_id=1, source_target_pairs={{0,2},{2,0},{4,6},{6,4},{8,10},{10,8},{12,14},{14,12},{16,18},{18,... | collective-permute-start | bytes 393224 | tf_op jit(solution)/shard_map/ppermute | solution.py:33
  64.5 1.0 collective-permute-done.7.refs_1_
  65.5 0.5 shard_map.108
  66.0 1.4 %collective-permute-done.11.refs_3_ = bf16[2,256,256]{2,1,0:T(8,128)(2,1)S(1)} collective-permute-done((bf16[2,256,256]{2,1,0:T(8,128)(2,1)S(1)}, bf16[2,256,256]{2,1,0:T(8,128)(2,1)S(1)}, u32[]{:S(2)}, u32[]{:S(2)}) %collective-permute-start.11) | collective-permute-done | bytes 262176 | tf_op jit(solution)/shard_map/ppermute | solution.py:39
  67.4 0.2 shard_map.109
  67.6 3.5 %collective-permute-start.14 = (bf16[2,256,256]{2,1,0:T(8,128)(2,1)S(1)}, bf16[2,256,256]{2,1,0:T(8,128)(2,1)S(1)}, u32[]{:S(2)}, u32[]{:S(2)}) collective-permute-start(bf16[2,256,256]{2,1,0:T(8,128)(2,1)S(1)} %get-tuple-element.58), channel_id=1, source_target_pairs={{0,2},{2,0},{4,6},{6,4},{8,10},{10,8},{12,14},{14,12},{16,18},{18,... | collective-permute-start | bytes 786440 | tf_op jit(solution)/shard_map/ppermute | solution.py:33
  71.1 0.3 shard_map.111.refs_0_
  71.4 0.8 collective-permute-done.14.refs_2_.refs_1_
  72.3 0.3 shard_map.112
  72.6 0.4 collective-permute-start.15
  73.0 0.5 shard_map.110.own_ref
  73.5 6.6 %collective-permute-done.15.got_ref = bf16[256,512]{1,0:T(8,128)(2,1)S(1)} collective-permute-done((bf16[256,512]{1,0:T(8,128)(2,1)S(1)}, bf16[256,512]{1,0:T(8,128)(2,1)S(1)}, u32[]{:S(2)}, u32[]{:S(2)}) %collective-permute-start.15) | collective-permute-done | bytes 262176 | tf_op jit(solution)/shard_map/ppermute | solution.py:456
  80.1 0.3 shard_map.113
  80.6 26.3 %all_to_all.11 = bf16[128,4,512]{2,1,0:T(4,128)(2,1)S(1)} all-to-all(bf16[128,4,512]{2,1,0:T(4,128)(2,1)S(1)} %all_to_all.7), channel_id=1, replica_groups={{208,210,212,214,224,226,228,230,56,58,60,62,8,10,12,14,24,26,28,30,232..., dimensions={0} | all-to-all | bytes 1048576 | tf_op jit(solution)/shard_map/all_to_all | solution.py:467
  107.0 0.8 shard_map.114
  (31 shorter events, 1.0 us)
Async XLA Ops:
  1.4 4.9 %collective-permute-start = (bf16[272,1024]{1,0:T(8,128)(2,1)S(1)}, bf16[272,1024]{1,0:T(8,128)(2,1)S(1)}, u32[]{:S(2)}, u32[]{:S(2)}) collective-permute-start(bf16[272,1024]{1,0:T(8,128)(2,1)S(1)} %get-tuple-element.34), channel_id=1, source_target_pairs={{0,2},{2,0},{4,6},{6,4},{8,10},{10,8},{12,14},{14,12},{16,18},{18,... | collective-permute-start | bytes 1671176 | tf_op jit(solution)/shard_map/ppermute | solution.py:33
  6.3 17.0 %copy-start.3 = (s32[512,1]{1,0:T(8,128)S(1)}, s32[512,1]{1,0:T(8,128)}, u32[]{:S(2)}) copy-start(s32[512,1]{1,0:T(8,128)} %constant.12.clone.label_ref) | copy-start | bytes 6148
  6.4 16.8 %copy-start.4 = (s32[256,1]{0,1:T(1,128)S(1)}, s32[256,1]{0,1:T(1,128)}, u32[]{:S(2)}) copy-start(s32[256,1]{0,1:T(1,128)} %param.18) | copy-start | bytes 3076
  6.4 11.0 %collective-permute-start.3 = (bf16[2,256,256]{2,1,0:T(8,128)(2,1)S(1)}, bf16[2,256,256]{2,1,0:T(8,128)(2,1)S(1)}, u32[]{:S(2)}, u32[]{:S(2)}) collective-permute-start(bf16[2,256,256]{2,1,0:T(8,128)(2,1)S(1)} %get-tuple-element.35.refs_0_), channel_id=1, source_target_pairs={{0,4},{2,6},{4,0},{6,2},{8,12},{10,14},{12,8},{14,10},{16,20},{18,... | collective-permute-start | bytes 786440 | tf_op jit(solution)/shard_map/ppermute | solution.py:39
  6.5 16.7 %collective-permute-start.1 = (bf16[2,256,256]{2,1,0:T(8,128)(2,1)S(1)}, bf16[2,256,256]{2,1,0:T(8,128)(2,1)S(1)}, u32[]{:S(2)}, u32[]{:S(2)}) collective-permute-start(bf16[2,256,256]{2,1,0:T(8,128)(2,1)S(1)} %get-tuple-element.36.refs_1_), channel_id=1, source_target_pairs={{0,252},{2,254},{4,8},{6,10},{8,4},{10,6},{12,16},{14,18},{16,12},... | collective-permute-start | bytes 786440 | tf_op jit(solution)/shard_map/ppermute | solution.py:39
  16.0 7.5 %collective-permute-start.6 = (bf16[2,256,256]{2,1,0:T(8,128)(2,1)S(1)}, bf16[2,256,256]{2,1,0:T(8,128)(2,1)S(1)}, u32[]{:S(2)}, u32[]{:S(2)}) collective-permute-start(bf16[2,256,256]{2,1,0:T(8,128)(2,1)S(1)} %get-tuple-element.36.refs_1_), channel_id=1, source_target_pairs={{0,4},{2,6},{4,0},{6,2},{8,12},{10,14},{12,8},{14,10},{16,20},{18,... | collective-permute-start | bytes 786440 | tf_op jit(solution)/shard_map/ppermute | solution.py:39
  16.0 12.6 %collective-permute-start.5 = (bf16[2,256,256]{2,1,0:T(8,128)(2,1)S(1)}, bf16[2,256,256]{2,1,0:T(8,128)(2,1)S(1)}, u32[]{:S(2)}, u32[]{:S(2)}) collective-permute-start(bf16[2,256,256]{2,1,0:T(8,128)(2,1)S(1)} %get-tuple-element.35.refs_0_), channel_id=1, source_target_pairs={{0,252},{2,254},{4,8},{6,10},{8,4},{10,6},{12,16},{14,18},{16,12},... | collective-permute-start | bytes 786440 | tf_op jit(solution)/shard_map/ppermute | solution.py:39
  17.4 16.8 %collective-permute-start.4 = (bf16[2,256,256]{2,1,0:T(8,128)(2,1)S(1)}, bf16[2,256,256]{2,1,0:T(8,128)(2,1)S(1)}, u32[]{:S(2)}, u32[]{:S(2)}) collective-permute-start(bf16[2,256,256]{2,1,0:T(8,128)(2,1)S(1)} %collective-permute-done.3.refs_2_.refs_0_), channel_id=1, source_target_pairs={{0,252},{2,254},{4,8},{6,10},{8,4},{10,6},{12,16},{14,18},{16,12},... | collective-permute-start | bytes 786440 | tf_op jit(solution)/shard_map/ppermute | solution.py:39
  23.2 11.0 %collective-permute-start.2 = (bf16[2,256,256]{2,1,0:T(8,128)(2,1)S(1)}, bf16[2,256,256]{2,1,0:T(8,128)(2,1)S(1)}, u32[]{:S(2)}, u32[]{:S(2)}) collective-permute-start(bf16[2,256,256]{2,1,0:T(8,128)(2,1)S(1)} %collective-permute-done.1.refs_0_.refs_1_), channel_id=1, source_target_pairs={{0,4},{2,6},{4,0},{6,2},{8,12},{10,14},{12,8},{14,10},{16,20},{18,... | collective-permute-start | bytes 786440 | tf_op jit(solution)/shard_map/ppermute | solution.py:39
  37.2 14.7 %collective-permute-start.8 = (bf16[2,256,256]{2,1,0:T(8,128)(2,1)S(1)}, bf16[2,256,256]{2,1,0:T(8,128)(2,1)S(1)}, u32[]{:S(2)}, u32[]{:S(2)}) collective-permute-start(bf16[2,256,256]{2,1,0:T(8,128)(2,1)S(1)} %get-tuple-element.52), channel_id=1, source_target_pairs={{0,252},{2,254},{4,8},{6,10},{8,4},{10,6},{12,16},{14,18},{16,12},... | collective-permute-start | bytes 786440 | tf_op jit(solution)/shard_map/ppermute | solution.py:39
  43.2 8.8 %collective-permute-start.10 = (bf16[2,256,256]{2,1,0:T(8,128)(2,1)S(1)}, bf16[2,256,256]{2,1,0:T(8,128)(2,1)S(1)}, u32[]{:S(2)}, u32[]{:S(2)}) collective-permute-start(bf16[2,256,256]{2,1,0:T(8,128)(2,1)S(1)} %get-tuple-element.54), channel_id=1, source_target_pairs={{0,4},{2,6},{4,0},{6,2},{8,12},{10,14},{12,8},{14,10},{16,20},{18,... | collective-permute-start | bytes 786440 | tf_op jit(solution)/shard_map/ppermute | solution.py:39
  49.1 16.9 %collective-permute-start.12 = (bf16[2,256,256]{2,1,0:T(8,128)(2,1)S(1)}, bf16[2,256,256]{2,1,0:T(8,128)(2,1)S(1)}, u32[]{:S(2)}, u32[]{:S(2)}) collective-permute-start(bf16[2,256,256]{2,1,0:T(8,128)(2,1)S(1)} %get-tuple-element.55), channel_id=1, source_target_pairs={{0,4},{2,6},{4,0},{6,2},{8,12},{10,14},{12,8},{14,10},{16,20},{18,... | collective-permute-start | bytes 786440 | tf_op jit(solution)/shard_map/ppermute | solution.py:39
  50.6 15.4 %collective-permute-start.13 = (bf16[2,256,256]{2,1,0:T(8,128)(2,1)S(1)}, bf16[2,256,256]{2,1,0:T(8,128)(2,1)S(1)}, u32[]{:S(2)}, u32[]{:S(2)}) collective-permute-start(bf16[2,256,256]{2,1,0:T(8,128)(2,1)S(1)} %get-tuple-element.56), channel_id=1, source_target_pairs={{0,252},{2,254},{4,8},{6,10},{8,4},{10,6},{12,16},{14,18},{16,12},... | collective-permute-start | bytes 786440 | tf_op jit(solution)/shard_map/ppermute | solution.py:39
  52.0 14.1 %collective-permute-start.9 = (bf16[2,256,256]{2,1,0:T(8,128)(2,1)S(1)}, bf16[2,256,256]{2,1,0:T(8,128)(2,1)S(1)}, u32[]{:S(2)}, u32[]{:S(2)}) collective-permute-start(bf16[2,256,256]{2,1,0:T(8,128)(2,1)S(1)} %add_convert_fusion.1), channel_id=1, source_target_pairs={{0,4},{2,6},{4,0},{6,2},{8,12},{10,14},{12,8},{14,10},{16,20},{18,... | collective-permute-start | bytes 786440 | tf_op jit(solution)/shard_map/ppermute | solution.py:39
  52.1 13.4 %copy-start.2 = (bf16[1024,512]{1,0:T(8,128)(2,1)S(1)}, bf16[1024,512]{1,0:T(8,128)(2,1)}, u32[]{:S(2)}) copy-start(bf16[1024,512]{1,0:T(8,128)(2,1)} %refs_2_.5) | copy-start | bytes 3145732
  52.2 15.2 %collective-permute-start.11 = (bf16[2,256,256]{2,1,0:T(8,128)(2,1)S(1)}, bf16[2,256,256]{2,1,0:T(8,128)(2,1)S(1)}, u32[]{:S(2)}, u32[]{:S(2)}) collective-permute-start(bf16[2,256,256]{2,1,0:T(8,128)(2,1)S(1)} %add_convert_fusion), channel_id=1, source_target_pairs={{0,252},{2,254},{4,8},{6,10},{8,4},{10,6},{12,16},{14,18},{16,12},... | collective-permute-start | bytes 786440 | tf_op jit(solution)/shard_map/ppermute | solution.py:39
  61.5 4.0 %collective-permute-start.7 = (bf16[256,256]{1,0:T(8,128)(2,1)S(1)}, bf16[256,256]{1,0:T(8,128)(2,1)S(1)}, u32[]{:S(2)}, u32[]{:S(2)}) collective-permute-start(bf16[256,256]{1,0:T(8,128)(2,1)S(1)} %get-tuple-element.45), channel_id=1, source_target_pairs={{0,2},{2,0},{4,6},{6,4},{8,10},{10,8},{12,14},{14,12},{16,18},{18,... | collective-permute-start | bytes 393224 | tf_op jit(solution)/shard_map/ppermute | solution.py:33
  67.4 3.7 %copy-start = (bf16[1024,512]{1,0:T(8,128)(2,1)S(1)}, bf16[1024,512]{1,0:T(8,128)(2,1)}, u32[]{:S(2)}) copy-start(bf16[1024,512]{1,0:T(8,128)(2,1)} %refs_2_.7) | copy-start | bytes 3145732
  67.4 3.7 %copy-start.1 = (bf16[1024,512]{1,0:T(8,128)(2,1)S(1)}, bf16[1024,512]{1,0:T(8,128)(2,1)}, u32[]{:S(2)}) copy-start(bf16[1024,512]{1,0:T(8,128)(2,1)} %refs_3_.7) | copy-start | bytes 3145732
  67.6 4.6 %collective-permute-start.14 = (bf16[2,256,256]{2,1,0:T(8,128)(2,1)S(1)}, bf16[2,256,256]{2,1,0:T(8,128)(2,1)S(1)}, u32[]{:S(2)}, u32[]{:S(2)}) collective-permute-start(bf16[2,256,256]{2,1,0:T(8,128)(2,1)S(1)} %get-tuple-element.58), channel_id=1, source_target_pairs={{0,2},{2,0},{4,6},{6,4},{8,10},{10,8},{12,14},{14,12},{16,18},{18,... | collective-permute-start | bytes 786440 | tf_op jit(solution)/shard_map/ppermute | solution.py:33
  72.6 7.5 %collective-permute-start.15 = (bf16[256,512]{1,0:T(8,128)(2,1)S(1)}, bf16[256,512]{1,0:T(8,128)(2,1)S(1)}, u32[]{:S(2)}, u32[]{:S(2)}) collective-permute-start(bf16[256,512]{1,0:T(8,128)(2,1)S(1)} %shard_map.112), channel_id=1, source_target_pairs={{0,1},{1,0},{2,3},{3,2},{4,5},{5,4},{6,7},{7,6},{8,9},{9,8},{10,11... | collective-permute-start | bytes 786440 | tf_op jit(solution)/shard_map/ppermute | solution.py:456

commit v4 on v3

--- a/solution.py
+++ b/solution.py
@@ -35,7 +35,7 @@
 
 def chip_swapped(value, odd):
     count = lax.axis_size("blk")
-    ahead = [2 if (s // 2) % 2 == odd else -2 for s in range(count)]
+    ahead = [-2 if (s // 2) % 2 == odd else 2 for s in range(count)]
     return lax.ppermute(value, "blk", [(s, (s + ahead[s]) % count) for s in range(count)])
 
 
@@ -137,16 +137,16 @@
                 stats_ref[t, h, row : row + 1, :] = stats[row]
 
 
-def first_stats_kernel(ids, a_ref, b_ref, ea_ref, eb_ref, qg_ref, bias_ref, stats_ref):
+def first_stats_kernel(ids, a_ref, b_ref, oa_ref, ob_ref, qg_ref, bias_ref, stats_ref):
     odd = ids[1]
-    names = (4 - odd, 3 + odd, 5 - 3 * odd, 6 - 5 * odd)
-    fold_windows(names, (a_ref, b_ref, ea_ref, eb_ref), qg_ref, bias_ref, None, stats_ref)
-
-
-def second_stats_kernel(ids, oa_ref, ob_ref, qg_ref, bias_ref, before_ref, stats_ref):
+    names = (4 - odd, 3 + odd, 2 + 3 * odd, 1 + 5 * odd)
+    fold_windows(names, (a_ref, b_ref, oa_ref, ob_ref), qg_ref, bias_ref, None, stats_ref)
+
+
+def second_stats_kernel(ids, ea_ref, eb_ref, qg_ref, bias_ref, before_ref, stats_ref):
     odd = ids[1]
-    names = (2 + 3 * odd, 1 + 5 * odd)
-    fold_windows(names, (oa_ref, ob_ref), qg_ref, bias_ref, before_ref, stats_ref)
+    names = (5 - 3 * odd, 6 - 5 * odd)
+    fold_windows(names, (ea_ref, eb_ref), qg_ref, bias_ref, before_ref, stats_ref)
 
 
 def head_rows_of(first, second):
@@ -164,33 +164,58 @@
 
 
 def far_kernel(
-    ids, e_ref, o_ref, qg_ref, bias_ref, stats_ref, final_ref, de_ref, do_ref, dq_ref,
-    ps_ref, ds_ref, qs_ref, gs_ref,
+    ids, e_ref, o_ref, qg_ref, bias_ref, stats_ref, final_ref, de_ref, do_ref, ds_ref, ps_ref, qs_ref, gs_ref
 ):
     rows = qg_ref.shape[2]
     odd = ids[1]
-    for n, (t, window, out_ref) in enumerate(((1 - odd, e_ref, de_ref), (odd, o_ref, do_ref))):
-        for h in range(2):
-            cols = slice(h * rows, (h + 1) * rows)
-            qh = one_head(qg_ref.at[0, t], h)
-            gh = one_head(qg_ref.at[1, t], h)
-            qs_ref[n, cols, :] = qh
-            gs_ref[n, cols, :] = gh
-            bias_pair = bias_pair_of(bias_ref, t, (SPAN - 1) * t)
-            stats = tuple(stats_ref[t, h, row : row + 1, :] for row in range(3))
-            (top, total, delta), scores, grads = fold_stats(stats, window, qh, gh, bias_pair)
-            log_total = top * LOG2E + jnp.log2(total)
-            delta = delta / total
-            final_ref[t, h, 0:1, :] = log_total
-            final_ref[t, h, 1:2, :] = delta
-            for b in range(2):
-                at = slice(b * BLOCK, (b + 1) * BLOCK)
-                prob = jnp.exp2(scores[at] * LOG2E + (bias_pair[b] * LOG2E - log_total))
-                ps_ref[n, at, cols] = prob.astype(BF)
-                ds_ref[n, at, cols] = (prob * (grads[at] - delta)).astype(BF)
-        out_ref[0] = dot(ds_ref[n], qs_ref[n], NN).astype(BF)
+    sides = ((1 - odd, e_ref, de_ref), (odd, o_ref, do_ref))
+    halves = [slice(b * BLOCK, (b + 1) * BLOCK) for b in range(2)]
+    items = [(n, h) for n in range(2) for h in range(2)]
+    scores, grads, biases = [], [], []
+    for n, h in items:
+        t, window, _ = sides[n]
+        cols = slice(h * rows, (h + 1) * rows)
+        qh = one_head(qg_ref.at[0, t], h)
+        gh = one_head(qg_ref.at[1, t], h)
+        qs_ref[n, cols, :] = qh
+        gs_ref[n, cols, :] = gh
+        scores.append(dot(window[0], qh, NT))
+        grads.append(dot(window[1], gh, NT))
+        biases.append(bias_pair_of(bias_ref, t, (SPAN - 1) * t))
+    before = [[stats_ref[sides[n][0], h, row : row + 1, :] for row in range(3)] for n, h in items]
+    tops = []
+    for value, bias, (top, _, _) in zip(scores, biases, before):
+        for at, block_bias in zip(halves, bias):
+            top = jnp.maximum(top, jnp.max(value[at], axis=0, keepdims=True) + block_bias)
+        tops.append(top)
+    weights, totals, deltas = [], [], []
+    for value, grad, bias, top, (old, total, delta) in zip(scores, grads, biases, tops, before):
+        shrink = jnp.exp2((old - top) * LOG2E)
+        total = total * shrink
+        delta = delta * shrink
+        parts = []
+        for at, block_bias in zip(halves, bias):
+            weight = jnp.exp2(value[at] * LOG2E + (block_bias - top) * LOG2E)
+            total = total + jnp.sum(weight, axis=0, keepdims=True)
+            delta = delta + jnp.sum(weight * grad[at], axis=0, keepdims=True)
+            parts.append(weight)
+        weights.append(parts)
+        totals.append(total)
+        deltas.append(delta)
+    for (n, h), parts, grad, top, total, delta in zip(items, weights, grads, tops, totals, deltas):
+        cols = slice(h * rows, (h + 1) * rows)
+        scale = 1.0 / total
+        delta = delta * scale
+        final_ref[sides[n][0], h, 0:1, :] = top * LOG2E + jnp.log2(total)
+        final_ref[sides[n][0], h, 1:2, :] = delta
+        for at, weight in zip(halves, parts):
+            prob = weight * scale
+            ps_ref[n, at, cols] = prob.astype(BF)
+            ds_ref[0, n, at, cols] = (prob * (grad[at] - delta)).astype(BF)
+    for n in range(2):
+        out_ref = sides[n][2]
+        out_ref[0] = dot(ds_ref[0, n], qs_ref[n], NN).astype(BF)
         out_ref[1] = dot(ps_ref[n], gs_ref[n], NN).astype(BF)
-        dq_ref[0, t] = query_grad(flipped(window[0]), ds_ref[n], rows)
 
 
 def shared_kernel(names, qg_ref, bias_ref, final_ref, windows, outs, ps_ref, ds_ref, qs_ref, gs_ref, kt_ref):
@@ -227,20 +252,25 @@
     ]
 
 
-def near_kernel(ids, ea_ref, oa_ref, eb_ref, ob_ref, qg_ref, bias_ref, final_ref, part_ref, *refs):
+def near_kernel(ids, ea_ref, oa_ref, eb_ref, ob_ref, qg_ref, bias_ref, final_ref, *refs):
     outs, dq_ref, scratch = refs[0:4], refs[4], refs[5:]
     odd = ids[1]
     names = (5 - 3 * odd, 2 + 3 * odd, 6 - 5 * odd, 1 + 5 * odd)
     grads = shared_kernel(names, qg_ref, bias_ref, final_ref, (ea_ref, oa_ref, eb_ref, ob_ref), outs, *scratch)
     for t in range(2):
-        dq_ref[0, t] = part_ref[0, t] + grads[t]
-
-
-def local_kernel(ids, a_ref, b_ref, qg_ref, bias_ref, final_ref, part_ref, *refs):
+        dq_ref[0, t] = grads[t]
+
+
+def local_kernel(ids, a_ref, b_ref, ef_ref, of_ref, qg_ref, bias_ref, final_ref, part_ref, far_ref, *refs):
     outs, (dq_own_ref, dq_send_ref), scratch = refs[0:2], refs[2:4], refs[4:]
+    rows = qg_ref.shape[2]
     odd = ids[1]
     grads = shared_kernel((4 - odd, 3 + odd), qg_ref, bias_ref, final_ref, (a_ref, b_ref), outs, *scratch)
-    total = [part_ref[0, t] + grads[t] for t in range(2)]
+    far_e = query_grad(flipped(ef_ref[0]), far_ref[0, 0], rows)
+    far_o = query_grad(flipped(of_ref[0]), far_ref[0, 1], rows)
+    even = odd == 0
+    far = (jnp.where(even, far_o, far_e), jnp.where(even, far_e, far_o))
+    total = [part_ref[0, t] + grads[t] + far[t] for t in range(2)]
     first = ids[0] == 0
     scale = 1.0 / math.sqrt(HD)
     dq_own_ref[...] = jnp.transpose(jnp.where(first, total[0], total[1]) * scale).astype(BF)
@@ -326,7 +356,7 @@
     block = lax.axis_index("blk")
     ids = tuple(
         jnp.reshape(value, (1,)).astype(jnp.int32)
-        for value in (block & 1, (block >> 1) & 1, lax.axis_index("head"))
+        for value in (block & 1, 1 - ((block >> 1) & 1), lax.axis_index("head"))
     )
     smem = pl.BlockSpec(memory_space=pltpu.SMEM)
     hbm = pl.BlockSpec(memory_space=pltpu.HBM)
@@ -401,25 +431,26 @@
     stats = call(
         first_stats_kernel, stat_shape, (pairs,), [win] * 4 + [near, bias_spec], stat_spec,
         estimate=cost(16 * step, 4 << 20),
-    )(*ids, a, b, ea, eb, qg, bias)
+    )(*ids, a, b, oa, ob, qg, bias)
     stats = call(
         second_stats_kernel, stat_shape, (pairs,), [win] * 2 + [near, bias_spec, stat_spec], stat_spec,
         estimate=cost(8 * step, 2 << 20),
-    )(*ids, oa, ob, qg, bias, stats)
+    )(*ids, ea, eb, qg, bias, stats)
     stats, place = lax.optimization_barrier((stats, place))
-    far_probs = pltpu.VMEM((2, rows, 2 * rows), BF)
     far_rows = pltpu.VMEM((2, 2 * rows, pair), BF)
-    final, d_ef, d_of, dq_far = call(
-        far_kernel, (stat_shape, kv_shape, kv_shape, part_shape), (pairs,),
-        [win] * 2 + [near, bias_spec, stat_spec], (stat_spec, win, win, part_spec),
-        scratch=(far_probs, far_probs, far_rows, far_rows), estimate=cost(8 * step, 2 << 20),
+    far_shape = sds((pairs, 2, rows, 2 * rows), BF)
+    far_spec = pl.BlockSpec((1, 2, rows, 2 * rows), lambda i, *p: (i, 0, 0, 0))
+    final, d_ef, d_of, ds_far = call(
+        far_kernel, (stat_shape, kv_shape, kv_shape, far_shape), (pairs,),
+        [win] * 2 + [near, bias_spec, stat_spec], (stat_spec, win, win, far_spec),
+        scratch=(pltpu.VMEM((2, rows, 2 * rows), BF), far_rows, far_rows), estimate=cost(8 * step, 2 << 20),
     )(*ids, ef, of, qg, bias, stats)
     back_ef = chip_swapped(d_ef, 0)
     back_of = chip_swapped(d_of, 1)
     d_ea, d_oa, d_eb, d_ob, dq_near = call(
-        near_kernel, (kv_shape,) * 4 + (part_shape,), (pairs,), [win] * 4 + [near, bias_spec, stat_spec, part_spec],
+        near_kernel, (kv_shape,) * 4 + (part_shape,), (pairs,), [win] * 4 + [near, bias_spec, stat_spec],
         (win,) * 4 + (part_spec,), scratch=scratch(4), estimate=cost(32 * step, 4 << 20),
-    )(*ids, ea, oa, eb, ob, qg, bias, final, dq_far)
+    )(*ids, ea, oa, eb, ob, qg, bias, final)
     back_eb = chip_swapped(d_eb, 0)
     back_ob = chip_swapped(d_ob, 1)
     back_ea = chip_swapped(joined(d_ea, back_of), 0)
@@ -427,9 +458,9 @@
     own_shape = sds((2, rows, half), F32)
     d_a, d_b, dq_own, dq_send = call(
         local_kernel, (own_shape, own_shape, sds((rows, half), BF), sds((rows, half), BF)), (pairs,),
-        [win] * 2 + [near, bias_spec, stat_spec, part_spec], (win, win, dq_spec, dq_spec),
+        [win] * 4 + [near, bias_spec, stat_spec, part_spec, far_spec], (win, win, dq_spec, dq_spec),
         scratch=scratch(2), estimate=cost(16 * step, 4 << 20),
-    )(*ids, a, b, qg, bias, final, dq_near)
+    )(*ids, a, b, ef, of, qg, bias, final, dq_near, ds_far)
     dq_got = core_swapped(dq_send)
     q_other, q_own = call(
         query_kernel, (sds((rows, cols), F32), sds((rows, cols), F32)), (1,),

time: 108 us -> 106 us (0.981)
    ppermute x12, starting transfers between devices: 31.7 us -> 29.8 us  [chip_swapped(): lax.ppermute(value, 'blk', [(s, (s + ahead[s]) % count) for s in range(co...]
  transfers between devices with their start and end apart: 16 -> 16, of which waited for: 7 -> 6; matrix products, arithmetic and copies ran while one was open for 0% -> 0% of each run, Pallas kernels for 15% -> 16%
where the time goes in v4:
time: 106 us
  starting transfers between devices  41 us (39%)
  blocking collectives  26.3 us (25%)
  Pallas kernels  22.2 us (21%)
  waiting for transfers between devices  15.7 us (15%)
    ppermute x12, starting transfers between devices, chip_swapped(): lax.ppermute(value, 'blk', [(s, (s + ahead[s]) % count) for s in range(co...  29.8 us
    all_to_all x1, blocking collectives, on_device(): lax.all_to_all(outgoing, 'blk', split_axis=0, concat_axis=0, tiled=True,...  26.3 us
    ppermute x3, starting transfers between devices, core_swapped(): return lax.ppermute(value, 'blk', [(s, s ^ 1) for s in range(count)])  10.9 us
    ppermute x1, waiting for transfers between devices, on_device(): partial_got = lax.ppermute(partial_other, 'head', [(0, 1), (1, 0)])  6.66 us
    pallas_call x1, Pallas kernels, on_device(): call(near_kernel, (kv_shape,) * 4 + (part_shape,), (pairs,), [win] * 4 +...  5.8 us
    ppermute x12, waiting for transfers between devices, chip_swapped(): lax.ppermute(value, 'blk', [(s, (s + ahead[s]) % count) for s in range(co...  5.65 us
    pallas_call x1, Pallas kernels, on_device(): call(local_kernel, (own_shape, own_shape, sds((rows, half), BF), sds((row...  3.63 us
    pallas_call x1, Pallas kernels, on_device(): call(first_stats_kernel, stat_shape, (pairs,), [win] * 4 + [near, bias_sp...  3.56 us
  transfers between devices with their start and end apart: 16, of which 6 were waited for; matrix products, arithmetic and copies ran while one was open for 0% of the time, Pallas kernels for 16%

profile of v4, /device:TPU:1, one launch (start us, length us, event | category | flops | bytes accessed | tf_op | source)
XLA Modules:
  0.0 106.1 jit_solution(10305419400719269787)
XLA Ops:
  0.0 1.4 %shard_map.100 = (bf16[272,1024]{1,0:T(8,128)(2,1)S(1)}, bf16[272,1024]{1,0:T(8,128)(2,1)S(1)}) custom-call(s32[1]{0:T(128)} %bitcast.core_ref, s32[1]{0:T(128)} %bitcast.1.chip_ref, s32[1]{0:T(128)} %bitcast.2.head_ref, s32[2,14]{1,0:T(2,128)} %refs_0_.1, bf16[256,512]{1,0:T(8,128)(2,1)} %refs_1_.1, bf16[256,512]{1,0:T(8,128)(2,1)} %refs_2_.4, ...), custom_call_target="tpu_custom_call" | custom-call | tf_op jit(solution)/shard_map/pallas_call | solution.py:380
  1.4 3.3 %collective-permute-start = (bf16[272,1024]{1,0:T(8,128)(2,1)S(1)}, bf16[272,1024]{1,0:T(8,128)(2,1)S(1)}, u32[]{:S(2)}, u32[]{:S(2)}) collective-permute-start(bf16[272,1024]{1,0:T(8,128)(2,1)S(1)} %get-tuple-element.34), channel_id=1, source_target_pairs={{0,2},{2,0},{4,6},{6,4},{8,10},{10,8},{12,14},{14,12},{16,18},{18,... | collective-permute-start | bytes 1671176 | tf_op jit(solution)/shard_map/ppermute | solution.py:33
  4.7 1.6 %collective-permute-done.refs_1_ = bf16[272,1024]{1,0:T(8,128)(2,1)S(1)} collective-permute-done((bf16[272,1024]{1,0:T(8,128)(2,1)S(1)}, bf16[272,1024]{1,0:T(8,128)(2,1)S(1)}, u32[]{:S(2)}, u32[]{:S(2)}) %collective-permute-start) | collective-permute-done | bytes 557088 | tf_op jit(solution)/shard_map/ppermute | solution.py:33
  6.4 8.8 %collective-permute-start.3 = (bf16[2,256,256]{2,1,0:T(8,128)(2,1)S(1)}, bf16[2,256,256]{2,1,0:T(8,128)(2,1)S(1)}, u32[]{:S(2)}, u32[]{:S(2)}) collective-permute-start(bf16[2,256,256]{2,1,0:T(8,128)(2,1)S(1)} %get-tuple-element.35.refs_0_), channel_id=1, source_target_pairs={{0,252},{2,254},{4,8},{6,10},{8,4},{10,6},{12,16},{14,18},{16,12},... | collective-permute-start | bytes 786440 | tf_op jit(solution)/shard_map/ppermute | solution.py:39
  15.2 1.5 %collective-permute-start.6 = (bf16[2,256,256]{2,1,0:T(8,128)(2,1)S(1)}, bf16[2,256,256]{2,1,0:T(8,128)(2,1)S(1)}, u32[]{:S(2)}, u32[]{:S(2)}) collective-permute-start(bf16[2,256,256]{2,1,0:T(8,128)(2,1)S(1)} %get-tuple-element.35.refs_0_), channel_id=1, source_target_pairs={{0,4},{2,6},{4,0},{6,2},{8,12},{10,14},{12,8},{14,10},{16,20},{18,... | collective-permute-start | bytes 786440 | tf_op jit(solution)/shard_map/ppermute | solution.py:39
  16.8 4.8 %collective-permute-done.3.refs_0_ = bf16[2,256,256]{2,1,0:T(8,128)(2,1)S(1)} collective-permute-done((bf16[2,256,256]{2,1,0:T(8,128)(2,1)S(1)}, bf16[2,256,256]{2,1,0:T(8,128)(2,1)S(1)}, u32[]{:S(2)}, u32[]{:S(2)}) %collective-permute-start.3) | collective-permute-done | bytes 262176 | tf_op jit(solution)/shard_map/ppermute | solution.py:39
  21.6 0.8 collective-permute-done.1.refs_2_.refs_1_
  22.4 6.1 %collective-permute-start.2 = (bf16[2,256,256]{2,1,0:T(8,128)(2,1)S(1)}, bf16[2,256,256]{2,1,0:T(8,128)(2,1)S(1)}, u32[]{:S(2)}, u32[]{:S(2)}) collective-permute-start(bf16[2,256,256]{2,1,0:T(8,128)(2,1)S(1)} %collective-permute-done.1.refs_2_.refs_1_), channel_id=1, source_target_pairs={{0,252},{2,254},{4,8},{6,10},{8,4},{10,6},{12,16},{14,18},{16,12},... | collective-permute-start | bytes 786440 | tf_op jit(solution)/shard_map/ppermute | solution.py:39
  28.5 0.1 copy.11.owner_col_ref
  28.6 0.2 shard_map.104.place_ref
  28.8 3.6 %shard_map.102.refs_4_ = f32[2,4,8,256]{3,2,1,0:T(8,128)S(1)} custom-call(s32[1]{0:T(128)} %bitcast.core_ref, s32[1]{0:T(128)} %bitcast.1.chip_ref, s32[1]{0:T(128)} %bitcast.2.head_ref, bf16[2,256,256]{2,1,0:T(8,128)(2,1)S(1)} %get-tuple-element.35.refs_0_, bf16[2,256,256]{2,1,0:T(8,128)(2,1)S(1)} %get-tuple-element.36.refs_1_, ...), custom_call_target="tpu_custom_call" | custom-call | flops 536870912 | bytes 4194304 | tf_op jit(solution)/shard_map/pallas_call | solution.py:431
  32.4 2.1 %shard_map.103.refs_4_ = f32[2,4,8,256]{3,2,1,0:T(8,128)S(1)} custom-call(s32[1]{0:T(128)} %bitcast.core_ref, s32[1]{0:T(128)} %bitcast.1.chip_ref, s32[1]{0:T(128)} %bitcast.2.head_ref, bf16[2,256,256]{2,1,0:T(8,128)(2,1)S(1)} %collective-permute-done.3.refs_0_, bf16[2,256,256]{2,1,0:T(8,128)(2,1)S(1)} %collective-permute-done.5.refs_1_.refs_2_, ...), custom_call_target="tpu_custom_call" | custom-call | flops 268435456 | bytes 2097152 | tf_op jit(solution)/shard_map/pallas_call | solution.py:435
  34.5 2.6 %shard_map.105 = (f32[2,4,8,256]{3,2,1,0:T(8,128)S(1)}, bf16[2,256,256]{2,1,0:T(8,128)(2,1)S(1)}, bf16[2,256,256]{2,1,0:T(8,128)(2,1)S(1)}, bf16[2,2,256,512]{3,2,1,0:T(8,128)(2,1)S(1)}) custom-call(s32[1]{0:T(128)} %bitcast.core_ref, s32[1]{0:T(128)} %bitcast.1.chip_ref, s32[1]{0:T(128)} %bitcast.2.head_ref, ...), custom_call_target="tpu_custom_call" | custom-call | flops 268435456 | bytes 2097152 | tf_op jit(solution)/shard_map/pallas_call | solution.py:443
  37.2 5.7 %collective-permute-start.10 = (bf16[2,256,256]{2,1,0:T(8,128)(2,1)S(1)}, bf16[2,256,256]{2,1,0:T(8,128)(2,1)S(1)}, u32[]{:S(2)}, u32[]{:S(2)}) collective-permute-start(bf16[2,256,256]{2,1,0:T(8,128)(2,1)S(1)} %get-tuple-element.54), channel_id=1, source_target_pairs={{0,252},{2,254},{4,8},{6,10},{8,4},{10,6},{12,16},{14,18},{16,12},... | collective-permute-start | bytes 786440 | tf_op jit(solution)/shard_map/ppermute | solution.py:39
  43.0 5.8 %shard_map.106 = (bf16[2,256,256]{2,1,0:T(8,128)(2,1)S(1)}, bf16[2,256,256]{2,1,0:T(8,128)(2,1)S(1)}, bf16[2,256,256]{2,1,0:T(8,128)(2,1)S(1)}, bf16[2,256,256]{2,1,0:T(8,128)(2,1)S(1)}, f32[2,2,128,256]{3,2,1,0:T(8,128)S(1)}) custom-call(s32[1]{0:T(128)} %bitcast.core_ref, s32[1]{0:T(128)} %bitcast.1.chip_ref, s32[1]{0:T(128)} %bitcast.2.head_ref, ...), custom_call_target="tpu_custom_call" | custom-call | flops 1073741824 | bytes 4194304 | tf_op jit(solution)/shard_map/pallas_call | solution.py:450
  48.8 1.8 %collective-permute-start.12 = (bf16[2,256,256]{2,1,0:T(8,128)(2,1)S(1)}, bf16[2,256,256]{2,1,0:T(8,128)(2,1)S(1)}, u32[]{:S(2)}, u32[]{:S(2)}) collective-permute-start(bf16[2,256,256]{2,1,0:T(8,128)(2,1)S(1)} %get-tuple-element.55), channel_id=1, source_target_pairs={{0,252},{2,254},{4,8},{6,10},{8,4},{10,6},{12,16},{14,18},{16,12},... | collective-permute-start | bytes 786440 | tf_op jit(solution)/shard_map/ppermute | solution.py:39
  50.7 5.6 %collective-permute-start.9 = (bf16[2,256,256]{2,1,0:T(8,128)(2,1)S(1)}, bf16[2,256,256]{2,1,0:T(8,128)(2,1)S(1)}, u32[]{:S(2)}, u32[]{:S(2)}) collective-permute-start(bf16[2,256,256]{2,1,0:T(8,128)(2,1)S(1)} %add_convert_fusion.1), channel_id=1, source_target_pairs={{0,252},{2,254},{4,8},{6,10},{8,4},{10,6},{12,16},{14,18},{16,12},... | collective-permute-start | bytes 786440 | tf_op jit(solution)/shard_map/ppermute | solution.py:39
  56.4 3.6 %shard_map.107 = (f32[2,256,256]{2,1,0:T(8,128)S(1)}, f32[2,256,256]{2,1,0:T(8,128)S(1)}, bf16[256,256]{1,0:T(8,128)(2,1)S(1)}, bf16[256,256]{1,0:T(8,128)(2,1)S(1)}) custom-call(s32[1]{0:T(128)} %bitcast.core_ref, s32[1]{0:T(128)} %bitcast.1.chip_ref, s32[1]{0:T(128)} %bitcast.2.head_ref, bf16[2,256,256]{2,1,0:T(8,128)(2,1)S(1)} %get-tuple-element.35.refs_0_, ...), custom_call_target="tpu_custom_call" | custom-call | flops 536870912 | bytes 4194304 | tf_op jit(solution)/shard_map/pallas_call | solution.py:459
  60.1 3.9 %collective-permute-start.7 = (bf16[256,256]{1,0:T(8,128)(2,1)S(1)}, bf16[256,256]{1,0:T(8,128)(2,1)S(1)}, u32[]{:S(2)}, u32[]{:S(2)}) collective-permute-start(bf16[256,256]{1,0:T(8,128)(2,1)S(1)} %get-tuple-element.45), channel_id=1, source_target_pairs={{0,2},{2,0},{4,6},{6,4},{8,10},{10,8},{12,14},{14,12},{16,18},{18,... | collective-permute-start | bytes 393224 | tf_op jit(solution)/shard_map/ppermute | solution.py:33
  63.9 1.0 collective-permute-done.7.refs_1_
  64.9 0.5 shard_map.108
  65.4 0.2 shard_map.109
  65.7 3.7 %collective-permute-start.14 = (bf16[2,256,256]{2,1,0:T(8,128)(2,1)S(1)}, bf16[2,256,256]{2,1,0:T(8,128)(2,1)S(1)}, u32[]{:S(2)}, u32[]{:S(2)}) collective-permute-start(bf16[2,256,256]{2,1,0:T(8,128)(2,1)S(1)} %get-tuple-element.58), channel_id=1, source_target_pairs={{0,2},{2,0},{4,6},{6,4},{8,10},{10,8},{12,14},{14,12},{16,18},{18,... | collective-permute-start | bytes 786440 | tf_op jit(solution)/shard_map/ppermute | solution.py:33
  69.4 0.3 shard_map.111.refs_0_
  69.7 0.8 collective-permute-done.14.refs_2_.refs_1_
  70.5 0.3 shard_map.112
  70.8 0.4 collective-permute-start.15
  71.2 0.5 shard_map.110.own_ref
  71.7 6.7 %collective-permute-done.15.got_ref = bf16[256,512]{1,0:T(8,128)(2,1)S(1)} collective-permute-done((bf16[256,512]{1,0:T(8,128)(2,1)S(1)}, bf16[256,512]{1,0:T(8,128)(2,1)S(1)}, u32[]{:S(2)}, u32[]{:S(2)}) %collective-permute-start.15) | collective-permute-done | bytes 262176 | tf_op jit(solution)/shard_map/ppermute | solution.py:487
  78.4 0.3 shard_map.113
  78.8 26.3 %all_to_all.11 = bf16[128,4,512]{2,1,0:T(4,128)(2,1)S(1)} all-to-all(bf16[128,4,512]{2,1,0:T(4,128)(2,1)S(1)} %all_to_all.7), channel_id=1, replica_groups={{208,210,212,214,224,226,228,230,56,58,60,62,8,10,12,14,24,26,28,30,232..., dimensions={0} | all-to-all | bytes 1048576 | tf_op jit(solution)/shard_map/all_to_all | solution.py:498
  105.3 0.8 shard_map.114
  (31 shorter events, 0.8 us)
Async XLA Ops:
  1.4 4.9 %collective-permute-start = (bf16[272,1024]{1,0:T(8,128)(2,1)S(1)}, bf16[272,1024]{1,0:T(8,128)(2,1)S(1)}, u32[]{:S(2)}, u32[]{:S(2)}) collective-permute-start(bf16[272,1024]{1,0:T(8,128)(2,1)S(1)} %get-tuple-element.34), channel_id=1, source_target_pairs={{0,2},{2,0},{4,6},{6,4},{8,10},{10,8},{12,14},{14,12},{16,18},{18,... | collective-permute-start | bytes 1671176 | tf_op jit(solution)/shard_map/ppermute | solution.py:33
  6.3 22.3 %copy-start.3 = (s32[512,1]{1,0:T(8,128)S(1)}, s32[512,1]{1,0:T(8,128)}, u32[]{:S(2)}) copy-start(s32[512,1]{1,0:T(8,128)} %constant.12.clone.label_ref) | copy-start | bytes 6148
  6.4 22.1 %copy-start.4 = (s32[256,1]{0,1:T(1,128)S(1)}, s32[256,1]{0,1:T(1,128)}, u32[]{:S(2)}) copy-start(s32[256,1]{0,1:T(1,128)} %param.18) | copy-start | bytes 3076
  6.4 15.2 %collective-permute-start.3 = (bf16[2,256,256]{2,1,0:T(8,128)(2,1)S(1)}, bf16[2,256,256]{2,1,0:T(8,128)(2,1)S(1)}, u32[]{:S(2)}, u32[]{:S(2)}) collective-permute-start(bf16[2,256,256]{2,1,0:T(8,128)(2,1)S(1)} %get-tuple-element.35.refs_0_), channel_id=1, source_target_pairs={{0,252},{2,254},{4,8},{6,10},{8,4},{10,6},{12,16},{14,18},{16,12},... | collective-permute-start | bytes 786440 | tf_op jit(solution)/shard_map/ppermute | solution.py:39
  15.2 7.2 %collective-permute-start.1 = (bf16[2,256,256]{2,1,0:T(8,128)(2,1)S(1)}, bf16[2,256,256]{2,1,0:T(8,128)(2,1)S(1)}, u32[]{:S(2)}, u32[]{:S(2)}) collective-permute-start(bf16[2,256,256]{2,1,0:T(8,128)(2,1)S(1)} %get-tuple-element.36.refs_1_), channel_id=1, source_target_pairs={{0,4},{2,6},{4,0},{6,2},{8,12},{10,14},{12,8},{14,10},{16,20},{18,... | collective-permute-start | bytes 786440 | tf_op jit(solution)/shard_map/ppermute | solution.py:39
  15.2 13.6 %collective-permute-start.6 = (bf16[2,256,256]{2,1,0:T(8,128)(2,1)S(1)}, bf16[2,256,256]{2,1,0:T(8,128)(2,1)S(1)}, u32[]{:S(2)}, u32[]{:S(2)}) collective-permute-start(bf16[2,256,256]{2,1,0:T(8,128)(2,1)S(1)} %get-tuple-element.35.refs_0_), channel_id=1, source_target_pairs={{0,4},{2,6},{4,0},{6,2},{8,12},{10,14},{12,8},{14,10},{16,20},{18,... | collective-permute-start | bytes 786440 | tf_op jit(solution)/shard_map/ppermute | solution.py:39
  16.7 15.7 %collective-permute-start.5 = (bf16[2,256,256]{2,1,0:T(8,128)(2,1)S(1)}, bf16[2,256,256]{2,1,0:T(8,128)(2,1)S(1)}, u32[]{:S(2)}, u32[]{:S(2)}) collective-permute-start(bf16[2,256,256]{2,1,0:T(8,128)(2,1)S(1)} %get-tuple-element.36.refs_1_), channel_id=1, source_target_pairs={{0,252},{2,254},{4,8},{6,10},{8,4},{10,6},{12,16},{14,18},{16,12},... | collective-permute-start | bytes 786440 | tf_op jit(solution)/shard_map/ppermute | solution.py:39
  21.6 12.9 %collective-permute-start.4 = (bf16[2,256,256]{2,1,0:T(8,128)(2,1)S(1)}, bf16[2,256,256]{2,1,0:T(8,128)(2,1)S(1)}, u32[]{:S(2)}, u32[]{:S(2)}) collective-permute-start(bf16[2,256,256]{2,1,0:T(8,128)(2,1)S(1)} %collective-permute-done.3.refs_0_), channel_id=1, source_target_pairs={{0,4},{2,6},{4,0},{6,2},{8,12},{10,14},{12,8},{14,10},{16,20},{18,... | collective-permute-start | bytes 786440 | tf_op jit(solution)/shard_map/ppermute | solution.py:39
  22.4 12.1 %collective-permute-start.2 = (bf16[2,256,256]{2,1,0:T(8,128)(2,1)S(1)}, bf16[2,256,256]{2,1,0:T(8,128)(2,1)S(1)}, u32[]{:S(2)}, u32[]{:S(2)}) collective-permute-start(bf16[2,256,256]{2,1,0:T(8,128)(2,1)S(1)} %collective-permute-done.1.refs_2_.refs_1_), channel_id=1, source_target_pairs={{0,252},{2,254},{4,8},{6,10},{8,4},{10,6},{12,16},{14,18},{16,12},... | collective-permute-start | bytes 786440 | tf_op jit(solution)/shard_map/ppermute | solution.py:39
  37.1 13.5 %collective-permute-start.8 = (bf16[2,256,256]{2,1,0:T(8,128)(2,1)S(1)}, bf16[2,256,256]{2,1,0:T(8,128)(2,1)S(1)}, u32[]{:S(2)}, u32[]{:S(2)}) collective-permute-start(bf16[2,256,256]{2,1,0:T(8,128)(2,1)S(1)} %get-tuple-element.52), channel_id=1, source_target_pairs={{0,4},{2,6},{4,0},{6,2},{8,12},{10,14},{12,8},{14,10},{16,20},{18,... | collective-permute-start | bytes 786440 | tf_op jit(solution)/shard_map/ppermute | solution.py:39
  37.2 19.0 %collective-permute-start.10 = (bf16[2,256,256]{2,1,0:T(8,128)(2,1)S(1)}, bf16[2,256,256]{2,1,0:T(8,128)(2,1)S(1)}, u32[]{:S(2)}, u32[]{:S(2)}) collective-permute-start(bf16[2,256,256]{2,1,0:T(8,128)(2,1)S(1)} %get-tuple-element.54), channel_id=1, source_target_pairs={{0,252},{2,254},{4,8},{6,10},{8,4},{10,6},{12,16},{14,18},{16,12},... | collective-permute-start | bytes 786440 | tf_op jit(solution)/shard_map/ppermute | solution.py:39
  48.8 16.6 %collective-permute-start.12 = (bf16[2,256,256]{2,1,0:T(8,128)(2,1)S(1)}, bf16[2,256,256]{2,1,0:T(8,128)(2,1)S(1)}, u32[]{:S(2)}, u32[]{:S(2)}) collective-permute-start(bf16[2,256,256]{2,1,0:T(8,128)(2,1)S(1)} %get-tuple-element.55), channel_id=1, source_target_pairs={{0,252},{2,254},{4,8},{6,10},{8,4},{10,6},{12,16},{14,18},{16,12},... | collective-permute-start | bytes 786440 | tf_op jit(solution)/shard_map/ppermute | solution.py:39
  50.6 14.8 %collective-permute-start.13 = (bf16[2,256,256]{2,1,0:T(8,128)(2,1)S(1)}, bf16[2,256,256]{2,1,0:T(8,128)(2,1)S(1)}, u32[]{:S(2)}, u32[]{:S(2)}) collective-permute-start(bf16[2,256,256]{2,1,0:T(8,128)(2,1)S(1)} %get-tuple-element.56), channel_id=1, source_target_pairs={{0,4},{2,6},{4,0},{6,2},{8,12},{10,14},{12,8},{14,10},{16,20},{18,... | collective-permute-start | bytes 786440 | tf_op jit(solution)/shard_map/ppermute | solution.py:39
  50.7 14.7 %collective-permute-start.9 = (bf16[2,256,256]{2,1,0:T(8,128)(2,1)S(1)}, bf16[2,256,256]{2,1,0:T(8,128)(2,1)S(1)}, u32[]{:S(2)}, u32[]{:S(2)}) collective-permute-start(bf16[2,256,256]{2,1,0:T(8,128)(2,1)S(1)} %add_convert_fusion.1), channel_id=1, source_target_pairs={{0,252},{2,254},{4,8},{6,10},{8,4},{10,6},{12,16},{14,18},{16,12},... | collective-permute-start | bytes 786440 | tf_op jit(solution)/shard_map/ppermute | solution.py:39
  56.3 9.1 %collective-permute-start.11 = (bf16[2,256,256]{2,1,0:T(8,128)(2,1)S(1)}, bf16[2,256,256]{2,1,0:T(8,128)(2,1)S(1)}, u32[]{:S(2)}, u32[]{:S(2)}) collective-permute-start(bf16[2,256,256]{2,1,0:T(8,128)(2,1)S(1)} %add_convert_fusion), channel_id=1, source_target_pairs={{0,4},{2,6},{4,0},{6,2},{8,12},{10,14},{12,8},{14,10},{16,20},{18,... | collective-permute-start | bytes 786440 | tf_op jit(solution)/shard_map/ppermute | solution.py:39
  56.4 8.5 %copy-start.2 = (bf16[1024,512]{1,0:T(8,128)(2,1)S(1)}, bf16[1024,512]{1,0:T(8,128)(2,1)}, u32[]{:S(2)}) copy-start(bf16[1024,512]{1,0:T(8,128)(2,1)} %refs_2_.5) | copy-start | bytes 3145732
  60.1 4.8 %collective-permute-start.7 = (bf16[256,256]{1,0:T(8,128)(2,1)S(1)}, bf16[256,256]{1,0:T(8,128)(2,1)S(1)}, u32[]{:S(2)}, u32[]{:S(2)}) collective-permute-start(bf16[256,256]{1,0:T(8,128)(2,1)S(1)} %get-tuple-element.45), channel_id=1, source_target_pairs={{0,2},{2,0},{4,6},{6,4},{8,10},{10,8},{12,14},{14,12},{16,18},{18,... | collective-permute-start | bytes 393224 | tf_op jit(solution)/shard_map/ppermute | solution.py:33
  65.4 3.9 %copy-start = (bf16[1024,512]{1,0:T(8,128)(2,1)S(1)}, bf16[1024,512]{1,0:T(8,128)(2,1)}, u32[]{:S(2)}) copy-start(bf16[1024,512]{1,0:T(8,128)(2,1)} %refs_2_.7) | copy-start | bytes 3145732
  65.4 3.9 %copy-start.1 = (bf16[1024,512]{1,0:T(8,128)(2,1)S(1)}, bf16[1024,512]{1,0:T(8,128)(2,1)}, u32[]{:S(2)}) copy-start(bf16[1024,512]{1,0:T(8,128)(2,1)} %refs_3_.7) | copy-start | bytes 3145732
  65.7 4.9 %collective-permute-start.14 = (bf16[2,256,256]{2,1,0:T(8,128)(2,1)S(1)}, bf16[2,256,256]{2,1,0:T(8,128)(2,1)S(1)}, u32[]{:S(2)}, u32[]{:S(2)}) collective-permute-start(bf16[2,256,256]{2,1,0:T(8,128)(2,1)S(1)} %get-tuple-element.58), channel_id=1, source_target_pairs={{0,2},{2,0},{4,6},{6,4},{8,10},{10,8},{12,14},{14,12},{16,18},{18,... | collective-permute-start | bytes 786440 | tf_op jit(solution)/shard_map/ppermute | solution.py:33
  70.8 7.5 %collective-permute-start.15 = (bf16[256,512]{1,0:T(8,128)(2,1)S(1)}, bf16[256,512]{1,0:T(8,128)(2,1)S(1)}, u32[]{:S(2)}, u32[]{:S(2)}) collective-permute-start(bf16[256,512]{1,0:T(8,128)(2,1)S(1)} %shard_map.112), channel_id=1, source_target_pairs={{0,1},{1,0},{2,3},{3,2},{4,5},{5,4},{6,7},{7,6},{8,9},{9,8},{10,11... | collective-permute-start | bytes 786440 | tf_op jit(solution)/shard_map/ppermute | solution.py:487

commit v5 on v4

--- a/solution.py
+++ b/solution.py
@@ -170,19 +170,21 @@
     odd = ids[1]
     sides = ((1 - odd, e_ref, de_ref), (odd, o_ref, do_ref))
     halves = [slice(b * BLOCK, (b + 1) * BLOCK) for b in range(2)]
-    items = [(n, h) for n in range(2) for h in range(2)]
+    pairs = qg_ref.shape[3] // (2 * HD)
+    lanes = [slice(2 * HD * i, 2 * HD * (i + 1)) for i in range(pairs)]
+    items = [(i, n, h) for i in range(pairs) for n in range(2) for h in range(2)]
     scores, grads, biases = [], [], []
-    for n, h in items:
+    for i, n, h in items:
         t, window, _ = sides[n]
         cols = slice(h * rows, (h + 1) * rows)
-        qh = one_head(qg_ref.at[0, t], h)
-        gh = one_head(qg_ref.at[1, t], h)
-        qs_ref[n, cols, :] = qh
-        gs_ref[n, cols, :] = gh
-        scores.append(dot(window[0], qh, NT))
-        grads.append(dot(window[1], gh, NT))
+        qh = one_head(qg_ref.at[0, t, :, lanes[i]], h)
+        gh = one_head(qg_ref.at[1, t, :, lanes[i]], h)
+        qs_ref[i, n, cols, :] = qh
+        gs_ref[i, n, cols, :] = gh
+        scores.append(dot(window[0, :, lanes[i]], qh, NT))
+        grads.append(dot(window[1, :, lanes[i]], gh, NT))
         biases.append(bias_pair_of(bias_ref, t, (SPAN - 1) * t))
-    before = [[stats_ref[sides[n][0], h, row : row + 1, :] for row in range(3)] for n, h in items]
+    before = [[stats_ref[sides[n][0], 2 * i + h, row : row + 1, :] for row in range(3)] for i, n, h in items]
     tops = []
     for value, bias, (top, _, _) in zip(scores, biases, before):
         for at, block_bias in zip(halves, bias):
@@ -202,20 +204,21 @@
         weights.append(parts)
         totals.append(total)
         deltas.append(delta)
-    for (n, h), parts, grad, top, total, delta in zip(items, weights, grads, tops, totals, deltas):
+    for (i, n, h), parts, grad, top, total, delta in zip(items, weights, grads, tops, totals, deltas):
         cols = slice(h * rows, (h + 1) * rows)
         scale = 1.0 / total
         delta = delta * scale
-        final_ref[sides[n][0], h, 0:1, :] = top * LOG2E + jnp.log2(total)
-        final_ref[sides[n][0], h, 1:2, :] = delta
+        final_ref[sides[n][0], 2 * i + h, 0:1, :] = top * LOG2E + jnp.log2(total)
+        final_ref[sides[n][0], 2 * i + h, 1:2, :] = delta
         for at, weight in zip(halves, parts):
             prob = weight * scale
-            ps_ref[n, at, cols] = prob.astype(BF)
-            ds_ref[0, n, at, cols] = (prob * (grad[at] - delta)).astype(BF)
-    for n in range(2):
-        out_ref = sides[n][2]
-        out_ref[0] = dot(ds_ref[0, n], qs_ref[n], NN).astype(BF)
-        out_ref[1] = dot(ps_ref[n], gs_ref[n], NN).astype(BF)
+            ps_ref[i, n, at, cols] = prob.astype(BF)
+            ds_ref[i, n, at, cols] = (prob * (grad[at] - delta)).astype(BF)
+    for i in range(pairs):
+        for n in range(2):
+            out_ref = sides[n][2]
+            out_ref[0, :, lanes[i]] = dot(ds_ref[i, n], qs_ref[i, n], NN).astype(BF)
+            out_ref[1, :, lanes[i]] = dot(ps_ref[i, n], gs_ref[i, n], NN).astype(BF)
 
 
 def shared_kernel(names, qg_ref, bias_ref, final_ref, windows, outs, ps_ref, ds_ref, qs_ref, gs_ref, kt_ref):
@@ -437,13 +440,15 @@
         estimate=cost(8 * step, 2 << 20),
     )(*ids, ea, eb, qg, bias, stats)
     stats, place = lax.optimization_barrier((stats, place))
-    far_rows = pltpu.VMEM((2, 2 * rows, pair), BF)
+    far_rows = pltpu.VMEM((pairs, 2, 2 * rows, pair), BF)
     far_shape = sds((pairs, 2, rows, 2 * rows), BF)
     far_spec = pl.BlockSpec((1, 2, rows, 2 * rows), lambda i, *p: (i, 0, 0, 0))
+    stat_whole = whole(2, 2 * pairs, 8, rows)
     final, d_ef, d_of, ds_far = call(
-        far_kernel, (stat_shape, kv_shape, kv_shape, far_shape), (pairs,),
-        [win] * 2 + [near, bias_spec, stat_spec], (stat_spec, win, win, far_spec),
-        scratch=(pltpu.VMEM((2, rows, 2 * rows), BF), far_rows, far_rows), estimate=cost(8 * step, 2 << 20),
+        far_kernel, (stat_shape, kv_shape, kv_shape, far_shape), (1,),
+        [kv_whole] * 2 + [whole(2, 2, rows, half), bias_spec, stat_whole],
+        (stat_whole, kv_whole, kv_whole, whole(pairs, 2, rows, 2 * rows)),
+        scratch=(pltpu.VMEM((pairs, 2, rows, 2 * rows), BF), far_rows, far_rows), estimate=cost(8 * step, 2 << 20),
     )(*ids, ef, of, qg, bias, stats)
     back_ef = chip_swapped(d_ef, 0)
     back_of = chip_swapped(d_of, 1)

time: 106 us -> 106 us (level)
  no operation moved by 1% of the time
where the time goes in v5:
time: 106 us; the launch traced here: 105 us
  starting transfers between devices  41 us (39%)
  blocking collectives  26.3 us (25%)
  Pallas kernels  21.6 us (20%)
  waiting for transfers between devices  15.7 us (15%)
    ppermute x12, starting transfers between devices, chip_swapped(): lax.ppermute(value, 'blk', [(s, (s + ahead[s]) % count) for s in range(co...  29.8 us
    all_to_all x1, blocking collectives, on_device(): lax.all_to_all(outgoing, 'blk', split_axis=0, concat_axis=0, tiled=True,...  26.3 us
    ppermute x3, starting transfers between devices, core_swapped(): return lax.ppermute(value, 'blk', [(s, s ^ 1) for s in range(count)])  10.9 us
    ppermute x1, waiting for transfers between devices, on_device(): partial_got = lax.ppermute(partial_other, 'head', [(0, 1), (1, 0)])  6.65 us
    pallas_call x1, Pallas kernels, on_device(): call(near_kernel, (kv_shape,) * 4 + (part_shape,), (pairs,), [win] * 4 +...  5.8 us
    ppermute x12, waiting for transfers between devices, chip_swapped(): lax.ppermute(value, 'blk', [(s, (s + ahead[s]) % count) for s in range(co...  5.65 us
    pallas_call x1, Pallas kernels, on_device(): call(local_kernel, (own_shape, own_shape, sds((rows, half), BF), sds((row...  3.63 us
    pallas_call x1, Pallas kernels, on_device(): call(first_stats_kernel, stat_shape, (pairs,), [win] * 4 + [near, bias_sp...  3.56 us
  transfers between devices with their start and end apart: 16, of which 6 were waited for; matrix products, arithmetic and copies ran while one was open for 0% of the time, Pallas kernels for 16%

profile of v5, /device:TPU:1, one launch (start us, length us, event | category | flops | bytes accessed | tf_op | source)
XLA Modules:
  0.0 105.4 jit_solution(7914666789710028227)
XLA Ops:
  0.0 1.4 %shard_map.100 = (bf16[272,1024]{1,0:T(8,128)(2,1)S(1)}, bf16[272,1024]{1,0:T(8,128)(2,1)S(1)}) custom-call(s32[1]{0:T(128)} %bitcast.core_ref, s32[1]{0:T(128)} %bitcast.1.chip_ref, s32[1]{0:T(128)} %bitcast.2.head_ref, s32[2,14]{1,0:T(2,128)} %refs_0_.1, bf16[256,512]{1,0:T(8,128)(2,1)} %refs_1_.1, bf16[256,512]{1,0:T(8,128)(2,1)} %refs_2_.4, ...), custom_call_target="tpu_custom_call" | custom-call | tf_op jit(solution)/shard_map/pallas_call | solution.py:383
  1.4 3.3 %collective-permute-start = (bf16[272,1024]{1,0:T(8,128)(2,1)S(1)}, bf16[272,1024]{1,0:T(8,128)(2,1)S(1)}, u32[]{:S(2)}, u32[]{:S(2)}) collective-permute-start(bf16[272,1024]{1,0:T(8,128)(2,1)S(1)} %get-tuple-element.34), channel_id=1, source_target_pairs={{0,2},{2,0},{4,6},{6,4},{8,10},{10,8},{12,14},{14,12},{16,18},{18,... | collective-permute-start | bytes 1671176 | tf_op jit(solution)/shard_map/ppermute | solution.py:33
  4.7 1.6 %collective-permute-done.refs_1_ = bf16[272,1024]{1,0:T(8,128)(2,1)S(1)} collective-permute-done((bf16[272,1024]{1,0:T(8,128)(2,1)S(1)}, bf16[272,1024]{1,0:T(8,128)(2,1)S(1)}, u32[]{:S(2)}, u32[]{:S(2)}) %collective-permute-start) | collective-permute-done | bytes 557088 | tf_op jit(solution)/shard_map/ppermute | solution.py:33
  6.4 8.8 %collective-permute-start.3 = (bf16[2,256,256]{2,1,0:T(8,128)(2,1)S(1)}, bf16[2,256,256]{2,1,0:T(8,128)(2,1)S(1)}, u32[]{:S(2)}, u32[]{:S(2)}) collective-permute-start(bf16[2,256,256]{2,1,0:T(8,128)(2,1)S(1)} %get-tuple-element.35.refs_0_), channel_id=1, source_target_pairs={{0,252},{2,254},{4,8},{6,10},{8,4},{10,6},{12,16},{14,18},{16,12},... | collective-permute-start | bytes 786440 | tf_op jit(solution)/shard_map/ppermute | solution.py:39
  15.2 1.5 %collective-permute-start.6 = (bf16[2,256,256]{2,1,0:T(8,128)(2,1)S(1)}, bf16[2,256,256]{2,1,0:T(8,128)(2,1)S(1)}, u32[]{:S(2)}, u32[]{:S(2)}) collective-permute-start(bf16[2,256,256]{2,1,0:T(8,128)(2,1)S(1)} %get-tuple-element.35.refs_0_), channel_id=1, source_target_pairs={{0,4},{2,6},{4,0},{6,2},{8,12},{10,14},{12,8},{14,10},{16,20},{18,... | collective-permute-start | bytes 786440 | tf_op jit(solution)/shard_map/ppermute | solution.py:39
  16.8 4.8 %collective-permute-done.3.refs_0_ = bf16[2,256,256]{2,1,0:T(8,128)(2,1)S(1)} collective-permute-done((bf16[2,256,256]{2,1,0:T(8,128)(2,1)S(1)}, bf16[2,256,256]{2,1,0:T(8,128)(2,1)S(1)}, u32[]{:S(2)}, u32[]{:S(2)}) %collective-permute-start.3) | collective-permute-done | bytes 262176 | tf_op jit(solution)/shard_map/ppermute | solution.py:39
  21.6 0.8 collective-permute-done.1.refs_2_.refs_1_
  22.4 6.1 %collective-permute-start.2 = (bf16[2,256,256]{2,1,0:T(8,128)(2,1)S(1)}, bf16[2,256,256]{2,1,0:T(8,128)(2,1)S(1)}, u32[]{:S(2)}, u32[]{:S(2)}) collective-permute-start(bf16[2,256,256]{2,1,0:T(8,128)(2,1)S(1)} %collective-permute-done.1.refs_2_.refs_1_), channel_id=1, source_target_pairs={{0,252},{2,254},{4,8},{6,10},{8,4},{10,6},{12,16},{14,18},{16,12},... | collective-permute-start | bytes 786440 | tf_op jit(solution)/shard_map/ppermute | solution.py:39
  28.5 0.1 copy.11.owner_col_ref
  28.6 0.2 shard_map.104.place_ref
  28.8 3.6 %shard_map.102.refs_4_ = f32[2,4,8,256]{3,2,1,0:T(8,128)S(1)} custom-call(s32[1]{0:T(128)} %bitcast.core_ref, s32[1]{0:T(128)} %bitcast.1.chip_ref, s32[1]{0:T(128)} %bitcast.2.head_ref, bf16[2,256,256]{2,1,0:T(8,128)(2,1)S(1)} %get-tuple-element.35.refs_0_, bf16[2,256,256]{2,1,0:T(8,128)(2,1)S(1)} %get-tuple-element.36.refs_1_, ...), custom_call_target="tpu_custom_call" | custom-call | flops 536870912 | bytes 4194304 | tf_op jit(solution)/shard_map/pallas_call | solution.py:434
  32.4 2.1 %shard_map.103.refs_4_ = f32[2,4,8,256]{3,2,1,0:T(8,128)S(1)} custom-call(s32[1]{0:T(128)} %bitcast.core_ref, s32[1]{0:T(128)} %bitcast.1.chip_ref, s32[1]{0:T(128)} %bitcast.2.head_ref, bf16[2,256,256]{2,1,0:T(8,128)(2,1)S(1)} %collective-permute-done.3.refs_0_, bf16[2,256,256]{2,1,0:T(8,128)(2,1)S(1)} %collective-permute-done.5.refs_1_.refs_2_, ...), custom_call_target="tpu_custom_call" | custom-call | flops 268435456 | bytes 2097152 | tf_op jit(solution)/shard_map/pallas_call | solution.py:438
  34.5 2.0 %shard_map.105 = (f32[2,4,8,256]{3,2,1,0:T(8,128)S(1)}, bf16[2,256,256]{2,1,0:T(8,128)(2,1)S(1)}, bf16[2,256,256]{2,1,0:T(8,128)(2,1)S(1)}, bf16[2,2,256,512]{3,2,1,0:T(8,128)(2,1)S(1)}) custom-call(s32[1]{0:T(128)} %bitcast.core_ref, s32[1]{0:T(128)} %bitcast.1.chip_ref, s32[1]{0:T(128)} %bitcast.2.head_ref, ...), custom_call_target="tpu_custom_call" | custom-call | flops 268435456 | bytes 2097152 | tf_op jit(solution)/shard_map/pallas_call | solution.py:447
  36.6 5.8 %collective-permute-start.10 = (bf16[2,256,256]{2,1,0:T(8,128)(2,1)S(1)}, bf16[2,256,256]{2,1,0:T(8,128)(2,1)S(1)}, u32[]{:S(2)}, u32[]{:S(2)}) collective-permute-start(bf16[2,256,256]{2,1,0:T(8,128)(2,1)S(1)} %get-tuple-element.54), channel_id=1, source_target_pairs={{0,252},{2,254},{4,8},{6,10},{8,4},{10,6},{12,16},{14,18},{16,12},... | collective-permute-start | bytes 786440 | tf_op jit(solution)/shard_map/ppermute | solution.py:39
  42.3 5.8 %shard_map.106 = (bf16[2,256,256]{2,1,0:T(8,128)(2,1)S(1)}, bf16[2,256,256]{2,1,0:T(8,128)(2,1)S(1)}, bf16[2,256,256]{2,1,0:T(8,128)(2,1)S(1)}, bf16[2,256,256]{2,1,0:T(8,128)(2,1)S(1)}, f32[2,2,128,256]{3,2,1,0:T(8,128)S(1)}) custom-call(s32[1]{0:T(128)} %bitcast.core_ref, s32[1]{0:T(128)} %bitcast.1.chip_ref, s32[1]{0:T(128)} %bitcast.2.head_ref, ...), custom_call_target="tpu_custom_call" | custom-call | flops 1073741824 | bytes 4194304 | tf_op jit(solution)/shard_map/pallas_call | solution.py:455
  48.1 1.8 %collective-permute-start.12 = (bf16[2,256,256]{2,1,0:T(8,128)(2,1)S(1)}, bf16[2,256,256]{2,1,0:T(8,128)(2,1)S(1)}, u32[]{:S(2)}, u32[]{:S(2)}) collective-permute-start(bf16[2,256,256]{2,1,0:T(8,128)(2,1)S(1)} %get-tuple-element.55), channel_id=1, source_target_pairs={{0,252},{2,254},{4,8},{6,10},{8,4},{10,6},{12,16},{14,18},{16,12},... | collective-permute-start | bytes 786440 | tf_op jit(solution)/shard_map/ppermute | solution.py:39
  50.0 5.6 %collective-permute-start.9 = (bf16[2,256,256]{2,1,0:T(8,128)(2,1)S(1)}, bf16[2,256,256]{2,1,0:T(8,128)(2,1)S(1)}, u32[]{:S(2)}, u32[]{:S(2)}) collective-permute-start(bf16[2,256,256]{2,1,0:T(8,128)(2,1)S(1)} %add_convert_fusion.1), channel_id=1, source_target_pairs={{0,252},{2,254},{4,8},{6,10},{8,4},{10,6},{12,16},{14,18},{16,12},... | collective-permute-start | bytes 786440 | tf_op jit(solution)/shard_map/ppermute | solution.py:39
  55.8 3.6 %shard_map.107 = (f32[2,256,256]{2,1,0:T(8,128)S(1)}, f32[2,256,256]{2,1,0:T(8,128)S(1)}, bf16[256,256]{1,0:T(8,128)(2,1)S(1)}, bf16[256,256]{1,0:T(8,128)(2,1)S(1)}) custom-call(s32[1]{0:T(128)} %bitcast.core_ref, s32[1]{0:T(128)} %bitcast.1.chip_ref, s32[1]{0:T(128)} %bitcast.2.head_ref, bf16[2,256,256]{2,1,0:T(8,128)(2,1)S(1)} %get-tuple-element.35.refs_0_, ...), custom_call_target="tpu_custom_call" | custom-call | flops 536870912 | bytes 4194304 | tf_op jit(solution)/shard_map/pallas_call | solution.py:464
  59.4 3.8 %collective-permute-start.7 = (bf16[256,256]{1,0:T(8,128)(2,1)S(1)}, bf16[256,256]{1,0:T(8,128)(2,1)S(1)}, u32[]{:S(2)}, u32[]{:S(2)}) collective-permute-start(bf16[256,256]{1,0:T(8,128)(2,1)S(1)} %get-tuple-element.45), channel_id=1, source_target_pairs={{0,2},{2,0},{4,6},{6,4},{8,10},{10,8},{12,14},{14,12},{16,18},{18,... | collective-permute-start | bytes 393224 | tf_op jit(solution)/shard_map/ppermute | solution.py:33
  63.3 1.0 collective-permute-done.7.refs_1_
  64.2 0.5 shard_map.108
  64.8 0.2 shard_map.109
  65.0 3.7 %collective-permute-start.14 = (bf16[2,256,256]{2,1,0:T(8,128)(2,1)S(1)}, bf16[2,256,256]{2,1,0:T(8,128)(2,1)S(1)}, u32[]{:S(2)}, u32[]{:S(2)}) collective-permute-start(bf16[2,256,256]{2,1,0:T(8,128)(2,1)S(1)} %get-tuple-element.58), channel_id=1, source_target_pairs={{0,2},{2,0},{4,6},{6,4},{8,10},{10,8},{12,14},{14,12},{16,18},{18,... | collective-permute-start | bytes 786440 | tf_op jit(solution)/shard_map/ppermute | solution.py:33
  68.7 0.3 shard_map.111.refs_0_
  69.0 0.8 collective-permute-done.14.refs_2_.refs_1_
  69.9 0.3 shard_map.112
  70.2 0.4 collective-permute-start.15
  70.6 0.5 shard_map.110.own_ref
  71.1 6.7 %collective-permute-done.15.got_ref = bf16[256,512]{1,0:T(8,128)(2,1)S(1)} collective-permute-done((bf16[256,512]{1,0:T(8,128)(2,1)S(1)}, bf16[256,512]{1,0:T(8,128)(2,1)S(1)}, u32[]{:S(2)}, u32[]{:S(2)}) %collective-permute-start.15) | collective-permute-done | bytes 262176 | tf_op jit(solution)/shard_map/ppermute | solution.py:492
  77.7 0.3 shard_map.113
  78.2 26.3 %all_to_all.11 = bf16[128,4,512]{2,1,0:T(4,128)(2,1)S(1)} all-to-all(bf16[128,4,512]{2,1,0:T(4,128)(2,1)S(1)} %all_to_all.7), channel_id=1, replica_groups={{208,210,212,214,224,226,228,230,56,58,60,62,8,10,12,14,24,26,28,30,232..., dimensions={0} | all-to-all | bytes 1048576 | tf_op jit(solution)/shard_map/all_to_all | solution.py:503
  104.6 0.8 shard_map.114
  (31 shorter events, 0.8 us)
Async XLA Ops:
  1.4 4.9 %collective-permute-start = (bf16[272,1024]{1,0:T(8,128)(2,1)S(1)}, bf16[272,1024]{1,0:T(8,128)(2,1)S(1)}, u32[]{:S(2)}, u32[]{:S(2)}) collective-permute-start(bf16[272,1024]{1,0:T(8,128)(2,1)S(1)} %get-tuple-element.34), channel_id=1, source_target_pairs={{0,2},{2,0},{4,6},{6,4},{8,10},{10,8},{12,14},{14,12},{16,18},{18,... | collective-permute-start | bytes 1671176 | tf_op jit(solution)/shard_map/ppermute | solution.py:33
  6.3 22.3 %copy-start.3 = (s32[512,1]{1,0:T(8,128)S(1)}, s32[512,1]{1,0:T(8,128)}, u32[]{:S(2)}) copy-start(s32[512,1]{1,0:T(8,128)} %constant.12.clone.label_ref) | copy-start | bytes 6148
  6.4 22.1 %copy-start.4 = (s32[256,1]{0,1:T(1,128)S(1)}, s32[256,1]{0,1:T(1,128)}, u32[]{:S(2)}) copy-start(s32[256,1]{0,1:T(1,128)} %param.18) | copy-start | bytes 3076
  6.4 15.2 %collective-permute-start.3 = (bf16[2,256,256]{2,1,0:T(8,128)(2,1)S(1)}, bf16[2,256,256]{2,1,0:T(8,128)(2,1)S(1)}, u32[]{:S(2)}, u32[]{:S(2)}) collective-permute-start(bf16[2,256,256]{2,1,0:T(8,128)(2,1)S(1)} %get-tuple-element.35.refs_0_), channel_id=1, source_target_pairs={{0,252},{2,254},{4,8},{6,10},{8,4},{10,6},{12,16},{14,18},{16,12},... | collective-permute-start | bytes 786440 | tf_op jit(solution)/shard_map/ppermute | solution.py:39
  15.2 7.2 %collective-permute-start.1 = (bf16[2,256,256]{2,1,0:T(8,128)(2,1)S(1)}, bf16[2,256,256]{2,1,0:T(8,128)(2,1)S(1)}, u32[]{:S(2)}, u32[]{:S(2)}) collective-permute-start(bf16[2,256,256]{2,1,0:T(8,128)(2,1)S(1)} %get-tuple-element.36.refs_1_), channel_id=1, source_target_pairs={{0,4},{2,6},{4,0},{6,2},{8,12},{10,14},{12,8},{14,10},{16,20},{18,... | collective-permute-start | bytes 786440 | tf_op jit(solution)/shard_map/ppermute | solution.py:39
  15.2 13.6 %collective-permute-start.6 = (bf16[2,256,256]{2,1,0:T(8,128)(2,1)S(1)}, bf16[2,256,256]{2,1,0:T(8,128)(2,1)S(1)}, u32[]{:S(2)}, u32[]{:S(2)}) collective-permute-start(bf16[2,256,256]{2,1,0:T(8,128)(2,1)S(1)} %get-tuple-element.35.refs_0_), channel_id=1, source_target_pairs={{0,4},{2,6},{4,0},{6,2},{8,12},{10,14},{12,8},{14,10},{16,20},{18,... | collective-permute-start | bytes 786440 | tf_op jit(solution)/shard_map/ppermute | solution.py:39
  16.7 15.7 %collective-permute-start.5 = (bf16[2,256,256]{2,1,0:T(8,128)(2,1)S(1)}, bf16[2,256,256]{2,1,0:T(8,128)(2,1)S(1)}, u32[]{:S(2)}, u32[]{:S(2)}) collective-permute-start(bf16[2,256,256]{2,1,0:T(8,128)(2,1)S(1)} %get-tuple-element.36.refs_1_), channel_id=1, source_target_pairs={{0,252},{2,254},{4,8},{6,10},{8,4},{10,6},{12,16},{14,18},{16,12},... | collective-permute-start | bytes 786440 | tf_op jit(solution)/shard_map/ppermute | solution.py:39
  21.6 12.9 %collective-permute-start.4 = (bf16[2,256,256]{2,1,0:T(8,128)(2,1)S(1)}, bf16[2,256,256]{2,1,0:T(8,128)(2,1)S(1)}, u32[]{:S(2)}, u32[]{:S(2)}) collective-permute-start(bf16[2,256,256]{2,1,0:T(8,128)(2,1)S(1)} %collective-permute-done.3.refs_0_), channel_id=1, source_target_pairs={{0,4},{2,6},{4,0},{6,2},{8,12},{10,14},{12,8},{14,10},{16,20},{18,... | collective-permute-start | bytes 786440 | tf_op jit(solution)/shard_map/ppermute | solution.py:39
  22.4 12.1 %collective-permute-start.2 = (bf16[2,256,256]{2,1,0:T(8,128)(2,1)S(1)}, bf16[2,256,256]{2,1,0:T(8,128)(2,1)S(1)}, u32[]{:S(2)}, u32[]{:S(2)}) collective-permute-start(bf16[2,256,256]{2,1,0:T(8,128)(2,1)S(1)} %collective-permute-done.1.refs_2_.refs_1_), channel_id=1, source_target_pairs={{0,252},{2,254},{4,8},{6,10},{8,4},{10,6},{12,16},{14,18},{16,12},... | collective-permute-start | bytes 786440 | tf_op jit(solution)/shard_map/ppermute | solution.py:39
  36.5 13.5 %collective-permute-start.8 = (bf16[2,256,256]{2,1,0:T(8,128)(2,1)S(1)}, bf16[2,256,256]{2,1,0:T(8,128)(2,1)S(1)}, u32[]{:S(2)}, u32[]{:S(2)}) collective-permute-start(bf16[2,256,256]{2,1,0:T(8,128)(2,1)S(1)} %get-tuple-element.52), channel_id=1, source_target_pairs={{0,4},{2,6},{4,0},{6,2},{8,12},{10,14},{12,8},{14,10},{16,20},{18,... | collective-permute-start | bytes 786440 | tf_op jit(solution)/shard_map/ppermute | solution.py:39
  36.6 19.0 %collective-permute-start.10 = (bf16[2,256,256]{2,1,0:T(8,128)(2,1)S(1)}, bf16[2,256,256]{2,1,0:T(8,128)(2,1)S(1)}, u32[]{:S(2)}, u32[]{:S(2)}) collective-permute-start(bf16[2,256,256]{2,1,0:T(8,128)(2,1)S(1)} %get-tuple-element.54), channel_id=1, source_target_pairs={{0,252},{2,254},{4,8},{6,10},{8,4},{10,6},{12,16},{14,18},{16,12},... | collective-permute-start | bytes 786440 | tf_op jit(solution)/shard_map/ppermute | solution.py:39
  48.1 16.6 %collective-permute-start.12 = (bf16[2,256,256]{2,1,0:T(8,128)(2,1)S(1)}, bf16[2,256,256]{2,1,0:T(8,128)(2,1)S(1)}, u32[]{:S(2)}, u32[]{:S(2)}) collective-permute-start(bf16[2,256,256]{2,1,0:T(8,128)(2,1)S(1)} %get-tuple-element.55), channel_id=1, source_target_pairs={{0,252},{2,254},{4,8},{6,10},{8,4},{10,6},{12,16},{14,18},{16,12},... | collective-permute-start | bytes 786440 | tf_op jit(solution)/shard_map/ppermute | solution.py:39
  49.9 14.8 %collective-permute-start.13 = (bf16[2,256,256]{2,1,0:T(8,128)(2,1)S(1)}, bf16[2,256,256]{2,1,0:T(8,128)(2,1)S(1)}, u32[]{:S(2)}, u32[]{:S(2)}) collective-permute-start(bf16[2,256,256]{2,1,0:T(8,128)(2,1)S(1)} %get-tuple-element.56), channel_id=1, source_target_pairs={{0,4},{2,6},{4,0},{6,2},{8,12},{10,14},{12,8},{14,10},{16,20},{18,... | collective-permute-start | bytes 786440 | tf_op jit(solution)/shard_map/ppermute | solution.py:39
  50.0 14.7 %collective-permute-start.9 = (bf16[2,256,256]{2,1,0:T(8,128)(2,1)S(1)}, bf16[2,256,256]{2,1,0:T(8,128)(2,1)S(1)}, u32[]{:S(2)}, u32[]{:S(2)}) collective-permute-start(bf16[2,256,256]{2,1,0:T(8,128)(2,1)S(1)} %add_convert_fusion.1), channel_id=1, source_target_pairs={{0,252},{2,254},{4,8},{6,10},{8,4},{10,6},{12,16},{14,18},{16,12},... | collective-permute-start | bytes 786440 | tf_op jit(solution)/shard_map/ppermute | solution.py:39
  55.7 9.1 %collective-permute-start.11 = (bf16[2,256,256]{2,1,0:T(8,128)(2,1)S(1)}, bf16[2,256,256]{2,1,0:T(8,128)(2,1)S(1)}, u32[]{:S(2)}, u32[]{:S(2)}) collective-permute-start(bf16[2,256,256]{2,1,0:T(8,128)(2,1)S(1)} %add_convert_fusion), channel_id=1, source_target_pairs={{0,4},{2,6},{4,0},{6,2},{8,12},{10,14},{12,8},{14,10},{16,20},{18,... | collective-permute-start | bytes 786440 | tf_op jit(solution)/shard_map/ppermute | solution.py:39
  55.8 8.5 %copy-start.2 = (bf16[1024,512]{1,0:T(8,128)(2,1)S(1)}, bf16[1024,512]{1,0:T(8,128)(2,1)}, u32[]{:S(2)}) copy-start(bf16[1024,512]{1,0:T(8,128)(2,1)} %refs_2_.5) | copy-start | bytes 3145732
  59.4 4.8 %collective-permute-start.7 = (bf16[256,256]{1,0:T(8,128)(2,1)S(1)}, bf16[256,256]{1,0:T(8,128)(2,1)S(1)}, u32[]{:S(2)}, u32[]{:S(2)}) collective-permute-start(bf16[256,256]{1,0:T(8,128)(2,1)S(1)} %get-tuple-element.45), channel_id=1, source_target_pairs={{0,2},{2,0},{4,6},{6,4},{8,10},{10,8},{12,14},{14,12},{16,18},{18,... | collective-permute-start | bytes 393224 | tf_op jit(solution)/shard_map/ppermute | solution.py:33
  64.8 3.9 %copy-start = (bf16[1024,512]{1,0:T(8,128)(2,1)S(1)}, bf16[1024,512]{1,0:T(8,128)(2,1)}, u32[]{:S(2)}) copy-start(bf16[1024,512]{1,0:T(8,128)(2,1)} %refs_2_.7) | copy-start | bytes 3145732
  64.8 3.9 %copy-start.1 = (bf16[1024,512]{1,0:T(8,128)(2,1)S(1)}, bf16[1024,512]{1,0:T(8,128)(2,1)}, u32[]{:S(2)}) copy-start(bf16[1024,512]{1,0:T(8,128)(2,1)} %refs_3_.7) | copy-start | bytes 3145732
  65.0 4.9 %collective-permute-start.14 = (bf16[2,256,256]{2,1,0:T(8,128)(2,1)S(1)}, bf16[2,256,256]{2,1,0:T(8,128)(2,1)S(1)}, u32[]{:S(2)}, u32[]{:S(2)}) collective-permute-start(bf16[2,256,256]{2,1,0:T(8,128)(2,1)S(1)} %get-tuple-element.58), channel_id=1, source_target_pairs={{0,2},{2,0},{4,6},{6,4},{8,10},{10,8},{12,14},{14,12},{16,18},{18,... | collective-permute-start | bytes 786440 | tf_op jit(solution)/shard_map/ppermute | solution.py:33
  70.2 7.5 %collective-permute-start.15 = (bf16[256,512]{1,0:T(8,128)(2,1)S(1)}, bf16[256,512]{1,0:T(8,128)(2,1)S(1)}, u32[]{:S(2)}, u32[]{:S(2)}) collective-permute-start(bf16[256,512]{1,0:T(8,128)(2,1)S(1)} %shard_map.112), channel_id=1, source_target_pairs={{0,1},{1,0},{2,3},{3,2},{4,5},{5,4},{6,7},{7,6},{8,9},{9,8},{10,11... | collective-permute-start | bytes 786440 | tf_op jit(solution)/shard_map/ppermute | solution.py:492

commit v6 on v5

--- a/solution.py
+++ b/solution.py
@@ -55,44 +55,45 @@
     kernel((core_ref[0], chip_ref[0], head_ref[0]), *refs)
 
 
-def pack_kernel(ids, adj_in_ref, k_ref, v_ref, q_ref, g_ref, send_ref, own_ref, adj_ref, sems):
+def pack_kernel(ids, adj_in_ref, k_ref, v_ref, q_ref, g_ref, send_kv_ref, own_kv_ref, send_qg_ref, own_qg_ref, adj_ref, sems):
     rows, cols = k_ref.shape
     half = cols // 2
-    copies = [pltpu.make_async_copy(adj_in_ref, adj_ref, sems.at[0])]
-    for to_ref, which in ((send_ref, 1 - ids[0]), (own_ref, ids[0])):
+    copies = []
+    for kv_ref, qg_ref, which in ((send_kv_ref, send_qg_ref, 1 - ids[0]), (own_kv_ref, own_qg_ref, ids[0])):
         at = pl.ds(pl.multiple_of(which * half, half), half)
-        for n, from_ref in enumerate((k_ref, v_ref, q_ref, g_ref)):
-            copies.append(
-                pltpu.make_async_copy(
-                    from_ref.at[:, at], to_ref.at[0:rows, n * half : (n + 1) * half], sems.at[len(copies)]
-                )
-            )
+        for n, from_ref in enumerate((k_ref, v_ref)):
+            copies.append(pltpu.make_async_copy(from_ref.at[:, at], kv_ref.at[n], sems.at[len(copies)]))
+        for n, from_ref in enumerate((q_ref, g_ref)):
+            to = qg_ref.at[0:rows, n * half : (n + 1) * half]
+            copies.append(pltpu.make_async_copy(from_ref.at[:, at], to, sems.at[len(copies)]))
+    adjacency = pltpu.make_async_copy(adj_in_ref, adj_ref, sems.at[len(copies)])
+    adjacency.start()
     for copy in copies:
         copy.start()
-    copies[0].wait()
+    adjacency.wait()
     bias = bias_rows(adj_ref).astype(BF)
-    for to_ref in (send_ref, own_ref):
+    for to_ref in (send_qg_ref, own_qg_ref):
         to_ref[rows : rows + 16, 0:half] = bias
-        to_ref[rows : rows + 16, half:] = jnp.zeros((16, 3 * half), BF)
-    for copy in copies[1:]:
+        to_ref[rows : rows + 16, half:] = jnp.zeros((16, half), BF)
+    for copy in copies:
         copy.wait()
 
 
-def order_kernel(ids, own_ref, got_ref, a_ref, b_ref, qg_ref, bias_ref):
-    rows = a_ref.shape[1]
-    cols = a_ref.shape[2]
-    par = ids[0]
+def order_keys_kernel(ids, own_ref, got_ref, a_ref, b_ref):
+    b_own = ids[0] == ids[1]
+    own = own_ref[...]
+    got = got_ref[...]
+    a_ref[...] = jnp.where(b_own, got, own)
+    b_ref[...] = jnp.where(b_own, own, got)
+
+
+def order_queries_kernel(ids, own_ref, got_ref, qg_ref, bias_ref):
+    rows, cols = qg_ref.shape[2:]
     scale = 1.0 / math.sqrt(HD)
-    for sector, from_ref in ((par, own_ref), (1 - par, got_ref)):
-        qg_ref[0, sector] = from_ref[0:rows, 2 * cols : 3 * cols] * scale
-        qg_ref[1, sector] = from_ref[0:rows, 3 * cols : 4 * cols]
+    for sector, from_ref in ((ids[0], own_ref), (1 - ids[0], got_ref)):
+        qg_ref[0, sector] = from_ref[0:rows, 0:cols] * scale
+        qg_ref[1, sector] = from_ref[0:rows, cols : 2 * cols]
         bias_ref[sector] = from_ref[rows : rows + 16, 0:cols].astype(F32)
-    b_own = par == ids[1]
-    for which in range(2):
-        own = own_ref[0:rows, which * cols : (which + 1) * cols]
-        got = got_ref[0:rows, which * cols : (which + 1) * cols]
-        a_ref[which] = jnp.where(b_own, got, own)
-        b_ref[which] = jnp.where(b_own, own, got)
 
 
 def one_head(pair_ref, h):
@@ -379,21 +380,25 @@
     def whole(*shape):
         return pl.BlockSpec(shape, lambda i, *p: (0,) * len(shape))
 
-    packed = sds((rows + 16, 4 * half), BF)
-    send, own = call(
-        pack_kernel, (packed, packed), (1,), [hbm] * 5, (whole(rows + 16, 4 * half),) * 2,
+    kv_shape = sds((2, rows, half), BF)
+    kv_whole = whole(2, rows, half)
+    qg_packed = sds((rows + 16, 2 * half), BF)
+    packed_whole = whole(rows + 16, 2 * half)
+    send_kv, own_kv, send_qg, own_qg = call(
+        pack_kernel, (kv_shape, kv_shape, qg_packed, qg_packed), (1,), [hbm] * 5,
+        (kv_whole, kv_whole, packed_whole, packed_whole),
         scratch=(pltpu.SMEM(adjacency.shape, jnp.int32), pltpu.SemaphoreType.DMA((9,))),
     )(*ids, *[pltpu.with_memory_space_constraint(x, pltpu.HBM) for x in (adjacency, key, value, query, out_grad)])
-    got = core_swapped(send)
-    kv_shape = sds((2, rows, half), BF)
-    kv_whole = whole(2, rows, half)
-    a, b, qg, bias = call(
-        order_kernel,
-        (kv_shape, kv_shape, sds((2, 2, rows, half), BF), sds((2, 16, rows), F32)),
-        (1,),
-        [whole(rows + 16, 4 * half)] * 2,
-        (kv_whole, kv_whole, whole(2, 2, rows, half), whole(2, 16, rows)),
-    )(*ids, own, got)
+    got_kv = core_swapped(send_kv)
+    a, b = call(order_keys_kernel, (kv_shape, kv_shape), (1,), [kv_whole] * 2, (kv_whole, kv_whole))(
+        *ids, own_kv, got_kv
+    )
+    send_qg, a, b = lax.optimization_barrier((send_qg, a, b))
+    got_qg = core_swapped(send_qg)
+    qg, bias = call(
+        order_queries_kernel, (sds((2, 2, rows, half), BF), sds((2, 16, rows), F32)), (1,),
+        [packed_whole] * 2, (whole(2, 2, rows, half), whole(2, 16, rows)),
+    )(*ids, own_qg, got_qg)
     ea = chip_swapped(a, 0)
     oa = chip_swapped(b, 1)
     eb = chip_swapped(b, 0)

time: 106 us -> 105 us (level)
    ppermute x3 -> x4, starting transfers between devices: 10.9 us -> 11.5 us  [core_swapped(): return lax.ppermute(value, 'blk', [(s, s ^ 1) for s in range(count)])]
    ppermute x3 -> x4, waiting for transfers between devices: 3.39 us -> 2.97 us  [core_swapped(): return lax.ppermute(value, 'blk', [(s, s ^ 1) for s in range(count)])]
  transfers between devices with their start and end apart: 16 -> 17, of which waited for: 6 -> 7; matrix products, arithmetic and copies ran while one was open for 0% -> 0% of each run, Pallas kernels for 16% -> 16%
where the time goes in v6:
time: 105 us
  starting transfers between devices  41.4 us (39%)
  blocking collectives  26.3 us (25%)
  Pallas kernels  21.6 us (21%)
  waiting for transfers between devices  14.8 us (14%)
    ppermute x12, starting transfers between devices, chip_swapped(): lax.ppermute(value, 'blk', [(s, (s + ahead[s]) % count) for s in range(co...  29.5 us
    all_to_all x1, blocking collectives, on_device(): lax.all_to_all(outgoing, 'blk', split_axis=0, concat_axis=0, tiled=True,...  26.3 us
    ppermute x4, starting transfers between devices, core_swapped(): return lax.ppermute(value, 'blk', [(s, s ^ 1) for s in range(count)])  11.5 us
    ppermute x1, waiting for transfers between devices, on_device(): partial_got = lax.ppermute(partial_other, 'head', [(0, 1), (1, 0)])  6.65 us
    pallas_call x1, Pallas kernels, on_device(): call(near_kernel, (kv_shape,) * 4 + (part_shape,), (pairs,), [win] * 4 +...  5.8 us
    ppermute x12, waiting for transfers between devices, chip_swapped(): lax.ppermute(value, 'blk', [(s, (s + ahead[s]) % count) for s in range(co...  5.21 us
    pallas_call x1, Pallas kernels, on_device(): call(local_kernel, (own_shape, own_shape, sds((rows, half), BF), sds((row...  3.63 us
    pallas_call x1, Pallas kernels, on_device(): call(first_stats_kernel, stat_shape, (pairs,), [win] * 4 + [near, bias_sp...  3.54 us
  transfers between devices with their start and end apart: 17, of which 7 were waited for; matrix products, arithmetic and copies ran while one was open for 0% of the time, Pallas kernels for 16%

profile of v6, /device:TPU:1, one launch (start us, length us, event | category | flops | bytes accessed | tf_op | source)
XLA Modules:
  0.0 105.0 jit_solution(14511270245671480723)
XLA Ops:
  0.0 1.4 %shard_map.100 = (bf16[2,256,256]{2,1,0:T(8,128)(2,1)S(1)}, bf16[2,256,256]{2,1,0:T(8,128)(2,1)S(1)}, bf16[272,512]{1,0:T(8,128)(2,1)S(1)}, bf16[272,512]{1,0:T(8,128)(2,1)S(1)}) custom-call(s32[1]{0:T(128)} %bitcast.core_ref, s32[1]{0:T(128)} %bitcast.1.chip_ref, s32[1]{0:T(128)} %bitcast.2.head_ref, s32[2,14]{1,0:T(2,128)} %refs_0_.1, ...), custom_call_target="tpu_custom_call" | custom-call | tf_op jit(solution)/shard_map/pallas_call | solution.py:387
  1.4 3.3 %collective-permute-start = (bf16[2,256,256]{2,1,0:T(8,128)(2,1)S(1)}, bf16[2,256,256]{2,1,0:T(8,128)(2,1)S(1)}, u32[]{:S(2)}, u32[]{:S(2)}) collective-permute-start(bf16[2,256,256]{2,1,0:T(8,128)(2,1)S(1)} %get-tuple-element.40), channel_id=1, source_target_pairs={{0,2},{2,0},{4,6},{6,4},{8,10},{10,8},{12,14},{14,12},{16,18},{18,... | collective-permute-start | bytes 786440 | tf_op jit(solution)/shard_map/ppermute | solution.py:33
  4.7 1.2 %collective-permute-done.refs_1_ = bf16[2,256,256]{2,1,0:T(8,128)(2,1)S(1)} collective-permute-done((bf16[2,256,256]{2,1,0:T(8,128)(2,1)S(1)}, bf16[2,256,256]{2,1,0:T(8,128)(2,1)S(1)}, u32[]{:S(2)}, u32[]{:S(2)}) %collective-permute-start) | collective-permute-done | bytes 262176 | tf_op jit(solution)/shard_map/ppermute | solution.py:33
  5.9 8.8 %collective-permute-start.3 = (bf16[2,256,256]{2,1,0:T(8,128)(2,1)S(1)}, bf16[2,256,256]{2,1,0:T(8,128)(2,1)S(1)}, u32[]{:S(2)}, u32[]{:S(2)}) collective-permute-start(bf16[2,256,256]{2,1,0:T(8,128)(2,1)S(1)} %get-tuple-element.43.refs_0_), channel_id=1, source_target_pairs={{0,252},{2,254},{4,8},{6,10},{8,4},{10,6},{12,16},{14,18},{16,12},... | collective-permute-start | bytes 786440 | tf_op jit(solution)/shard_map/ppermute | solution.py:39
  14.8 0.7 collective-permute-start.5
  15.4 1.8 %collective-permute-start.7 = (bf16[2,256,256]{2,1,0:T(8,128)(2,1)S(1)}, bf16[2,256,256]{2,1,0:T(8,128)(2,1)S(1)}, u32[]{:S(2)}, u32[]{:S(2)}) collective-permute-start(bf16[2,256,256]{2,1,0:T(8,128)(2,1)S(1)} %get-tuple-element.43.refs_0_), channel_id=1, source_target_pairs={{0,4},{2,6},{4,0},{6,2},{8,12},{10,14},{12,8},{14,10},{16,20},{18,... | collective-permute-start | bytes 786440 | tf_op jit(solution)/shard_map/ppermute | solution.py:39
  17.2 3.9 %collective-permute-done.3.refs_0_ = bf16[2,256,256]{2,1,0:T(8,128)(2,1)S(1)} collective-permute-done((bf16[2,256,256]{2,1,0:T(8,128)(2,1)S(1)}, bf16[2,256,256]{2,1,0:T(8,128)(2,1)S(1)}, u32[]{:S(2)}, u32[]{:S(2)}) %collective-permute-start.3) | collective-permute-done | bytes 262176 | tf_op jit(solution)/shard_map/ppermute | solution.py:39
  21.1 0.8 collective-permute-done.1.refs_2_.refs_1_
  21.9 6.1 %collective-permute-start.2 = (bf16[2,256,256]{2,1,0:T(8,128)(2,1)S(1)}, bf16[2,256,256]{2,1,0:T(8,128)(2,1)S(1)}, u32[]{:S(2)}, u32[]{:S(2)}) collective-permute-start(bf16[2,256,256]{2,1,0:T(8,128)(2,1)S(1)} %collective-permute-done.1.refs_2_.refs_1_), channel_id=1, source_target_pairs={{0,252},{2,254},{4,8},{6,10},{8,4},{10,6},{12,16},{14,18},{16,12},... | collective-permute-start | bytes 786440 | tf_op jit(solution)/shard_map/ppermute | solution.py:39
  28.4 3.5 %shard_map.103.refs_4_ = f32[2,4,8,256]{3,2,1,0:T(8,128)S(1)} custom-call(s32[1]{0:T(128)} %bitcast.core_ref, s32[1]{0:T(128)} %bitcast.1.chip_ref, s32[1]{0:T(128)} %bitcast.2.head_ref, bf16[2,256,256]{2,1,0:T(8,128)(2,1)S(1)} %get-tuple-element.43.refs_0_, bf16[2,256,256]{2,1,0:T(8,128)(2,1)S(1)} %get-tuple-element.44.refs_1_, ...), custom_call_target="tpu_custom_call" | custom-call | flops 536870912 | bytes 4194304 | tf_op jit(solution)/shard_map/pallas_call | solution.py:439
  32.0 2.1 %shard_map.104.refs_4_ = f32[2,4,8,256]{3,2,1,0:T(8,128)S(1)} custom-call(s32[1]{0:T(128)} %bitcast.core_ref, s32[1]{0:T(128)} %bitcast.1.chip_ref, s32[1]{0:T(128)} %bitcast.2.head_ref, bf16[2,256,256]{2,1,0:T(8,128)(2,1)S(1)} %collective-permute-done.3.refs_0_, bf16[2,256,256]{2,1,0:T(8,128)(2,1)S(1)} %collective-permute-done.6.refs_1_.refs_2_, ...), custom_call_target="tpu_custom_call" | custom-call | flops 268435456 | bytes 2097152 | tf_op jit(solution)/shard_map/pallas_call | solution.py:443
  34.1 0.4 collective-permute-done.2.refs_0_.refs_2_
  34.5 2.0 %shard_map.106 = (f32[2,4,8,256]{3,2,1,0:T(8,128)S(1)}, bf16[2,256,256]{2,1,0:T(8,128)(2,1)S(1)}, bf16[2,256,256]{2,1,0:T(8,128)(2,1)S(1)}, bf16[2,2,256,512]{3,2,1,0:T(8,128)(2,1)S(1)}) custom-call(s32[1]{0:T(128)} %bitcast.core_ref, s32[1]{0:T(128)} %bitcast.1.chip_ref, s32[1]{0:T(128)} %bitcast.2.head_ref, ...), custom_call_target="tpu_custom_call" | custom-call | flops 268435456 | bytes 2097152 | tf_op jit(solution)/shard_map/pallas_call | solution.py:452
  36.6 5.3 %collective-permute-start.11 = (bf16[2,256,256]{2,1,0:T(8,128)(2,1)S(1)}, bf16[2,256,256]{2,1,0:T(8,128)(2,1)S(1)}, u32[]{:S(2)}, u32[]{:S(2)}) collective-permute-start(bf16[2,256,256]{2,1,0:T(8,128)(2,1)S(1)} %get-tuple-element.64), channel_id=1, source_target_pairs={{0,252},{2,254},{4,8},{6,10},{8,4},{10,6},{12,16},{14,18},{16,12},... | collective-permute-start | bytes 786440 | tf_op jit(solution)/shard_map/ppermute | solution.py:39
  41.9 5.8 %shard_map.107 = (bf16[2,256,256]{2,1,0:T(8,128)(2,1)S(1)}, bf16[2,256,256]{2,1,0:T(8,128)(2,1)S(1)}, bf16[2,256,256]{2,1,0:T(8,128)(2,1)S(1)}, bf16[2,256,256]{2,1,0:T(8,128)(2,1)S(1)}, f32[2,2,128,256]{3,2,1,0:T(8,128)S(1)}) custom-call(s32[1]{0:T(128)} %bitcast.core_ref, s32[1]{0:T(128)} %bitcast.1.chip_ref, s32[1]{0:T(128)} %bitcast.2.head_ref, ...), custom_call_target="tpu_custom_call" | custom-call | flops 1073741824 | bytes 4194304 | tf_op jit(solution)/shard_map/pallas_call | solution.py:460
  47.7 2.3 %collective-permute-start.13 = (bf16[2,256,256]{2,1,0:T(8,128)(2,1)S(1)}, bf16[2,256,256]{2,1,0:T(8,128)(2,1)S(1)}, u32[]{:S(2)}, u32[]{:S(2)}) collective-permute-start(bf16[2,256,256]{2,1,0:T(8,128)(2,1)S(1)} %get-tuple-element.65), channel_id=1, source_target_pairs={{0,252},{2,254},{4,8},{6,10},{8,4},{10,6},{12,16},{14,18},{16,12},... | collective-permute-start | bytes 786440 | tf_op jit(solution)/shard_map/ppermute | solution.py:39
  50.0 5.1 %collective-permute-start.10 = (bf16[2,256,256]{2,1,0:T(8,128)(2,1)S(1)}, bf16[2,256,256]{2,1,0:T(8,128)(2,1)S(1)}, u32[]{:S(2)}, u32[]{:S(2)}) collective-permute-start(bf16[2,256,256]{2,1,0:T(8,128)(2,1)S(1)} %add_convert_fusion.1), channel_id=1, source_target_pairs={{0,252},{2,254},{4,8},{6,10},{8,4},{10,6},{12,16},{14,18},{16,12},... | collective-permute-start | bytes 786440 | tf_op jit(solution)/shard_map/ppermute | solution.py:39
  55.3 3.6 %shard_map.108 = (f32[2,256,256]{2,1,0:T(8,128)S(1)}, f32[2,256,256]{2,1,0:T(8,128)S(1)}, bf16[256,256]{1,0:T(8,128)(2,1)S(1)}, bf16[256,256]{1,0:T(8,128)(2,1)S(1)}) custom-call(s32[1]{0:T(128)} %bitcast.core_ref, s32[1]{0:T(128)} %bitcast.1.chip_ref, s32[1]{0:T(128)} %bitcast.2.head_ref, bf16[2,256,256]{2,1,0:T(8,128)(2,1)S(1)} %get-tuple-element.43.refs_0_, ...), custom_call_target="tpu_custom_call" | custom-call | flops 536870912 | bytes 4194304 | tf_op jit(solution)/shard_map/pallas_call | solution.py:469
  59.0 3.8 %collective-permute-start.8 = (bf16[256,256]{1,0:T(8,128)(2,1)S(1)}, bf16[256,256]{1,0:T(8,128)(2,1)S(1)}, u32[]{:S(2)}, u32[]{:S(2)}) collective-permute-start(bf16[256,256]{1,0:T(8,128)(2,1)S(1)} %get-tuple-element.55), channel_id=1, source_target_pairs={{0,2},{2,0},{4,6},{6,4},{8,10},{10,8},{12,14},{14,12},{16,18},{18,... | collective-permute-start | bytes 393224 | tf_op jit(solution)/shard_map/ppermute | solution.py:33
  62.8 1.0 collective-permute-done.8.refs_1_
  63.8 0.5 shard_map.109
  64.3 0.2 shard_map.110
  64.5 3.7 %collective-permute-start.15 = (bf16[2,256,256]{2,1,0:T(8,128)(2,1)S(1)}, bf16[2,256,256]{2,1,0:T(8,128)(2,1)S(1)}, u32[]{:S(2)}, u32[]{:S(2)}) collective-permute-start(bf16[2,256,256]{2,1,0:T(8,128)(2,1)S(1)} %get-tuple-element.68), channel_id=1, source_target_pairs={{0,2},{2,0},{4,6},{6,4},{8,10},{10,8},{12,14},{14,12},{16,18},{18,... | collective-permute-start | bytes 786440 | tf_op jit(solution)/shard_map/ppermute | solution.py:33
  68.2 0.3 shard_map.112.refs_0_
  68.6 0.8 collective-permute-done.15.refs_2_.refs_1_
  69.4 0.3 shard_map.113
  69.7 0.4 collective-permute-start.16
  70.1 0.5 shard_map.111.own_ref
  70.6 6.6 %collective-permute-done.16.got_ref = bf16[256,512]{1,0:T(8,128)(2,1)S(1)} collective-permute-done((bf16[256,512]{1,0:T(8,128)(2,1)S(1)}, bf16[256,512]{1,0:T(8,128)(2,1)S(1)}, u32[]{:S(2)}, u32[]{:S(2)}) %collective-permute-start.16) | collective-permute-done | bytes 262176 | tf_op jit(solution)/shard_map/ppermute | solution.py:497
  77.3 0.3 shard_map.114
  77.7 26.3 %all_to_all.11 = bf16[128,4,512]{2,1,0:T(4,128)(2,1)S(1)} all-to-all(bf16[128,4,512]{2,1,0:T(4,128)(2,1)S(1)} %all_to_all.7), channel_id=1, replica_groups={{208,210,212,214,224,226,228,230,56,58,60,62,8,10,12,14,24,26,28,30,232..., dimensions={0} | all-to-all | bytes 1048576 | tf_op jit(solution)/shard_map/all_to_all | solution.py:508
  104.2 0.8 shard_map.115
  (34 shorter events, 1.0 us)
Async XLA Ops:
  1.4 4.5 %collective-permute-start = (bf16[2,256,256]{2,1,0:T(8,128)(2,1)S(1)}, bf16[2,256,256]{2,1,0:T(8,128)(2,1)S(1)}, u32[]{:S(2)}, u32[]{:S(2)}) collective-permute-start(bf16[2,256,256]{2,1,0:T(8,128)(2,1)S(1)} %get-tuple-element.40), channel_id=1, source_target_pairs={{0,2},{2,0},{4,6},{6,4},{8,10},{10,8},{12,14},{14,12},{16,18},{18,... | collective-permute-start | bytes 786440 | tf_op jit(solution)/shard_map/ppermute | solution.py:33
  5.9 22.3 %copy-start.3 = (s32[512,1]{1,0:T(8,128)S(1)}, s32[512,1]{1,0:T(8,128)}, u32[]{:S(2)}) copy-start(s32[512,1]{1,0:T(8,128)} %constant.12.clone.label_ref) | copy-start | bytes 6148
  5.9 22.1 %copy-start.4 = (s32[256,1]{0,1:T(1,128)S(1)}, s32[256,1]{0,1:T(1,128)}, u32[]{:S(2)}) copy-start(s32[256,1]{0,1:T(1,128)} %param.18) | copy-start | bytes 3076
  5.9 15.2 %collective-permute-start.3 = (bf16[2,256,256]{2,1,0:T(8,128)(2,1)S(1)}, bf16[2,256,256]{2,1,0:T(8,128)(2,1)S(1)}, u32[]{:S(2)}, u32[]{:S(2)}) collective-permute-start(bf16[2,256,256]{2,1,0:T(8,128)(2,1)S(1)} %get-tuple-element.43.refs_0_), channel_id=1, source_target_pairs={{0,252},{2,254},{4,8},{6,10},{8,4},{10,6},{12,16},{14,18},{16,12},... | collective-permute-start | bytes 786440 | tf_op jit(solution)/shard_map/ppermute | solution.py:39
  14.7 7.2 %collective-permute-start.1 = (bf16[2,256,256]{2,1,0:T(8,128)(2,1)S(1)}, bf16[2,256,256]{2,1,0:T(8,128)(2,1)S(1)}, u32[]{:S(2)}, u32[]{:S(2)}) collective-permute-start(bf16[2,256,256]{2,1,0:T(8,128)(2,1)S(1)} %get-tuple-element.44.refs_1_), channel_id=1, source_target_pairs={{0,4},{2,6},{4,0},{6,2},{8,12},{10,14},{12,8},{14,10},{16,20},{18,... | collective-permute-start | bytes 786440 | tf_op jit(solution)/shard_map/ppermute | solution.py:39
  14.8 13.6 %collective-permute-start.5 = (bf16[272,512]{1,0:T(8,128)(2,1)S(1)}, bf16[272,512]{1,0:T(8,128)(2,1)S(1)}, u32[]{:S(2)}, u32[]{:S(2)}) collective-permute-start(bf16[272,512]{1,0:T(8,128)(2,1)S(1)} %get-tuple-element.46), channel_id=1, source_target_pairs={{0,2},{2,0},{4,6},{6,4},{8,10},{10,8},{12,14},{14,12},{16,18},{18,... | collective-permute-start | bytes 835592 | tf_op jit(solution)/shard_map/ppermute | solution.py:33
  15.4 13.0 %collective-permute-start.7 = (bf16[2,256,256]{2,1,0:T(8,128)(2,1)S(1)}, bf16[2,256,256]{2,1,0:T(8,128)(2,1)S(1)}, u32[]{:S(2)}, u32[]{:S(2)}) collective-permute-start(bf16[2,256,256]{2,1,0:T(8,128)(2,1)S(1)} %get-tuple-element.43.refs_0_), channel_id=1, source_target_pairs={{0,4},{2,6},{4,0},{6,2},{8,12},{10,14},{12,8},{14,10},{16,20},{18,... | collective-permute-start | bytes 786440 | tf_op jit(solution)/shard_map/ppermute | solution.py:39
  17.2 14.8 %collective-permute-start.6 = (bf16[2,256,256]{2,1,0:T(8,128)(2,1)S(1)}, bf16[2,256,256]{2,1,0:T(8,128)(2,1)S(1)}, u32[]{:S(2)}, u32[]{:S(2)}) collective-permute-start(bf16[2,256,256]{2,1,0:T(8,128)(2,1)S(1)} %get-tuple-element.44.refs_1_), channel_id=1, source_target_pairs={{0,252},{2,254},{4,8},{6,10},{8,4},{10,6},{12,16},{14,18},{16,12},... | collective-permute-start | bytes 786440 | tf_op jit(solution)/shard_map/ppermute | solution.py:39
  21.1 13.0 %collective-permute-start.4 = (bf16[2,256,256]{2,1,0:T(8,128)(2,1)S(1)}, bf16[2,256,256]{2,1,0:T(8,128)(2,1)S(1)}, u32[]{:S(2)}, u32[]{:S(2)}) collective-permute-start(bf16[2,256,256]{2,1,0:T(8,128)(2,1)S(1)} %collective-permute-done.3.refs_0_), channel_id=1, source_target_pairs={{0,4},{2,6},{4,0},{6,2},{8,12},{10,14},{12,8},{14,10},{16,20},{18,... | collective-permute-start | bytes 786440 | tf_op jit(solution)/shard_map/ppermute | solution.py:39
  21.9 12.6 %collective-permute-start.2 = (bf16[2,256,256]{2,1,0:T(8,128)(2,1)S(1)}, bf16[2,256,256]{2,1,0:T(8,128)(2,1)S(1)}, u32[]{:S(2)}, u32[]{:S(2)}) collective-permute-start(bf16[2,256,256]{2,1,0:T(8,128)(2,1)S(1)} %collective-permute-done.1.refs_2_.refs_1_), channel_id=1, source_target_pairs={{0,252},{2,254},{4,8},{6,10},{8,4},{10,6},{12,16},{14,18},{16,12},... | collective-permute-start | bytes 786440 | tf_op jit(solution)/shard_map/ppermute | solution.py:39
  36.5 13.5 %collective-permute-start.9 = (bf16[2,256,256]{2,1,0:T(8,128)(2,1)S(1)}, bf16[2,256,256]{2,1,0:T(8,128)(2,1)S(1)}, u32[]{:S(2)}, u32[]{:S(2)}) collective-permute-start(bf16[2,256,256]{2,1,0:T(8,128)(2,1)S(1)} %get-tuple-element.62), channel_id=1, source_target_pairs={{0,4},{2,6},{4,0},{6,2},{8,12},{10,14},{12,8},{14,10},{16,20},{18,... | collective-permute-start | bytes 786440 | tf_op jit(solution)/shard_map/ppermute | solution.py:39
  36.6 18.5 %collective-permute-start.11 = (bf16[2,256,256]{2,1,0:T(8,128)(2,1)S(1)}, bf16[2,256,256]{2,1,0:T(8,128)(2,1)S(1)}, u32[]{:S(2)}, u32[]{:S(2)}) collective-permute-start(bf16[2,256,256]{2,1,0:T(8,128)(2,1)S(1)} %get-tuple-element.64), channel_id=1, source_target_pairs={{0,252},{2,254},{4,8},{6,10},{8,4},{10,6},{12,16},{14,18},{16,12},... | collective-permute-start | bytes 786440 | tf_op jit(solution)/shard_map/ppermute | solution.py:39
  47.7 16.6 %collective-permute-start.13 = (bf16[2,256,256]{2,1,0:T(8,128)(2,1)S(1)}, bf16[2,256,256]{2,1,0:T(8,128)(2,1)S(1)}, u32[]{:S(2)}, u32[]{:S(2)}) collective-permute-start(bf16[2,256,256]{2,1,0:T(8,128)(2,1)S(1)} %get-tuple-element.65), channel_id=1, source_target_pairs={{0,252},{2,254},{4,8},{6,10},{8,4},{10,6},{12,16},{14,18},{16,12},... | collective-permute-start | bytes 786440 | tf_op jit(solution)/shard_map/ppermute | solution.py:39
  50.0 14.3 %collective-permute-start.14 = (bf16[2,256,256]{2,1,0:T(8,128)(2,1)S(1)}, bf16[2,256,256]{2,1,0:T(8,128)(2,1)S(1)}, u32[]{:S(2)}, u32[]{:S(2)}) collective-permute-start(bf16[2,256,256]{2,1,0:T(8,128)(2,1)S(1)} %get-tuple-element.66), channel_id=1, source_target_pairs={{0,4},{2,6},{4,0},{6,2},{8,12},{10,14},{12,8},{14,10},{16,20},{18,... | collective-permute-start | bytes 786440 | tf_op jit(solution)/shard_map/ppermute | solution.py:39
  50.0 14.2 %collective-permute-start.10 = (bf16[2,256,256]{2,1,0:T(8,128)(2,1)S(1)}, bf16[2,256,256]{2,1,0:T(8,128)(2,1)S(1)}, u32[]{:S(2)}, u32[]{:S(2)}) collective-permute-start(bf16[2,256,256]{2,1,0:T(8,128)(2,1)S(1)} %add_convert_fusion.1), channel_id=1, source_target_pairs={{0,252},{2,254},{4,8},{6,10},{8,4},{10,6},{12,16},{14,18},{16,12},... | collective-permute-start | bytes 786440 | tf_op jit(solution)/shard_map/ppermute | solution.py:39
  55.2 9.1 %collective-permute-start.12 = (bf16[2,256,256]{2,1,0:T(8,128)(2,1)S(1)}, bf16[2,256,256]{2,1,0:T(8,128)(2,1)S(1)}, u32[]{:S(2)}, u32[]{:S(2)}) collective-permute-start(bf16[2,256,256]{2,1,0:T(8,128)(2,1)S(1)} %add_convert_fusion), channel_id=1, source_target_pairs={{0,4},{2,6},{4,0},{6,2},{8,12},{10,14},{12,8},{14,10},{16,20},{18,... | collective-permute-start | bytes 786440 | tf_op jit(solution)/shard_map/ppermute | solution.py:39
  55.3 8.5 %copy-start.2 = (bf16[1024,512]{1,0:T(8,128)(2,1)S(1)}, bf16[1024,512]{1,0:T(8,128)(2,1)}, u32[]{:S(2)}) copy-start(bf16[1024,512]{1,0:T(8,128)(2,1)} %refs_2_.5) | copy-start | bytes 3145732
  59.0 4.8 %collective-permute-start.8 = (bf16[256,256]{1,0:T(8,128)(2,1)S(1)}, bf16[256,256]{1,0:T(8,128)(2,1)S(1)}, u32[]{:S(2)}, u32[]{:S(2)}) collective-permute-start(bf16[256,256]{1,0:T(8,128)(2,1)S(1)} %get-tuple-element.55), channel_id=1, source_target_pairs={{0,2},{2,0},{4,6},{6,4},{8,10},{10,8},{12,14},{14,12},{16,18},{18,... | collective-permute-start | bytes 393224 | tf_op jit(solution)/shard_map/ppermute | solution.py:33
  64.3 3.9 %copy-start = (bf16[1024,512]{1,0:T(8,128)(2,1)S(1)}, bf16[1024,512]{1,0:T(8,128)(2,1)}, u32[]{:S(2)}) copy-start(bf16[1024,512]{1,0:T(8,128)(2,1)} %refs_2_.7) | copy-start | bytes 3145732
  64.3 3.9 %copy-start.1 = (bf16[1024,512]{1,0:T(8,128)(2,1)S(1)}, bf16[1024,512]{1,0:T(8,128)(2,1)}, u32[]{:S(2)}) copy-start(bf16[1024,512]{1,0:T(8,128)(2,1)} %refs_3_.7) | copy-start | bytes 3145732
  64.5 4.9 %collective-permute-start.15 = (bf16[2,256,256]{2,1,0:T(8,128)(2,1)S(1)}, bf16[2,256,256]{2,1,0:T(8,128)(2,1)S(1)}, u32[]{:S(2)}, u32[]{:S(2)}) collective-permute-start(bf16[2,256,256]{2,1,0:T(8,128)(2,1)S(1)} %get-tuple-element.68), channel_id=1, source_target_pairs={{0,2},{2,0},{4,6},{6,4},{8,10},{10,8},{12,14},{14,12},{16,18},{18,... | collective-permute-start | bytes 786440 | tf_op jit(solution)/shard_map/ppermute | solution.py:33
  69.7 7.5 %collective-permute-start.16 = (bf16[256,512]{1,0:T(8,128)(2,1)S(1)}, bf16[256,512]{1,0:T(8,128)(2,1)S(1)}, u32[]{:S(2)}, u32[]{:S(2)}) collective-permute-start(bf16[256,512]{1,0:T(8,128)(2,1)S(1)} %shard_map.113), channel_id=1, source_target_pairs={{0,1},{1,0},{2,3},{3,2},{4,5},{5,4},{6,7},{7,6},{8,9},{9,8},{10,11... | collective-permute-start | bytes 786440 | tf_op jit(solution)/shard_map/ppermute | solution.py:497

commit v7 on v6

--- a/solution.py
+++ b/solution.py
@@ -338,7 +338,7 @@
 
 
 def spread_order(count):
-    groups = [int(g) for g in np.random.default_rng(1).permutation(count // 4)]
+    groups = [int(g) for g in np.random.default_rng(8).permutation(count // 4)]
     return [4 * g + i for g in groups for i in range(4)]
 
 

time: 105 us -> 105 us (level)
  no operation moved by 1% of the time
where the time goes in v7:
time: 105 us
  starting transfers between devices  41.4 us (39%)
  blocking collectives  26.1 us (25%)
  Pallas kernels  21.6 us (21%)
  waiting for transfers between devices  14.8 us (14%)
    ppermute x12, starting transfers between devices, chip_swapped(): lax.ppermute(value, 'blk', [(s, (s + ahead[s]) % count) for s in range(co...  29.5 us
    all_to_all x1, blocking collectives, on_device(): lax.all_to_all(outgoing, 'blk', split_axis=0, concat_axis=0, tiled=True,...  26.1 us
    ppermute x4, starting transfers between devices, core_swapped(): return lax.ppermute(value, 'blk', [(s, s ^ 1) for s in range(count)])  11.5 us
    ppermute x1, waiting for transfers between devices, on_device(): partial_got = lax.ppermute(partial_other, 'head', [(0, 1), (1, 0)])  6.65 us
    pallas_call x1, Pallas kernels, on_device(): call(near_kernel, (kv_shape,) * 4 + (part_shape,), (pairs,), [win] * 4 +...  5.8 us
    ppermute x12, waiting for transfers between devices, chip_swapped(): lax.ppermute(value, 'blk', [(s, (s + ahead[s]) % count) for s in range(co...  5.21 us
    pallas_call x1, Pallas kernels, on_device(): call(local_kernel, (own_shape, own_shape, sds((rows, half), BF), sds((row...  3.63 us
    pallas_call x1, Pallas kernels, on_device(): call(first_stats_kernel, stat_shape, (pairs,), [win] * 4 + [near, bias_sp...  3.54 us
  transfers between devices with their start and end apart: 17, of which 7 were waited for; matrix products, arithmetic and copies ran while one was open for 0% of the time, Pallas kernels for 16%

profile of v7, /device:TPU:1, one launch (start us, length us, event | category | flops | bytes accessed | tf_op | source)
XLA Modules:
  0.0 104.8 jit_solution(9646147342061031686)
XLA Ops:
  0.0 1.4 %shard_map.100 = (bf16[2,256,256]{2,1,0:T(8,128)(2,1)S(1)}, bf16[2,256,256]{2,1,0:T(8,128)(2,1)S(1)}, bf16[272,512]{1,0:T(8,128)(2,1)S(1)}, bf16[272,512]{1,0:T(8,128)(2,1)S(1)}) custom-call(s32[1]{0:T(128)} %bitcast.core_ref, s32[1]{0:T(128)} %bitcast.1.chip_ref, s32[1]{0:T(128)} %bitcast.2.head_ref, s32[2,14]{1,0:T(2,128)} %refs_0_.1, ...), custom_call_target="tpu_custom_call" | custom-call | tf_op jit(solution)/shard_map/pallas_call | solution.py:387
  1.4 3.3 %collective-permute-start = (bf16[2,256,256]{2,1,0:T(8,128)(2,1)S(1)}, bf16[2,256,256]{2,1,0:T(8,128)(2,1)S(1)}, u32[]{:S(2)}, u32[]{:S(2)}) collective-permute-start(bf16[2,256,256]{2,1,0:T(8,128)(2,1)S(1)} %get-tuple-element.40), channel_id=1, source_target_pairs={{0,2},{2,0},{4,6},{6,4},{8,10},{10,8},{12,14},{14,12},{16,18},{18,... | collective-permute-start | bytes 786440 | tf_op jit(solution)/shard_map/ppermute | solution.py:33
  4.7 1.2 %collective-permute-done.refs_1_ = bf16[2,256,256]{2,1,0:T(8,128)(2,1)S(1)} collective-permute-done((bf16[2,256,256]{2,1,0:T(8,128)(2,1)S(1)}, bf16[2,256,256]{2,1,0:T(8,128)(2,1)S(1)}, u32[]{:S(2)}, u32[]{:S(2)}) %collective-permute-start) | collective-permute-done | bytes 262176 | tf_op jit(solution)/shard_map/ppermute | solution.py:33
  5.9 8.8 %collective-permute-start.3 = (bf16[2,256,256]{2,1,0:T(8,128)(2,1)S(1)}, bf16[2,256,256]{2,1,0:T(8,128)(2,1)S(1)}, u32[]{:S(2)}, u32[]{:S(2)}) collective-permute-start(bf16[2,256,256]{2,1,0:T(8,128)(2,1)S(1)} %get-tuple-element.43.refs_0_), channel_id=1, source_target_pairs={{0,252},{2,254},{4,8},{6,10},{8,4},{10,6},{12,16},{14,18},{16,12},... | collective-permute-start | bytes 786440 | tf_op jit(solution)/shard_map/ppermute | solution.py:39
  14.8 0.7 collective-permute-start.5
  15.4 1.8 %collective-permute-start.7 = (bf16[2,256,256]{2,1,0:T(8,128)(2,1)S(1)}, bf16[2,256,256]{2,1,0:T(8,128)(2,1)S(1)}, u32[]{:S(2)}, u32[]{:S(2)}) collective-permute-start(bf16[2,256,256]{2,1,0:T(8,128)(2,1)S(1)} %get-tuple-element.43.refs_0_), channel_id=1, source_target_pairs={{0,4},{2,6},{4,0},{6,2},{8,12},{10,14},{12,8},{14,10},{16,20},{18,... | collective-permute-start | bytes 786440 | tf_op jit(solution)/shard_map/ppermute | solution.py:39
  17.2 3.9 %collective-permute-done.3.refs_0_ = bf16[2,256,256]{2,1,0:T(8,128)(2,1)S(1)} collective-permute-done((bf16[2,256,256]{2,1,0:T(8,128)(2,1)S(1)}, bf16[2,256,256]{2,1,0:T(8,128)(2,1)S(1)}, u32[]{:S(2)}, u32[]{:S(2)}) %collective-permute-start.3) | collective-permute-done | bytes 262176 | tf_op jit(solution)/shard_map/ppermute | solution.py:39
  21.1 0.8 collective-permute-done.1.refs_2_.refs_1_
  21.9 6.1 %collective-permute-start.2 = (bf16[2,256,256]{2,1,0:T(8,128)(2,1)S(1)}, bf16[2,256,256]{2,1,0:T(8,128)(2,1)S(1)}, u32[]{:S(2)}, u32[]{:S(2)}) collective-permute-start(bf16[2,256,256]{2,1,0:T(8,128)(2,1)S(1)} %collective-permute-done.1.refs_2_.refs_1_), channel_id=1, source_target_pairs={{0,252},{2,254},{4,8},{6,10},{8,4},{10,6},{12,16},{14,18},{16,12},... | collective-permute-start | bytes 786440 | tf_op jit(solution)/shard_map/ppermute | solution.py:39
  28.4 3.5 %shard_map.103.refs_4_ = f32[2,4,8,256]{3,2,1,0:T(8,128)S(1)} custom-call(s32[1]{0:T(128)} %bitcast.core_ref, s32[1]{0:T(128)} %bitcast.1.chip_ref, s32[1]{0:T(128)} %bitcast.2.head_ref, bf16[2,256,256]{2,1,0:T(8,128)(2,1)S(1)} %get-tuple-element.43.refs_0_, bf16[2,256,256]{2,1,0:T(8,128)(2,1)S(1)} %get-tuple-element.44.refs_1_, ...), custom_call_target="tpu_custom_call" | custom-call | flops 536870912 | bytes 4194304 | tf_op jit(solution)/shard_map/pallas_call | solution.py:439
  32.0 2.1 %shard_map.104.refs_4_ = f32[2,4,8,256]{3,2,1,0:T(8,128)S(1)} custom-call(s32[1]{0:T(128)} %bitcast.core_ref, s32[1]{0:T(128)} %bitcast.1.chip_ref, s32[1]{0:T(128)} %bitcast.2.head_ref, bf16[2,256,256]{2,1,0:T(8,128)(2,1)S(1)} %collective-permute-done.3.refs_0_, bf16[2,256,256]{2,1,0:T(8,128)(2,1)S(1)} %collective-permute-done.6.refs_1_.refs_2_, ...), custom_call_target="tpu_custom_call" | custom-call | flops 268435456 | bytes 2097152 | tf_op jit(solution)/shard_map/pallas_call | solution.py:443
  34.1 0.4 collective-permute-done.2.refs_0_.refs_2_
  34.5 2.0 %shard_map.106 = (f32[2,4,8,256]{3,2,1,0:T(8,128)S(1)}, bf16[2,256,256]{2,1,0:T(8,128)(2,1)S(1)}, bf16[2,256,256]{2,1,0:T(8,128)(2,1)S(1)}, bf16[2,2,256,512]{3,2,1,0:T(8,128)(2,1)S(1)}) custom-call(s32[1]{0:T(128)} %bitcast.core_ref, s32[1]{0:T(128)} %bitcast.1.chip_ref, s32[1]{0:T(128)} %bitcast.2.head_ref, ...), custom_call_target="tpu_custom_call" | custom-call | flops 268435456 | bytes 2097152 | tf_op jit(solution)/shard_map/pallas_call | solution.py:452
  36.6 5.3 %collective-permute-start.11 = (bf16[2,256,256]{2,1,0:T(8,128)(2,1)S(1)}, bf16[2,256,256]{2,1,0:T(8,128)(2,1)S(1)}, u32[]{:S(2)}, u32[]{:S(2)}) collective-permute-start(bf16[2,256,256]{2,1,0:T(8,128)(2,1)S(1)} %get-tuple-element.64), channel_id=1, source_target_pairs={{0,252},{2,254},{4,8},{6,10},{8,4},{10,6},{12,16},{14,18},{16,12},... | collective-permute-start | bytes 786440 | tf_op jit(solution)/shard_map/ppermute | solution.py:39
  41.9 5.8 %shard_map.107 = (bf16[2,256,256]{2,1,0:T(8,128)(2,1)S(1)}, bf16[2,256,256]{2,1,0:T(8,128)(2,1)S(1)}, bf16[2,256,256]{2,1,0:T(8,128)(2,1)S(1)}, bf16[2,256,256]{2,1,0:T(8,128)(2,1)S(1)}, f32[2,2,128,256]{3,2,1,0:T(8,128)S(1)}) custom-call(s32[1]{0:T(128)} %bitcast.core_ref, s32[1]{0:T(128)} %bitcast.1.chip_ref, s32[1]{0:T(128)} %bitcast.2.head_ref, ...), custom_call_target="tpu_custom_call" | custom-call | flops 1073741824 | bytes 4194304 | tf_op jit(solution)/shard_map/pallas_call | solution.py:460
  47.7 2.3 %collective-permute-start.13 = (bf16[2,256,256]{2,1,0:T(8,128)(2,1)S(1)}, bf16[2,256,256]{2,1,0:T(8,128)(2,1)S(1)}, u32[]{:S(2)}, u32[]{:S(2)}) collective-permute-start(bf16[2,256,256]{2,1,0:T(8,128)(2,1)S(1)} %get-tuple-element.65), channel_id=1, source_target_pairs={{0,252},{2,254},{4,8},{6,10},{8,4},{10,6},{12,16},{14,18},{16,12},... | collective-permute-start | bytes 786440 | tf_op jit(solution)/shard_map/ppermute | solution.py:39
  50.0 5.1 %collective-permute-start.10 = (bf16[2,256,256]{2,1,0:T(8,128)(2,1)S(1)}, bf16[2,256,256]{2,1,0:T(8,128)(2,1)S(1)}, u32[]{:S(2)}, u32[]{:S(2)}) collective-permute-start(bf16[2,256,256]{2,1,0:T(8,128)(2,1)S(1)} %add_convert_fusion.1), channel_id=1, source_target_pairs={{0,252},{2,254},{4,8},{6,10},{8,4},{10,6},{12,16},{14,18},{16,12},... | collective-permute-start | bytes 786440 | tf_op jit(solution)/shard_map/ppermute | solution.py:39
  55.3 3.6 %shard_map.108 = (f32[2,256,256]{2,1,0:T(8,128)S(1)}, f32[2,256,256]{2,1,0:T(8,128)S(1)}, bf16[256,256]{1,0:T(8,128)(2,1)S(1)}, bf16[256,256]{1,0:T(8,128)(2,1)S(1)}) custom-call(s32[1]{0:T(128)} %bitcast.core_ref, s32[1]{0:T(128)} %bitcast.1.chip_ref, s32[1]{0:T(128)} %bitcast.2.head_ref, bf16[2,256,256]{2,1,0:T(8,128)(2,1)S(1)} %get-tuple-element.43.refs_0_, ...), custom_call_target="tpu_custom_call" | custom-call | flops 536870912 | bytes 4194304 | tf_op jit(solution)/shard_map/pallas_call | solution.py:469
  59.0 3.8 %collective-permute-start.8 = (bf16[256,256]{1,0:T(8,128)(2,1)S(1)}, bf16[256,256]{1,0:T(8,128)(2,1)S(1)}, u32[]{:S(2)}, u32[]{:S(2)}) collective-permute-start(bf16[256,256]{1,0:T(8,128)(2,1)S(1)} %get-tuple-element.55), channel_id=1, source_target_pairs={{0,2},{2,0},{4,6},{6,4},{8,10},{10,8},{12,14},{14,12},{16,18},{18,... | collective-permute-start | bytes 393224 | tf_op jit(solution)/shard_map/ppermute | solution.py:33
  62.8 1.0 collective-permute-done.8.refs_1_
  63.8 0.5 shard_map.109
  64.3 0.2 shard_map.110
  64.5 3.7 %collective-permute-start.15 = (bf16[2,256,256]{2,1,0:T(8,128)(2,1)S(1)}, bf16[2,256,256]{2,1,0:T(8,128)(2,1)S(1)}, u32[]{:S(2)}, u32[]{:S(2)}) collective-permute-start(bf16[2,256,256]{2,1,0:T(8,128)(2,1)S(1)} %get-tuple-element.68), channel_id=1, source_target_pairs={{0,2},{2,0},{4,6},{6,4},{8,10},{10,8},{12,14},{14,12},{16,18},{18,... | collective-permute-start | bytes 786440 | tf_op jit(solution)/shard_map/ppermute | solution.py:33
  68.2 0.3 shard_map.112.refs_0_
  68.6 0.8 collective-permute-done.15.refs_2_.refs_1_
  69.4 0.3 shard_map.113
  69.7 0.4 collective-permute-start.16
  70.1 0.5 shard_map.111.own_ref
  70.6 6.6 %collective-permute-done.16.got_ref = bf16[256,512]{1,0:T(8,128)(2,1)S(1)} collective-permute-done((bf16[256,512]{1,0:T(8,128)(2,1)S(1)}, bf16[256,512]{1,0:T(8,128)(2,1)S(1)}, u32[]{:S(2)}, u32[]{:S(2)}) %collective-permute-start.16) | collective-permute-done | bytes 262176 | tf_op jit(solution)/shard_map/ppermute | solution.py:497
  77.3 0.3 shard_map.114
  77.7 26.1 %all_to_all.11 = bf16[128,4,512]{2,1,0:T(4,128)(2,1)S(1)} all-to-all(bf16[128,4,512]{2,1,0:T(4,128)(2,1)S(1)} %all_to_all.7), channel_id=1, replica_groups={{240,242,244,246,80,82,84,86,104,106,108,110,152,154,156,158,136,138,14..., dimensions={0} | all-to-all | bytes 1048576 | tf_op jit(solution)/shard_map/all_to_all | solution.py:508
  103.9 0.8 shard_map.115
  (34 shorter events, 1.0 us)
Async XLA Ops:
  1.4 4.5 %collective-permute-start = (bf16[2,256,256]{2,1,0:T(8,128)(2,1)S(1)}, bf16[2,256,256]{2,1,0:T(8,128)(2,1)S(1)}, u32[]{:S(2)}, u32[]{:S(2)}) collective-permute-start(bf16[2,256,256]{2,1,0:T(8,128)(2,1)S(1)} %get-tuple-element.40), channel_id=1, source_target_pairs={{0,2},{2,0},{4,6},{6,4},{8,10},{10,8},{12,14},{14,12},{16,18},{18,... | collective-permute-start | bytes 786440 | tf_op jit(solution)/shard_map/ppermute | solution.py:33
  5.9 22.3 %copy-start.3 = (s32[512,1]{1,0:T(8,128)S(1)}, s32[512,1]{1,0:T(8,128)}, u32[]{:S(2)}) copy-start(s32[512,1]{1,0:T(8,128)} %constant.12.clone.label_ref) | copy-start | bytes 6148
  5.9 22.1 %copy-start.4 = (s32[256,1]{0,1:T(1,128)S(1)}, s32[256,1]{0,1:T(1,128)}, u32[]{:S(2)}) copy-start(s32[256,1]{0,1:T(1,128)} %param.18) | copy-start | bytes 3076
  5.9 15.2 %collective-permute-start.3 = (bf16[2,256,256]{2,1,0:T(8,128)(2,1)S(1)}, bf16[2,256,256]{2,1,0:T(8,128)(2,1)S(1)}, u32[]{:S(2)}, u32[]{:S(2)}) collective-permute-start(bf16[2,256,256]{2,1,0:T(8,128)(2,1)S(1)} %get-tuple-element.43.refs_0_), channel_id=1, source_target_pairs={{0,252},{2,254},{4,8},{6,10},{8,4},{10,6},{12,16},{14,18},{16,12},... | collective-permute-start | bytes 786440 | tf_op jit(solution)/shard_map/ppermute | solution.py:39
  14.7 7.2 %collective-permute-start.1 = (bf16[2,256,256]{2,1,0:T(8,128)(2,1)S(1)}, bf16[2,256,256]{2,1,0:T(8,128)(2,1)S(1)}, u32[]{:S(2)}, u32[]{:S(2)}) collective-permute-start(bf16[2,256,256]{2,1,0:T(8,128)(2,1)S(1)} %get-tuple-element.44.refs_1_), channel_id=1, source_target_pairs={{0,4},{2,6},{4,0},{6,2},{8,12},{10,14},{12,8},{14,10},{16,20},{18,... | collective-permute-start | bytes 786440 | tf_op jit(solution)/shard_map/ppermute | solution.py:39
  14.8 13.6 %collective-permute-start.5 = (bf16[272,512]{1,0:T(8,128)(2,1)S(1)}, bf16[272,512]{1,0:T(8,128)(2,1)S(1)}, u32[]{:S(2)}, u32[]{:S(2)}) collective-permute-start(bf16[272,512]{1,0:T(8,128)(2,1)S(1)} %get-tuple-element.46), channel_id=1, source_target_pairs={{0,2},{2,0},{4,6},{6,4},{8,10},{10,8},{12,14},{14,12},{16,18},{18,... | collective-permute-start | bytes 835592 | tf_op jit(solution)/shard_map/ppermute | solution.py:33
  15.4 13.0 %collective-permute-start.7 = (bf16[2,256,256]{2,1,0:T(8,128)(2,1)S(1)}, bf16[2,256,256]{2,1,0:T(8,128)(2,1)S(1)}, u32[]{:S(2)}, u32[]{:S(2)}) collective-permute-start(bf16[2,256,256]{2,1,0:T(8,128)(2,1)S(1)} %get-tuple-element.43.refs_0_), channel_id=1, source_target_pairs={{0,4},{2,6},{4,0},{6,2},{8,12},{10,14},{12,8},{14,10},{16,20},{18,... | collective-permute-start | bytes 786440 | tf_op jit(solution)/shard_map/ppermute | solution.py:39
  17.2 14.8 %collective-permute-start.6 = (bf16[2,256,256]{2,1,0:T(8,128)(2,1)S(1)}, bf16[2,256,256]{2,1,0:T(8,128)(2,1)S(1)}, u32[]{:S(2)}, u32[]{:S(2)}) collective-permute-start(bf16[2,256,256]{2,1,0:T(8,128)(2,1)S(1)} %get-tuple-element.44.refs_1_), channel_id=1, source_target_pairs={{0,252},{2,254},{4,8},{6,10},{8,4},{10,6},{12,16},{14,18},{16,12},... | collective-permute-start | bytes 786440 | tf_op jit(solution)/shard_map/ppermute | solution.py:39
  21.1 13.0 %collective-permute-start.4 = (bf16[2,256,256]{2,1,0:T(8,128)(2,1)S(1)}, bf16[2,256,256]{2,1,0:T(8,128)(2,1)S(1)}, u32[]{:S(2)}, u32[]{:S(2)}) collective-permute-start(bf16[2,256,256]{2,1,0:T(8,128)(2,1)S(1)} %collective-permute-done.3.refs_0_), channel_id=1, source_target_pairs={{0,4},{2,6},{4,0},{6,2},{8,12},{10,14},{12,8},{14,10},{16,20},{18,... | collective-permute-start | bytes 786440 | tf_op jit(solution)/shard_map/ppermute | solution.py:39
  21.9 12.6 %collective-permute-start.2 = (bf16[2,256,256]{2,1,0:T(8,128)(2,1)S(1)}, bf16[2,256,256]{2,1,0:T(8,128)(2,1)S(1)}, u32[]{:S(2)}, u32[]{:S(2)}) collective-permute-start(bf16[2,256,256]{2,1,0:T(8,128)(2,1)S(1)} %collective-permute-done.1.refs_2_.refs_1_), channel_id=1, source_target_pairs={{0,252},{2,254},{4,8},{6,10},{8,4},{10,6},{12,16},{14,18},{16,12},... | collective-permute-start | bytes 786440 | tf_op jit(solution)/shard_map/ppermute | solution.py:39
  36.5 13.5 %collective-permute-start.9 = (bf16[2,256,256]{2,1,0:T(8,128)(2,1)S(1)}, bf16[2,256,256]{2,1,0:T(8,128)(2,1)S(1)}, u32[]{:S(2)}, u32[]{:S(2)}) collective-permute-start(bf16[2,256,256]{2,1,0:T(8,128)(2,1)S(1)} %get-tuple-element.62), channel_id=1, source_target_pairs={{0,4},{2,6},{4,0},{6,2},{8,12},{10,14},{12,8},{14,10},{16,20},{18,... | collective-permute-start | bytes 786440 | tf_op jit(solution)/shard_map/ppermute | solution.py:39
  36.6 18.5 %collective-permute-start.11 = (bf16[2,256,256]{2,1,0:T(8,128)(2,1)S(1)}, bf16[2,256,256]{2,1,0:T(8,128)(2,1)S(1)}, u32[]{:S(2)}, u32[]{:S(2)}) collective-permute-start(bf16[2,256,256]{2,1,0:T(8,128)(2,1)S(1)} %get-tuple-element.64), channel_id=1, source_target_pairs={{0,252},{2,254},{4,8},{6,10},{8,4},{10,6},{12,16},{14,18},{16,12},... | collective-permute-start | bytes 786440 | tf_op jit(solution)/shard_map/ppermute | solution.py:39
  47.7 16.6 %collective-permute-start.13 = (bf16[2,256,256]{2,1,0:T(8,128)(2,1)S(1)}, bf16[2,256,256]{2,1,0:T(8,128)(2,1)S(1)}, u32[]{:S(2)}, u32[]{:S(2)}) collective-permute-start(bf16[2,256,256]{2,1,0:T(8,128)(2,1)S(1)} %get-tuple-element.65), channel_id=1, source_target_pairs={{0,252},{2,254},{4,8},{6,10},{8,4},{10,6},{12,16},{14,18},{16,12},... | collective-permute-start | bytes 786440 | tf_op jit(solution)/shard_map/ppermute | solution.py:39
  50.0 14.3 %collective-permute-start.14 = (bf16[2,256,256]{2,1,0:T(8,128)(2,1)S(1)}, bf16[2,256,256]{2,1,0:T(8,128)(2,1)S(1)}, u32[]{:S(2)}, u32[]{:S(2)}) collective-permute-start(bf16[2,256,256]{2,1,0:T(8,128)(2,1)S(1)} %get-tuple-element.66), channel_id=1, source_target_pairs={{0,4},{2,6},{4,0},{6,2},{8,12},{10,14},{12,8},{14,10},{16,20},{18,... | collective-permute-start | bytes 786440 | tf_op jit(solution)/shard_map/ppermute | solution.py:39
  50.0 14.2 %collective-permute-start.10 = (bf16[2,256,256]{2,1,0:T(8,128)(2,1)S(1)}, bf16[2,256,256]{2,1,0:T(8,128)(2,1)S(1)}, u32[]{:S(2)}, u32[]{:S(2)}) collective-permute-start(bf16[2,256,256]{2,1,0:T(8,128)(2,1)S(1)} %add_convert_fusion.1), channel_id=1, source_target_pairs={{0,252},{2,254},{4,8},{6,10},{8,4},{10,6},{12,16},{14,18},{16,12},... | collective-permute-start | bytes 786440 | tf_op jit(solution)/shard_map/ppermute | solution.py:39
  55.2 9.1 %collective-permute-start.12 = (bf16[2,256,256]{2,1,0:T(8,128)(2,1)S(1)}, bf16[2,256,256]{2,1,0:T(8,128)(2,1)S(1)}, u32[]{:S(2)}, u32[]{:S(2)}) collective-permute-start(bf16[2,256,256]{2,1,0:T(8,128)(2,1)S(1)} %add_convert_fusion), channel_id=1, source_target_pairs={{0,4},{2,6},{4,0},{6,2},{8,12},{10,14},{12,8},{14,10},{16,20},{18,... | collective-permute-start | bytes 786440 | tf_op jit(solution)/shard_map/ppermute | solution.py:39
  55.3 8.5 %copy-start.2 = (bf16[1024,512]{1,0:T(8,128)(2,1)S(1)}, bf16[1024,512]{1,0:T(8,128)(2,1)}, u32[]{:S(2)}) copy-start(bf16[1024,512]{1,0:T(8,128)(2,1)} %refs_2_.5) | copy-start | bytes 3145732
  59.0 4.8 %collective-permute-start.8 = (bf16[256,256]{1,0:T(8,128)(2,1)S(1)}, bf16[256,256]{1,0:T(8,128)(2,1)S(1)}, u32[]{:S(2)}, u32[]{:S(2)}) collective-permute-start(bf16[256,256]{1,0:T(8,128)(2,1)S(1)} %get-tuple-element.55), channel_id=1, source_target_pairs={{0,2},{2,0},{4,6},{6,4},{8,10},{10,8},{12,14},{14,12},{16,18},{18,... | collective-permute-start | bytes 393224 | tf_op jit(solution)/shard_map/ppermute | solution.py:33
  64.3 3.9 %copy-start = (bf16[1024,512]{1,0:T(8,128)(2,1)S(1)}, bf16[1024,512]{1,0:T(8,128)(2,1)}, u32[]{:S(2)}) copy-start(bf16[1024,512]{1,0:T(8,128)(2,1)} %refs_2_.7) | copy-start | bytes 3145732
  64.3 3.9 %copy-start.1 = (bf16[1024,512]{1,0:T(8,128)(2,1)S(1)}, bf16[1024,512]{1,0:T(8,128)(2,1)}, u32[]{:S(2)}) copy-start(bf16[1024,512]{1,0:T(8,128)(2,1)} %refs_3_.7) | copy-start | bytes 3145732
  64.5 4.9 %collective-permute-start.15 = (bf16[2,256,256]{2,1,0:T(8,128)(2,1)S(1)}, bf16[2,256,256]{2,1,0:T(8,128)(2,1)S(1)}, u32[]{:S(2)}, u32[]{:S(2)}) collective-permute-start(bf16[2,256,256]{2,1,0:T(8,128)(2,1)S(1)} %get-tuple-element.68), channel_id=1, source_target_pairs={{0,2},{2,0},{4,6},{6,4},{8,10},{10,8},{12,14},{14,12},{16,18},{18,... | collective-permute-start | bytes 786440 | tf_op jit(solution)/shard_map/ppermute | solution.py:33
  69.7 7.5 %collective-permute-start.16 = (bf16[256,512]{1,0:T(8,128)(2,1)S(1)}, bf16[256,512]{1,0:T(8,128)(2,1)S(1)}, u32[]{:S(2)}, u32[]{:S(2)}) collective-permute-start(bf16[256,512]{1,0:T(8,128)(2,1)S(1)} %shard_map.113), channel_id=1, source_target_pairs={{0,1},{1,0},{2,3},{3,2},{4,5},{5,4},{6,7},{7,6},{8,9},{9,8},{10,11... | collective-permute-start | bytes 786440 | tf_op jit(solution)/shard_map/ppermute | solution.py:497
